TPU v7x, 128 devices: a whole 4x4x4 slice. The times are simulated.
128 devices in a mesh: row: 16 (over z_hi, x, core), col: 8 (over z_lo, y).
Axes of the slice: x: 4, y: 4, z: 4 (z_hi: 2, z_lo: 2; z = z_hi * 2 + z_lo), core: 2. Of those that a mesh axis runs over, the one named last changes fastest.
Arguments:
- integrals: bfloat16 [6144, 6144], P('row', 'col'), may hold values from -0.078125 to 0.078125
- amplitudes: bfloat16 [6144, 12288], P('row', 'col'), may hold values from -6 to 6
- tile_pattern: int32 [48, 48], replicated, may hold values 0 or 1
- pair_domain: int32 [48, 12288], P(None, 'col'), may hold values 0 or 1
- tile_order: int32 [48], replicated, may hold values from 0 to 47, each once
Outputs:
- ladder: float32 [6144, 12288], P('row', 'col')
Inputs may be any that keep to these rules, and one draw needn't show every extreme that they name: tile_order holds each tile number once.
All inputs are finite; a program needn't handle non-finite values. No bound on the sum of `pair_domain` on one device may be relied on, other than what follows from the above.
Results may differ from a plain program's by a relative error of at most 0.0003.
Values may be sent and summed in bfloat16 or wider, within the bound.
No kernel may reach another device: no remote copies, remote signals or barrier semaphores. Data moves between devices by JAX's collectives and lax.ppermute only.
A program may use at most 128 MiB of HBM per device.

v0:
```python
import jax
import jax.numpy as jnp
from jax import lax
from jax.sharding import PartitionSpec as P

TILE = 128


def storage_masks(tile_pattern, pair_domain, tile_order):
    count = tile_order.shape[0]
    placed = (tile_order[:, None] == jnp.arange(count, dtype=jnp.int32)[None, :]).astype(
        jnp.float32
    )
    pattern_stored = jnp.dot(
        jnp.dot(placed, tile_pattern.astype(jnp.float32), precision=lax.Precision.HIGHEST),
        placed.T,
        precision=lax.Precision.HIGHEST,
    )
    domain_stored = jnp.dot(
        placed, pair_domain.astype(jnp.float32), precision=lax.Precision.HIGHEST
    )
    return (pattern_stored, domain_stored)


def on_device(integrals, amplitudes, tile_pattern, pair_domain, tile_order):
    pattern_stored, domain_stored = storage_masks(tile_pattern, pair_domain, tile_order)
    tiles_here = pattern_stored.shape[0] // lax.axis_size("row")
    pattern_rows = lax.dynamic_slice_in_dim(
        pattern_stored, lax.axis_index("row") * tiles_here, tiles_here, 0
    )
    integral_mask = jnp.repeat(jnp.repeat(pattern_rows, TILE, axis=0), TILE, axis=1).astype(
        jnp.bfloat16
    )
    domain_mask = jnp.repeat(domain_stored, TILE, axis=0).astype(jnp.bfloat16)
    amplitude_full = lax.all_gather(amplitudes, "row", axis=0, tiled=True)
    restricted = amplitude_full * domain_mask
    return jnp.dot(
        lax.all_gather(integrals, "col", axis=1, tiled=True) * integral_mask,
        restricted,
        preferred_element_type=jnp.float32,
    )


def solution(mesh):
    in_specs = (P("row", "col"), P("row", "col"), P(), P(None, "col"), P())
    out_specs = P("row", "col")
    return jax.shard_map(
        on_device, mesh=mesh, in_specs=in_specs, out_specs=out_specs, check_vma=False
    )
```

profile of v0, /device:TPU:1, one launch (start us, length us, event | category | flops | bytes accessed | tf_op | source)
XLA Modules:
  0.0 212.6 jit_solution(6242452035439145097)
XLA Ops:
  6.5 0.0 all-gather.5.cloned.1.call-start
  6.5 0.7 all-gather.5.cloned.1.call-update
  7.3 0.0 all-gather.3.cloned.1.call-start
  7.3 0.7 all-gather.3.cloned.1.call-update
  8.0 0.9 fusion.3
  9.0 0.9 fusion.5
  9.9 1.3 convolution_convert_fusion
  11.2 122.2 %all-gather.5.cloned.1.call-done = bf16[6144,1536]{1,0:T(8,128)(2,1)} async-done(((bf16[384,1536]{1,0:T(8,128)(2,1)}), bf16[6144,1536]{1,0:T(8,128)(2,1)}) %all-gather.5.cloned.1.call-update) | async-done | bytes 18874384 | tf_op jit(solution)/shard_map/all_gather | solution.py:35
  133.4 16.6 %bitcast_multiply_fusion = bf16[6144,1536]{1,0:T(8,128)(2,1)} fusion(bf16[6144,1536]{1,0:T(8,128)(2,1)} %all-gather.5.cloned.1.call-done, bf16[48,1536]{1,0:T(8,128)(2,1)S(1)} %convolution_convert_fusion), kind=kLoop, calls=%fused_computation | loop fusion | flops 9437184 | bytes 37896192 | tf_op jit(solution)/shard_map/mul | solution.py:36
  150.0 39.8 %all-gather.3.cloned.1.call-done = bf16[384,6144]{1,0:T(8,128)(2,1)} async-done(((bf16[384,768]{1,0:T(8,128)(2,1)}), bf16[384,6144]{1,0:T(8,128)(2,1)}) %all-gather.3.cloned.1.call-update) | async-done | bytes 4718608 | tf_op jit(solution)/shard_map/all_gather | solution.py:38
  189.8 0.0 copy-start
  189.8 2.9 %broadcast_in_dim.12 = bf16[384,48,128]{2,1,0:T(8,128)(2,1)S(1)} broadcast(bf16[384,48]{1,0:T(8,128)(2,1)S(1)} %bitcast.10), dimensions={0,1} | broadcast | bytes 4755456 | tf_op jit(solution)/shard_map/broadcast_in_dim | solution.py:31
  192.7 0.0 copy-done
  192.7 13.0 %fusion = f32[384,1536]{1,0:T(8,128)} fusion(bf16[6144,1536]{1,0:T(8,128)(2,1)} %bitcast_multiply_fusion, bf16[384,6144]{1,0:T(8,128)(2,1)S(1)} %copy-done, bf16[48,8,48,128]{3,2,1,0:T(8,128)(2,1)S(1)} %bitcast.9), kind=kOutput, calls=%fused_computation.2 | convolution fusion | flops 7250116608 | bytes 30670848 | tf_op jit(solution)/shard_map/dot_general | solution.py:37
  (2 shorter events, 0.0 us)
Async XLA Ops:
  6.5 126.9 %all-gather.5.cloned.1.call-start = ((), (), s32[]{:S(2)}) async-start(), calls=%async_computation.1 | async-start | bytes 20054016 | tf_op jit(solution)/shard_map/all_gather | solution.py:35
  7.3 182.6 %all-gather.3.cloned.1.call-start = ((), (), s32[]{:S(2)}) async-start(), calls=%async_computation | async-start | bytes 5308416 | tf_op jit(solution)/shard_map/all_gather | solution.py:38
  189.8 2.9 %copy-start = (bf16[384,6144]{1,0:T(8,128)(2,1)S(1)}, bf16[384,6144]{1,0:T(8,128)(2,1)}, u32[]{:S(2)}) copy-start(bf16[384,6144]{1,0:T(8,128)(2,1)} %all-gather.3.cloned.1.call-done) | copy-start | bytes 14155780
Sparse Core Ops, SparseCore 0:
  9.8 123.5 all-gather.4
  135.1 54.7 all-gather.2
where the time goes:
time: 213 us
  waiting for transfers between devices  163 us (77%)
  other arithmetic  16.6 us (8%)
  matrix products  16.1 us (8%)
  between operations  13.5 us (6%)
  local copies, waits for them, and re-layouts  2.92 us (1%)
    all_gather x1, waiting for transfers between devices, on_device(): amplitude_full = lax.all_gather(amplitudes, 'row', axis=0, tiled=True)  122 us
    all_gather x1, waiting for transfers between devices, on_device(): lax.all_gather(integrals, 'col', axis=1, tiled=True) * integral_mask  39.8 us
    mul x1, other arithmetic, on_device(): restricted = amplitude_full * domain_mask  16.6 us
    dot_general x1, matrix products, on_device(): jnp.dot(lax.all_gather(integrals, 'col', axis=1, tiled=True) * integral_m...  13 us
  transfers between devices with their start and end apart: 2, of which 2 were waited for; matrix products, arithmetic and copies ran while one was open for 9% of the time, Pallas kernels for 0%

commit v1 on v0

v1 whole, which is shorter than its diff:
```python
import functools

import jax
import jax.numpy as jnp
import numpy as np
from jax import lax
from jax.experimental import pallas as pl
from jax.experimental.pallas import tpu as pltpu
from jax.sharding import Mesh, PartitionSpec as P

TILE = 128
AXES = ("zh", "x", "core", "zl", "y")
SIZES = (2, 4, 2, 2, 4)
ROW, COL = ("zh", "x", "core"), ("zl", "y")
BF16, F32, I32 = jnp.bfloat16, jnp.float32, jnp.int32
FLAG_ROWS = 8
VMEM_LIMIT = 60 << 20


def iota(shape, dim):
    return lax.broadcasted_iota(I32, shape, dim)


def whole(n, space=pltpu.VMEM):
    return [pl.BlockSpec(memory_space=space)] * n


def plan_kernel(tall, slots, order, pattern, place, a_ref, d_ref, keep_ref, send_ref, pos_ref, start_ref, dom):
    row, col, core = place[0], place[1], place[2]
    tiles, pairs = d_ref.shape
    rows, cols = a_ref.shape
    half = cols // TILE // 2
    for s in range(tiles):
        dom[pl.ds(s, 1), :] = d_ref[pl.ds(order[s], 1), :]
    live = dom[...].astype(F32).astype(BF16)
    blocks = pairs // TILE
    spread = (iota((pairs, TILE), 0) // TILE == iota((pairs, TILE), 1)).astype(F32).astype(BF16)
    counts = jnp.dot(live, spread, preferred_element_type=F32)
    below = (iota((TILE, TILE), 0) < iota((TILE, TILE), 1)).astype(F32).astype(BF16)
    upto = (iota((TILE, TILE), 0) <= iota((TILE, TILE), 1)).astype(F32).astype(BF16)
    s0, s1 = iota((tiles, tiles), 0), iota((tiles, tiles), 1)
    before = ((s0 // tall == s1 // tall) & (s1 < s0)).astype(F32).astype(BF16)
    counted = counts.astype(BF16)
    ahead = jnp.sum(jnp.dot(before, counted, preferred_element_type=F32), axis=1, keepdims=True)
    starts = jnp.dot(counted, below, preferred_element_type=F32) + ahead
    start_ref[...] = starts.astype(I32)
    for b in range(blocks):
        lanes = pl.ds(b * TILE, TILE)
        here = live[:, b * TILE : (b + 1) * TILE]
        slot = jnp.dot(here, upto, preferred_element_type=F32) + (starts[:, b : b + 1] - 1.0)
        pos_ref[:, lanes] = jnp.where(dom[:, lanes] > 0, slot.astype(I32), -1)
    most = jnp.max(ahead + jnp.sum(counts, axis=1, keepdims=True), axis=0, keepdims=True)
    flag = jnp.where(most > slots, 1.0, 0.0).astype(F32)
    keep_ref[pl.ds(rows, FLAG_ROWS), :] = jnp.broadcast_to(flag, (FLAG_ROWS, cols // 2)).astype(BF16)
    for i in range(rows // TILE):
        high = pl.ds(i * TILE, TILE)
        for j in range(half):
            for ref, base in ((keep_ref, core * half), (send_ref, (1 - core) * half)):
                tile = base + j
                on = pattern[order[row * tall + i], order[col * 2 * half + tile]]
                scale = on.astype(F32).astype(BF16)
                part = a_ref[high, pl.ds(pl.multiple_of(tile * TILE, TILE), TILE)]
                ref[high, pl.ds(j * TILE, TILE)] = part * scale


def plan(integrals, tile_pattern, pair_domain, tile_order, place, tall, slots):
    rows, cols = integrals.shape
    tiles, pairs = pair_domain.shape
    return pl.pallas_call(
        functools.partial(plan_kernel, tall, slots),
        grid_spec=pltpu.PrefetchScalarGridSpec(
            num_scalar_prefetch=3,
            grid=(),
            in_specs=whole(2),
            out_specs=whole(4),
            scratch_shapes=[pltpu.VMEM((tiles, pairs), I32)],
        ),
        out_shape=[
            jax.ShapeDtypeStruct((rows + FLAG_ROWS, cols // 2), BF16),
            jax.ShapeDtypeStruct((rows, cols // 2), BF16),
            jax.ShapeDtypeStruct((tiles, pairs), I32),
            jax.ShapeDtypeStruct((tiles, TILE), I32),
        ],
        name="plan",
    )(tile_order, tile_pattern, place, integrals, pair_domain)


def compact_kernel(slots, start, place, b_ref, pos_ref, u_ref, f_ref, g_ref, total):
    tall = b_ref.shape[0] // TILE
    total[...] = jnp.zeros_like(total)
    for i in range(tall):
        s = place[0] * tall + i
        slot = pos_ref[pl.ds(s, 1), :]
        for b in range(b_ref.shape[1] // TILE):
            lanes = pl.ds(b * TILE, TILE)
            at = jnp.minimum(start[s, b] // TILE * TILE, slots)
            at = pl.multiple_of(at, TILE)
            pick = (iota((2 * TILE, TILE), 0) + at == slot[:, b * TILE : (b + 1) * TILE]).astype(F32).astype(BF16)
            moved = lax.dot_general(
                b_ref[pl.ds(i * TILE, TILE), lanes], pick, (((1,), (1,)), ((), ())), preferred_element_type=F32
            )
            total[:, pl.ds(at, 2 * TILE)] += moved
    packed = total[:, :slots].astype(BF16)
    first = f_ref.shape[0]
    u_ref[...] = packed
    f_ref[...] = packed[:first]
    g_ref[...] = packed[first:]


def compact(start, place, amplitudes, pos, slots, first):
    return pl.pallas_call(
        functools.partial(compact_kernel, slots),
        grid_spec=pltpu.PrefetchScalarGridSpec(
            num_scalar_prefetch=2,
            grid=(),
            in_specs=whole(2),
            out_specs=whole(3),
            scratch_shapes=[pltpu.VMEM((TILE, slots + 2 * TILE), F32)],
        ),
        out_shape=[jax.ShapeDtypeStruct((h, slots), BF16) for h in (TILE, first, TILE - first)],
        name="compact",
    )(start, place, amplitudes, pos)


def expand_kernel(tall, cuts, start, ids, *refs):
    n = len(cuts)
    n_in = 1 + max(c[0] for cut in cuts for c in cut)
    in_refs, pos_ref, out_refs, (held, sem) = refs[:n_in], refs[n_in], refs[n_in + 1 : -2], refs[-2:]
    slots = in_refs[0].shape[1]

    def copies():
        out = []
        for k, cut in enumerate(cuts):
            high = 0
            for which, low, size in cut:
                out.append(
                    pltpu.make_async_copy(
                        in_refs[which].at[pl.ds(low, size), :],
                        held.at[k, pl.ds(high, size), pl.ds(0, slots)],
                        sem.at[len(out)],
                    )
                )
                high += size
        return out

    @pl.when(pl.program_id(0) == 0)
    def _():
        for c in copies():
            c.start()
        for k in range(n):
            held[k, :, pl.ds(slots, TILE)] = jnp.zeros((TILE, TILE), BF16)
        for c in copies():
            c.wait()

    wide = pos_ref.shape[1]
    strip = pl.program_id(0) * (wide // TILE)
    for k in range(n):
        for i in range(tall):
            s = ids[k] * tall + i
            slot = pos_ref[pl.ds(s, 1), :]
            for b in range(wide // TILE):
                lanes = pl.ds(b * TILE, TILE)
                at = jnp.minimum(start[s, strip + b] // TILE * TILE, slots - TILE)
                at = pl.multiple_of(at, TILE)
                pick = (iota((2 * TILE, TILE), 0) + at == slot[:, b * TILE : (b + 1) * TILE]).astype(F32).astype(BF16)
                spread = jnp.dot(held[k, :, pl.ds(at, 2 * TILE)], pick, preferred_element_type=F32)
                out_refs[k][pl.ds(i * TILE, TILE), lanes] = spread.astype(BF16)


def expand(start, ids, pos, arrays, cuts, tall, wide=256):
    tiles, pairs = pos.shape
    slots = arrays[0].shape[1]
    n = len(cuts)
    flops = 2 * n * tall * pairs * TILE * 2 * TILE
    return pl.pallas_call(
        functools.partial(expand_kernel, tall, cuts),
        grid_spec=pltpu.PrefetchScalarGridSpec(
            num_scalar_prefetch=2,
            grid=(pairs // wide,),
            in_specs=whole(len(arrays), pltpu.HBM) + [pl.BlockSpec((tiles, wide), lambda i, *_: (0, i))],
            out_specs=[pl.BlockSpec((tall * TILE, wide), lambda i, *_: (0, i))] * n,
            scratch_shapes=[
                pltpu.VMEM((n, TILE, slots + TILE), BF16),
                pltpu.SemaphoreType.DMA((sum(len(c) for c in cuts),)),
            ],
        ),
        out_shape=[jax.ShapeDtypeStruct((tall * TILE, pairs), BF16)] * n,
        compiler_params=pltpu.CompilerParams(vmem_limit_bytes=VMEM_LIMIT),
        cost_estimate=pl.CostEstimate(flops=flops, bytes_accessed=n * tall * TILE * pairs * 3, transcendentals=0),
        name="expand",
    )(start, ids, *arrays, pos)


def product_kernel(n, first, which, *refs):
    a_refs, refs = refs[:5], refs[5:]
    b_refs, refs = refs[:n], refs[n:]
    if not first:
        sums, refs = refs[:2], refs[2:]
    outs, (a_all, b_all, sem) = refs[:-3], refs[-3:]
    rows = outs[0].shape[0]
    high, depth = a_all.shape[0], b_refs[0].shape[0]

    @pl.when(pl.program_id(0) == 0)
    def _():
        for k in range(n):
            target = a_all.at[:, pl.ds(k * depth, depth)]

            @pl.when(which[k] < 4)
            def _():
                pltpu.make_async_copy(a_refs[0].at[which[k]], target, sem.at[k]).start()

            for d in range(4):

                @pl.when(which[k] == 4 + d)
                def _():
                    pltpu.make_async_copy(a_refs[1 + d], target, sem.at[k]).start()

        for k in range(n):
            target = a_all.at[:, pl.ds(k * depth, depth)]
            pltpu.make_async_copy(a_refs[1], target, sem.at[k]).wait()

    for k in range(n):
        b_all[pl.ds(k * depth, depth), :] = b_refs[k][...]
    for h in range(2):
        total = jnp.dot(a_all[pl.ds(h * rows, rows), :], b_all[...], preferred_element_type=F32)
        outs[h][...] = total if first else sums[h][...] + total
    if first:
        flags = [a_all[pl.ds(2 * rows, FLAG_ROWS), pl.ds(k * depth, TILE)].astype(F32) for k in range(n)]
        outs[2][...] = functools.reduce(jnp.maximum, flags)


def product(which, a_parts, blocks, sums=None, wide=256):
    n, (depth, pairs) = len(blocks), blocks[0].shape
    high = a_parts[1].shape[0]
    rows = (high - FLAG_ROWS) // 2
    first = sums is None
    strip = lambda h: pl.BlockSpec((h, wide), lambda i, *_: (0, i))
    out = [jax.ShapeDtypeStruct((rows, pairs), F32)] * 2
    out_specs = [strip(rows)] * 2
    if first:
        out.append(jax.ShapeDtypeStruct((FLAG_ROWS, TILE), F32))
        out_specs.append(pl.BlockSpec((FLAG_ROWS, TILE), lambda i, *_: (0, 0)))
    return pl.pallas_call(
        functools.partial(product_kernel, n, first),
        grid_spec=pltpu.PrefetchScalarGridSpec(
            num_scalar_prefetch=1,
            grid=(pairs // wide,),
            in_specs=whole(5, pltpu.HBM) + [strip(depth)] * n + ([] if first else [strip(rows)] * 2),
            out_specs=out_specs,
            scratch_shapes=[
                pltpu.VMEM((high, n * depth), BF16),
                pltpu.VMEM((n * depth, wide), BF16),
                pltpu.SemaphoreType.DMA((n,)),
            ],
        ),
        out_shape=out,
        compiler_params=pltpu.CompilerParams(vmem_limit_bytes=VMEM_LIMIT),
        cost_estimate=pl.CostEstimate(
            flops=4 * rows * n * depth * pairs, bytes_accessed=2 * n * depth * (high + pairs) + 8 * rows * pairs, transcendentals=0
        ),
        name="product",
    )(which, *a_parts, *blocks, *(() if first else sums))


def shift(value, axis, by):
    n = lax.axis_size(axis)
    return lax.ppermute(value, axis, [(i, (i + by) % n) for i in range(n)])


def after(value, *others):
    return lax.optimization_barrier((value, *others))[0]


def dense(integrals, amplitudes, tile_pattern, pair_domain, tile_order):
    count = tile_order.shape[0]
    placed = (tile_order[:, None] == jnp.arange(count, dtype=I32)[None, :]).astype(F32)
    exact = functools.partial(jnp.dot, precision=lax.Precision.HIGHEST)
    pattern = exact(exact(placed, tile_pattern.astype(F32)), placed.T)
    domain = exact(placed, pair_domain.astype(F32))
    here = count // (lax.axis_size(ROW))
    pattern = lax.dynamic_slice_in_dim(pattern, lax.axis_index(ROW) * here, here, 0)
    mask = jnp.repeat(jnp.repeat(pattern, TILE, axis=0), TILE, axis=1).astype(BF16)
    screened = lax.all_gather(integrals, COL, axis=1, tiled=True) * mask
    domain = jnp.repeat(domain, TILE, axis=0).astype(BF16)
    restricted = lax.all_gather(amplitudes, ROW, axis=0, tiled=True) * domain
    return jnp.dot(screened, restricted, preferred_element_type=F32)


def on_device(integrals, amplitudes, tile_pattern, pair_domain, tile_order):
    zh, x, core = lax.axis_index("zh"), lax.axis_index("x"), lax.axis_index("core")
    zl, y = lax.axis_index("zl"), lax.axis_index("y")
    tall = amplitudes.shape[0] // TILE
    slots = amplitudes.shape[1] * tall * 5 // 9 // TILE * TILE
    first = TILE * 3 // 4
    place = jnp.stack([(zh * 4 + x) * 2 + core, zl * 4 + y, core]).astype(I32)
    keep, send, pos, start = plan(integrals, tile_pattern, pair_domain, tile_order, place, tall, slots)
    u, f, g = compact(start, place, amplitudes, pos, slots, first)

    a_here = jnp.concatenate([shift(send, "core", 1), keep], axis=0)
    a_own = lax.all_gather(a_here, "y", axis=0, tiled=False)
    there = shift(a_here, "zl", 1)

    up, um, pf = shift(u, "x", -1), shift(u, "x", 1), shift(f, "zh", 1)
    pg3 = shift(jnp.concatenate([g, up[first:], um[first:]], axis=0), "zh", 1)
    pf_up, pf_um = shift(pf, "x", -1), shift(pf, "x", 1)
    t_up, t_um = shift(there, "y", -1), shift(there, "y", 1)
    rest = TILE - first
    u2 = shift(um, "x", 1)
    pf2 = shift(pf_up, "x", -1)
    pg2 = shift(pg3[rest : 2 * rest], "x", -1)
    t_two = shift(t_um, "y", 1)
    a_parts = [a_own, there, t_up, t_two, t_um]

    def shard(dz, dx):
        return (((zh + dz) % 2) * 4 + (x + dx) % 4) * 2 + core

    def where(dz, dx):
        far, across = (zh + dz) % 2, (x + dx) % 4
        return jnp.where(far == zl, across, 4 + (across - y) % 4)

    def listed(of, pairs):
        return jnp.stack([of(*p) for p in pairs]).astype(I32)

    near, far, last = [(0, 0), (0, 1), (0, 3)], [(1, 0), (1, 1), (1, 3)], [(0, 2), (1, 2)]
    whole_cut = [[(k, 0, TILE)] for k in range(3)]
    blocks = expand(start, listed(shard, near), pos, [u, up, um], whole_cut, tall)
    far_cut = [[(k, 0, first), (3, k * rest, rest)] for k in range(3)]
    blocks += expand(start, listed(shard, far), pos, [pf, pf_up, pf_um, pg3], far_cut, tall)
    last_cut = [[(0, 0, TILE)], [(1, 0, first), (2, 0, rest)]]
    final = expand(start, listed(shard, last), pos, [u2, pf2, pg2], last_cut, tall)
    *sums, flags = product(listed(where, near + far), a_parts, blocks)
    other, own = product(listed(where, last), a_parts, final, sums)
    theirs = shift(other, "core", 1)
    return lax.cond(
        jnp.max(flags) > 0.5,
        lambda *args: dense(*args[:5]),
        lambda *args: args[5] + args[6],
        integrals,
        amplitudes,
        tile_pattern,
        pair_domain,
        tile_order,
        own,
        theirs,
    )


def solution(mesh):
    fine = Mesh(np.asarray(mesh.devices).reshape(SIZES), AXES)
    return jax.shard_map(
        on_device,
        mesh=fine,
        in_specs=(P(ROW, COL), P(ROW, COL), P(), P(None, COL), P()),
        out_specs=P(ROW, COL),
        check_vma=False,
    )
```

time: 213 us -> 141 us (0.66)
  waiting for transfers between devices: 163 us -> 36.9 us
  Pallas kernels: 0 us -> 53.5 us
  starting transfers between devices: 0.04 us -> 19.6 us
  matrix products: 16.1 us -> 0 us
  other arithmetic: 16.6 us -> 8.26 us
  local copies, waits for them, and re-layouts: 2.92 us -> 6.59 us
    all_gather x2 -> x1, waiting for transfers between devices: 162 us -> 0.02 us  [on_device(): a_own = lax.all_gather(a_here, 'y', axis=0, tiled=False)]
    pallas_call x0 -> x7, Pallas kernels: none -> 53.5 us  [the longest x3 23.6 us: expand(): pl.pallas_call(functools.partial(expand_kernel, tall, cuts), grid_spec=pl...]
    ppermute x0 -> x15, waiting for transfers between devices: none -> 36.9 us  [shift(): return lax.ppermute(value, axis, [(i, (i + by) % n) for i in range(n)])]
    ppermute x0 -> x15, starting transfers between devices: none -> 19.6 us  [shift(): return lax.ppermute(value, axis, [(i, (i + by) % n) for i in range(n)])]
    mul x1 -> x0, other arithmetic: 16.6 us -> none  [on_device(): restricted = amplitude_full * domain_mask]
    dot_general x4 -> x0, matrix products: 16.1 us -> none  [the longest x1 13 us: on_device(): jnp.dot(lax.all_gather(integrals, 'col', axis=1, tiled=True) * integral_m...]
    add x0 -> x1, other arithmetic: none -> 3.45 us  [on_device(): args[5] + args[6]]
    another operation x0 -> x5, other arithmetic: none -> 3.27 us  [the longest x4 2.62 us: listed(): return jnp.stack([of(*p) for p in pairs]).astype(I32)]
  transfers between devices with their start and end apart: 2 -> 16, of which waited for: 2 -> 5; matrix products, arithmetic and copies ran while one was open for 9% -> 5% of each run, Pallas kernels for 0% -> 20%
where the time goes in v1:
time: 141 us; the launch traced here: 139 us
  Pallas kernels  53.5 us (38%)
  waiting for transfers between devices  36.9 us (26%)
  starting transfers between devices  19.6 us (14%)
  between operations  14.3 us (10%)
  other arithmetic  8.26 us (6%)
  local copies, waits for them, and re-layouts  6.59 us (5%)
    ppermute x15, waiting for transfers between devices, shift(): return lax.ppermute(value, axis, [(i, (i + by) % n) for i in range(n)])  36.9 us
    pallas_call x3, Pallas kernels, expand(): pl.pallas_call(functools.partial(expand_kernel, tall, cuts), grid_spec=pl...  23.6 us
    pallas_call x2, Pallas kernels, product(): pl.pallas_call(functools.partial(product_kernel, n, first), grid_spec=plt...  21.9 us
    ppermute x15, starting transfers between devices, shift(): return lax.ppermute(value, axis, [(i, (i + by) % n) for i in range(n)])  19.6 us
    pallas_call x1, Pallas kernels, compact(): pl.pallas_call(functools.partial(compact_kernel, slots), grid_spec=pltpu....  4.11 us
    pallas_call x1, Pallas kernels, plan(): pl.pallas_call(functools.partial(plan_kernel, tall, slots), grid_spec=plt...  3.91 us
    add x1, other arithmetic, on_device(): args[5] + args[6]  3.45 us
    unnamed x21, local copies, waits for them, and re-layouts  3.09 us
  transfers between devices with their start and end apart: 16, of which 5 were waited for; matrix products, arithmetic and copies ran while one was open for 5% of the time, Pallas kernels for 20%

profile of v1, /device:TPU:1, one launch (start us, length us, event | category | flops | bytes accessed | tf_op | source)
XLA Modules:
  0.0 139.2 jit_solution(13988494438750283711)
XLA Ops:
  6.5 0.0 all-gather.9.cloned.1.call-start
  6.5 0.7 pad_add_fusion.place
  7.2 3.9 %plan.1 = (bf16[392,384]{1,0:T(8,128)(2,1)}, bf16[384,384]{1,0:T(8,128)(2,1)}, s32[48,1536]{1,0:T(8,128)}, s32[48,128]{1,0:T(8,128)}) custom-call(s32[48]{0:T(128)} %order.1, s32[48,48]{1,0:T(8,128)} %pattern.1, s32[3]{0:T(128)} %pad_add_fusion.place, bf16[384,768]{1,0:T(8,128)(2,1)} %a_ref.1, s32[48,1536]{1,0:T(8,128)} %d_ref.1), custom_call_target="tpu_custom_call" | custom-call | tf_op jit(solution)/shard_map/plan/pallas_call | solution.py:69
  11.1 1.4 %collective-permute-start = (bf16[384,384]{1,0:T(8,128)(2,1)}, bf16[384,384]{1,0:T(8,128)(2,1)S(1)}, u32[]{:S(2)}, u32[]{:S(2)}) collective-permute-start(bf16[384,384]{1,0:T(8,128)(2,1)} %get-tuple-element.49), channel_id=1, source_target_pairs={{0,8},{8,0},{1,9},{9,1},{2,10},{10,2},{3,11},{11,3},{4,12},{12,4},... | collective-permute-start | bytes 884744 | tf_op jit(solution)/shard_map/ppermute | solution.py:267
  12.5 1.4 %collective-permute-done = bf16[384,384]{1,0:T(8,128)(2,1)S(1)} collective-permute-done((bf16[384,384]{1,0:T(8,128)(2,1)}, bf16[384,384]{1,0:T(8,128)(2,1)S(1)}, u32[]{:S(2)}, u32[]{:S(2)}) %collective-permute-start) | collective-permute-done | bytes 294944 | tf_op jit(solution)/shard_map/ppermute | solution.py:267
  14.0 1.0 constant_dynamic-update-slice_fusion
  15.0 0.0 copy-start.2
  15.0 0.8 copy-done.2
  15.8 0.0 all-gather.9.cloned.1.call-update
  15.9 0.0 copy-done
  15.9 4.1 %compact.1 = (bf16[128,2560]{1,0:T(8,128)(2,1)}, bf16[96,2560]{1,0:T(8,128)(2,1)}, bf16[32,2560]{1,0:T(8,128)(2,1)}) custom-call(s32[48,128]{1,0:T(8,128)} %get-tuple-element.51.start, s32[3]{0:T(128)} %pad_add_fusion.place, bf16[384,1536]{1,0:T(8,128)(2,1)S(1)} %copy-done, s32[48,1536]{1,0:T(8,128)} %get-tuple-element.52.pos_ref.refs_3_.refs_4_), custom_call_target="tpu_custom_call" | custom-call | tf_op jit(solution)/shard_map/compact/pallas_call | solution.py:111
  20.0 1.3 collective-permute-start.6
  21.3 1.4 %collective-permute-start.5 = (bf16[128,2560]{1,0:T(8,128)(2,1)}, bf16[128,2560]{1,0:T(8,128)(2,1)S(1)}, u32[]{:S(2)}, u32[]{:S(2)}) collective-permute-start(bf16[128,2560]{1,0:T(8,128)(2,1)} %get-tuple-element.53.refs_0_), channel_id=1, source_target_pairs={{0,48},{16,0},{32,16},{48,32},{1,49},{17,1},{33,17},{49,33},{2,50}... | collective-permute-start | bytes 1966088 | tf_op jit(solution)/shard_map/ppermute | solution.py:267
  22.7 1.7 %collective-permute-start.1 = (bf16[776,384]{1,0:T(8,128)(2,1)}, bf16[776,384]{1,0:T(8,128)(2,1)S(1)}, u32[]{:S(2)}, u32[]{:S(2)}) collective-permute-start(bf16[776,384]{1,0:T(8,128)(2,1)} %copy-done.2), channel_id=1, source_target_pairs={{0,4},{4,0},{1,5},{5,1},{2,6},{6,2},{3,7},{7,3},{8,12},{12,8},{9,1... | collective-permute-start | bytes 1787912 | tf_op jit(solution)/shard_map/ppermute | solution.py:267
  24.4 3.3 %collective-permute-start.7 = (bf16[96,2560]{1,0:T(8,128)(2,1)}, bf16[96,2560]{1,0:T(8,128)(2,1)}, u32[]{:S(2)}, u32[]{:S(2)}) collective-permute-start(bf16[96,2560]{1,0:T(8,128)(2,1)} %get-tuple-element.57), channel_id=1, source_target_pairs={{0,64},{64,0},{1,65},{65,1},{2,66},{66,2},{3,67},{67,3},{4,68},{68... | collective-permute-start | bytes 1474568 | tf_op jit(solution)/shard_map/ppermute | solution.py:267
  27.7 23.4 %collective-permute-done.7.refs_0_ = bf16[96,2560]{1,0:T(8,128)(2,1)} collective-permute-done((bf16[96,2560]{1,0:T(8,128)(2,1)}, bf16[96,2560]{1,0:T(8,128)(2,1)}, u32[]{:S(2)}, u32[]{:S(2)}) %collective-permute-start.7) | collective-permute-done | bytes 491552 | tf_op jit(solution)/shard_map/ppermute | solution.py:267
  51.1 1.3 collective-permute-start.8
  52.4 0.0 collective-permute-done.6.refs_2_
  52.4 0.9 slice.13
  53.3 0.0 collective-permute-done.5.refs_1_
  53.3 0.0 copy-start.6
  53.3 0.0 collective-permute-done.1.refs_1_
  53.3 0.0 copy-start.3
  53.4 1.4 collective-permute-start.3
  54.7 0.0 copy-done.6
  54.7 0.9 pad_maximum_fusion
  55.7 0.1 collective-permute-start.10
  55.8 0.3 collective-permute-start.9
  56.0 0.1 collective-permute-start.11
  56.1 6.1 %collective-permute-done.8.refs_1_ = bf16[96,2560]{1,0:T(8,128)(2,1)} collective-permute-done((bf16[96,2560]{1,0:T(8,128)(2,1)}, bf16[96,2560]{1,0:T(8,128)(2,1)}, u32[]{:S(2)}, u32[]{:S(2)}) %collective-permute-start.8) | collective-permute-done | bytes 491552 | tf_op jit(solution)/shard_map/ppermute | solution.py:267
  62.3 2.8 %collective-permute-start.2 = (bf16[776,384]{1,0:T(8,128)(2,1)S(1)}, bf16[776,384]{1,0:T(8,128)(2,1)S(1)}, u32[]{:S(2)}, u32[]{:S(2)}) collective-permute-start(bf16[776,384]{1,0:T(8,128)(2,1)S(1)} %collective-permute-done.1.refs_1_), channel_id=1, source_target_pairs={{0,3},{1,0},{2,1},{3,2},{4,7},{5,4},{6,5},{7,6},{8,11},{9,8},{10,9... | collective-permute-start | bytes 1787912 | tf_op jit(solution)/shard_map/ppermute | solution.py:267
  65.0 2.7 %collective-permute-done.3.refs_4_ = bf16[776,384]{1,0:T(8,128)(2,1)S(1)} collective-permute-done((bf16[776,384]{1,0:T(8,128)(2,1)S(1)}, bf16[776,384]{1,0:T(8,128)(2,1)S(1)}, u32[]{:S(2)}, u32[]{:S(2)}) %collective-permute-start.3) | collective-permute-done | bytes 596000 | tf_op jit(solution)/shard_map/ppermute | solution.py:267
  67.7 0.0 collective-permute-start.4
  67.7 0.7 pad_add_fusion.3.which
  68.4 0.6 stack.81.which
  69.1 0.0 collective-permute-done.10.refs_3_
  69.1 0.5 collective-permute-start.12
  69.6 0.6 pad_add_fusion.4.ids
  70.2 0.7 pad_add_fusion.1.ids
  70.8 0.7 pad_add_fusion.2.ids
  71.5 0.9 slice.14
  72.4 0.0 collective-permute-done.9.refs_2_
  72.4 0.3 collective-permute-start.13
  72.7 8.1 %expand.3 = (bf16[384,1536]{1,0:T(8,128)(2,1)}, bf16[384,1536]{1,0:T(8,128)(2,1)}, bf16[384,1536]{1,0:T(8,128)(2,1)}) custom-call(s32[48,128]{1,0:T(8,128)} %get-tuple-element.51.start, s32[3]{0:T(128)} %pad_add_fusion.1.ids, bf16[128,2560]{1,0:T(8,128)(2,1)} %get-tuple-element.53.refs_0_, bf16[128,2560]{1,0:T(8,128)(2,1)} %copy-done.6, ...), custom_call_target="tpu_custom_call" | custom-call | flops 905969664 | bytes 5308416 | tf_op jit(solution)/shard_map/expand/pallas_call | solution.py:175
  80.8 0.0 copy-done.3
  80.8 8.1 %expand.4 = (bf16[384,1536]{1,0:T(8,128)(2,1)}, bf16[384,1536]{1,0:T(8,128)(2,1)}, bf16[384,1536]{1,0:T(8,128)(2,1)}) custom-call(s32[48,128]{1,0:T(8,128)} %get-tuple-element.51.start, s32[3]{0:T(128)} %pad_add_fusion.2.ids, bf16[96,2560]{1,0:T(8,128)(2,1)} %collective-permute-done.7.refs_0_, bf16[96,2560]{1,0:T(8,128)(2,1)} %collective-permute-done.8.refs_1_, ...), custom_call_target="tpu_custom_call" | custom-call | flops 905969664 | bytes 5308416 | tf_op jit(solution)/shard_map/expand/pallas_call | solution.py:175
  88.9 0.0 collective-permute-done.11.refs_0_
  88.9 0.0 collective-permute-done.13.refs_2_
  88.9 0.0 collective-permute-done.12.refs_1_
  88.9 0.6 copy-done.11
  89.6 0.8 copy-done.10
  90.4 7.4 %expand.5 = (bf16[384,1536]{1,0:T(8,128)(2,1)}, bf16[384,1536]{1,0:T(8,128)(2,1)}) custom-call(s32[48,128]{1,0:T(8,128)} %get-tuple-element.51.start, s32[2]{0:T(128)} %pad_add_fusion.4.ids, bf16[128,2560]{1,0:T(8,128)(2,1)} %collective-permute-done.11.refs_0_, bf16[96,2560]{1,0:T(8,128)(2,1)} %copy-done.10, bf16[32,2560]{1,0:T(8,128)(2,1)} %copy-done.11, ...), custom_call_target="tpu_custom_call" | custom-call | flops 603979776 | bytes 3538944 | tf_op jit(solution)/shard_map/expand/pallas_call | solution.py:175
  97.8 0.0 collective-permute-done.2.refs_2_
  97.8 0.0 collective-permute-done.4.refs_3_
  97.8 0.0 all-gather.9.cloned.1.call-done
  97.9 0.8 copy-done.5
  98.6 12.7 %product.2 = (f32[384,1536]{1,0:T(8,128)}, f32[384,1536]{1,0:T(8,128)}, f32[8,128]{1,0:T(8,128)}) custom-call(s32[6]{0:T(128)} %stack.81.which, bf16[4,776,384]{2,1,0:T(8,128)(2,1)} %bitcast.30, bf16[776,384]{1,0:T(8,128)(2,1)} %copy-done.3, bf16[776,384]{1,0:T(8,128)(2,1)} %copy-done.5, bf16[776,384]{1,0:T(8,128)(2,1)} %collective-permute-done.4.refs_3_, ...), custom_call_target="tpu_custom_call" | custom-call | flops 5435817984 | bytes 15372288 | tf_op jit(solution)/shard_map/product/pallas_call | solution.py:243
  111.3 0.0 copy-start.8
  111.3 9.3 %product.3 = (f32[384,1536]{1,0:T(8,128)}, f32[384,1536]{1,0:T(8,128)S(1)}) custom-call(s32[2]{0:T(128)} %pad_add_fusion.3.which, bf16[4,776,384]{2,1,0:T(8,128)(2,1)} %bitcast.31, bf16[776,384]{1,0:T(8,128)(2,1)} %copy-done.3, bf16[776,384]{1,0:T(8,128)(2,1)} %copy-done.5, bf16[776,384]{1,0:T(8,128)(2,1)} %collective-permute-done.4.refs_3_, ...), custom_call_target="tpu_custom_call" | custom-call | flops 1811939328 | bytes 8269824 | tf_op jit(solution)/shard_map/product/pallas_call | solution.py:243
  120.6 3.8 %collective-permute-start.14 = (f32[384,1536]{1,0:T(8,128)}, f32[384,1536]{1,0:T(8,128)}, u32[]{:S(2)}, u32[]{:S(2)}) collective-permute-start(f32[384,1536]{1,0:T(8,128)} %get-tuple-element.68), channel_id=1, source_target_pairs={{0,8},{8,0},{1,9},{9,1},{2,10},{10,2},{3,11},{11,3},{4,12},{12,4},... | collective-permute-start | bytes 7077896 | tf_op jit(solution)/shard_map/ppermute | solution.py:267
  124.4 0.6 reduce_max.9
  125.7 3.2 %collective-permute-done.14 = f32[384,1536]{1,0:T(8,128)} collective-permute-done((f32[384,1536]{1,0:T(8,128)}, f32[384,1536]{1,0:T(8,128)}, u32[]{:S(2)}, u32[]{:S(2)}) %collective-permute-start.14) | collective-permute-done | bytes 2359328 | tf_op jit(solution)/shard_map/ppermute | solution.py:267
  128.9 3.4 %conditional.1 = (f32[384,1536]{1,0:T(8,128)}) conditional(s32[]{:T(128)} %convert_element_type.28, (f32[384,1536]{1,0:T(8,128)S(1)}, f32[384,1536]{1,0:T(8,128)}) %tuple.11, (bf16[384,768]{1,0:T(8,128)(2,1)}, s32[48]{0:T(128)S(1)}, s32[48,48]{1,0:T(8,128)}, bf16[384,1536]{1,0:T(8,128)(2,1)S(1)}, s32[48,1536]{1,0:T(8,128)}) %tuple.24), branch_computations={%region_1.2_spmd, %region_2.3_spmd} | conditional | flops 7304832000 | bytes 173516032 | solution.py:334
  128.9 3.4 %add.133 = f32[384,1536]{1,0:T(8,128)} add(f32[384,1536]{1,0:T(8,128)S(1)} %get-tuple-element.22, f32[384,1536]{1,0:T(8,128)} %get-tuple-element.23) | non-fusion elementwise | flops 589824 | bytes 7077888 | tf_op jit(solution)/shard_map/cond/branch_0_fun/add | solution.py:337
  (11 shorter events, 0.1 us)
Async XLA Ops:
  6.5 9.3 %copy-start = (bf16[384,1536]{1,0:T(8,128)(2,1)S(1)}, bf16[384,1536]{1,0:T(8,128)(2,1)}, u32[]{:S(2)}) copy-start(bf16[384,1536]{1,0:T(8,128)(2,1)} %b_ref.1) | copy-start | bytes 3538948
  6.5 91.3 %all-gather.9.cloned.1.call-start = ((), (), s32[]{:S(2)}) async-start(), calls=%async_computation.2 | async-start | bytes 2979840 | tf_op jit(solution)/shard_map/all_gather | solution.py:300
  11.1 2.8 %collective-permute-start = (bf16[384,384]{1,0:T(8,128)(2,1)}, bf16[384,384]{1,0:T(8,128)(2,1)S(1)}, u32[]{:S(2)}, u32[]{:S(2)}) collective-permute-start(bf16[384,384]{1,0:T(8,128)(2,1)} %get-tuple-element.49), channel_id=1, source_target_pairs={{0,8},{8,0},{1,9},{9,1},{2,10},{10,2},{3,11},{11,3},{4,12},{12,4},... | collective-permute-start | bytes 884744 | tf_op jit(solution)/shard_map/ppermute | solution.py:267
  15.0 0.8 copy-start.2
  20.0 32.4 %collective-permute-start.6 = (bf16[128,2560]{1,0:T(8,128)(2,1)}, bf16[128,2560]{1,0:T(8,128)(2,1)}, u32[]{:S(2)}, u32[]{:S(2)}) collective-permute-start(bf16[128,2560]{1,0:T(8,128)(2,1)} %get-tuple-element.53.refs_0_), channel_id=1, source_target_pairs={{0,16},{16,32},{32,48},{48,0},{1,17},{17,33},{33,49},{49,1},{2,18}... | collective-permute-start | bytes 1966088 | tf_op jit(solution)/shard_map/ppermute | solution.py:267
  21.3 32.0 %collective-permute-start.5 = (bf16[128,2560]{1,0:T(8,128)(2,1)}, bf16[128,2560]{1,0:T(8,128)(2,1)S(1)}, u32[]{:S(2)}, u32[]{:S(2)}) collective-permute-start(bf16[128,2560]{1,0:T(8,128)(2,1)} %get-tuple-element.53.refs_0_), channel_id=1, source_target_pairs={{0,48},{16,0},{32,16},{48,32},{1,49},{17,1},{33,17},{49,33},{2,50}... | collective-permute-start | bytes 1966088 | tf_op jit(solution)/shard_map/ppermute | solution.py:267
  22.7 30.7 %collective-permute-start.1 = (bf16[776,384]{1,0:T(8,128)(2,1)}, bf16[776,384]{1,0:T(8,128)(2,1)S(1)}, u32[]{:S(2)}, u32[]{:S(2)}) collective-permute-start(bf16[776,384]{1,0:T(8,128)(2,1)} %copy-done.2), channel_id=1, source_target_pairs={{0,4},{4,0},{1,5},{5,1},{2,6},{6,2},{3,7},{7,3},{8,12},{12,8},{9,1... | collective-permute-start | bytes 1787912 | tf_op jit(solution)/shard_map/ppermute | solution.py:267
  24.4 26.7 %collective-permute-start.7 = (bf16[96,2560]{1,0:T(8,128)(2,1)}, bf16[96,2560]{1,0:T(8,128)(2,1)}, u32[]{:S(2)}, u32[]{:S(2)}) collective-permute-start(bf16[96,2560]{1,0:T(8,128)(2,1)} %get-tuple-element.57), channel_id=1, source_target_pairs={{0,64},{64,0},{1,65},{65,1},{2,66},{66,2},{3,67},{67,3},{4,68},{68... | collective-permute-start | bytes 1474568 | tf_op jit(solution)/shard_map/ppermute | solution.py:267
  51.1 11.2 %collective-permute-start.8 = (bf16[96,2560]{1,0:T(8,128)(2,1)}, bf16[96,2560]{1,0:T(8,128)(2,1)}, u32[]{:S(2)}, u32[]{:S(2)}) collective-permute-start(bf16[96,2560]{1,0:T(8,128)(2,1)} %collective-permute-done.7.refs_0_), channel_id=1, source_target_pairs={{0,48},{16,0},{32,16},{48,32},{1,49},{17,1},{33,17},{49,33},{2,50}... | collective-permute-start | bytes 1474568 | tf_op jit(solution)/shard_map/ppermute | solution.py:267
  53.3 1.4 %copy-start.6 = (bf16[128,2560]{1,0:T(8,128)(2,1)}, bf16[128,2560]{1,0:T(8,128)(2,1)S(1)}, u32[]{:S(2)}) copy-start(bf16[128,2560]{1,0:T(8,128)(2,1)S(1)} %collective-permute-done.5.refs_1_) | copy-start | bytes 1966084
  53.3 27.5 %copy-start.3 = (bf16[776,384]{1,0:T(8,128)(2,1)}, bf16[776,384]{1,0:T(8,128)(2,1)S(1)}, u32[]{:S(2)}) copy-start(bf16[776,384]{1,0:T(8,128)(2,1)S(1)} %collective-permute-done.1.refs_1_) | copy-start | bytes 1787908
  53.4 14.4 %collective-permute-start.3 = (bf16[776,384]{1,0:T(8,128)(2,1)S(1)}, bf16[776,384]{1,0:T(8,128)(2,1)S(1)}, u32[]{:S(2)}, u32[]{:S(2)}) collective-permute-start(bf16[776,384]{1,0:T(8,128)(2,1)S(1)} %collective-permute-done.1.refs_1_), channel_id=1, source_target_pairs={{0,1},{1,2},{2,3},{3,0},{4,5},{5,6},{6,7},{7,4},{8,9},{9,10},{10,1... | collective-permute-start | bytes 1787912 | tf_op jit(solution)/shard_map/ppermute | solution.py:267
  55.7 13.4 %collective-permute-start.10 = (bf16[96,2560]{1,0:T(8,128)(2,1)S(1)}, bf16[96,2560]{1,0:T(8,128)(2,1)}, u32[]{:S(2)}, u32[]{:S(2)}) collective-permute-start(bf16[96,2560]{1,0:T(8,128)(2,1)S(1)} %pad_maximum_fusion), channel_id=1, source_target_pairs={{0,64},{64,0},{1,65},{65,1},{2,66},{66,2},{3,67},{67,3},{4,68},{68... | collective-permute-start | bytes 1474568 | tf_op jit(solution)/shard_map/ppermute | solution.py:267
  55.8 16.6 %collective-permute-start.9 = (bf16[96,2560]{1,0:T(8,128)(2,1)}, bf16[96,2560]{1,0:T(8,128)(2,1)}, u32[]{:S(2)}, u32[]{:S(2)}) collective-permute-start(bf16[96,2560]{1,0:T(8,128)(2,1)} %collective-permute-done.7.refs_0_), channel_id=1, source_target_pairs={{0,16},{16,32},{32,48},{48,0},{1,17},{17,33},{33,49},{49,1},{2,18}... | collective-permute-start | bytes 1474568 | tf_op jit(solution)/shard_map/ppermute | solution.py:267
  56.0 32.9 %collective-permute-start.11 = (bf16[128,2560]{1,0:T(8,128)(2,1)}, bf16[128,2560]{1,0:T(8,128)(2,1)}, u32[]{:S(2)}, u32[]{:S(2)}) collective-permute-start(bf16[128,2560]{1,0:T(8,128)(2,1)} %collective-permute-done.6.refs_2_), channel_id=1, source_target_pairs={{0,16},{16,32},{32,48},{48,0},{1,17},{17,33},{33,49},{49,1},{2,18}... | collective-permute-start | bytes 1966088 | tf_op jit(solution)/shard_map/ppermute | solution.py:267
  62.3 35.5 %collective-permute-start.2 = (bf16[776,384]{1,0:T(8,128)(2,1)S(1)}, bf16[776,384]{1,0:T(8,128)(2,1)S(1)}, u32[]{:S(2)}, u32[]{:S(2)}) collective-permute-start(bf16[776,384]{1,0:T(8,128)(2,1)S(1)} %collective-permute-done.1.refs_1_), channel_id=1, source_target_pairs={{0,3},{1,0},{2,1},{3,2},{4,7},{5,4},{6,5},{7,6},{8,11},{9,8},{10,9... | collective-permute-start | bytes 1787912 | tf_op jit(solution)/shard_map/ppermute | solution.py:267
  67.7 21.2 %copy-start.4 = (bf16[776,384]{1,0:T(8,128)(2,1)}, bf16[776,384]{1,0:T(8,128)(2,1)S(1)}, u32[]{:S(2)}) copy-start(bf16[776,384]{1,0:T(8,128)(2,1)S(1)} %collective-permute-done.3.refs_4_) | copy-start | bytes 1787908
  67.7 30.1 %collective-permute-start.4 = (bf16[776,384]{1,0:T(8,128)(2,1)S(1)}, bf16[776,384]{1,0:T(8,128)(2,1)}, u32[]{:S(2)}, u32[]{:S(2)}) collective-permute-start(bf16[776,384]{1,0:T(8,128)(2,1)S(1)} %collective-permute-done.3.refs_4_), channel_id=1, source_target_pairs={{0,1},{1,2},{2,3},{3,0},{4,5},{5,6},{6,7},{7,4},{8,9},{9,10},{10,1... | collective-permute-start | bytes 1787912 | tf_op jit(solution)/shard_map/ppermute | solution.py:267
  69.1 19.9 %collective-permute-start.12 = (bf16[96,2560]{1,0:T(8,128)(2,1)}, bf16[96,2560]{1,0:T(8,128)(2,1)S(1)}, u32[]{:S(2)}, u32[]{:S(2)}) collective-permute-start(bf16[96,2560]{1,0:T(8,128)(2,1)} %collective-permute-done.8.refs_1_), channel_id=1, source_target_pairs={{0,48},{16,0},{32,16},{48,32},{1,49},{17,1},{33,17},{49,33},{2,50}... | collective-permute-start | bytes 1474568 | tf_op jit(solution)/shard_map/ppermute | solution.py:267
  72.4 16.5 %collective-permute-start.13 = (bf16[32,2560]{1,0:T(8,128)(2,1)S(1)}, bf16[32,2560]{1,0:T(8,128)(2,1)S(1)}, u32[]{:S(2)}, u32[]{:S(2)}) collective-permute-start(bf16[32,2560]{1,0:T(8,128)(2,1)S(1)} %slice.14), channel_id=1, source_target_pairs={{0,48},{16,0},{32,16},{48,32},{1,49},{17,1},{33,17},{49,33},{2,50}... | collective-permute-start | bytes 491528 | tf_op jit(solution)/shard_map/ppermute | solution.py:267
  88.9 0.7 copy-start.11
  89.6 0.8 copy-start.10
  97.8 0.8 copy-start.5
  111.3 13.1 %copy-start.7 = (f32[8,128]{1,0:T(8,128)S(1)}, f32[8,128]{1,0:T(8,128)}, u32[]{:S(2)}) copy-start(f32[8,128]{1,0:T(8,128)} %get-tuple-element.62) | copy-start | bytes 12292
  111.3 17.6 %copy-start.8 = (s32[48]{0:T(128)S(1)}, s32[48]{0:T(128)}, u32[]{:S(2)}) copy-start(s32[48]{0:T(128)} %order.1) | copy-start | bytes 580
  120.6 8.3 %collective-permute-start.14 = (f32[384,1536]{1,0:T(8,128)}, f32[384,1536]{1,0:T(8,128)}, u32[]{:S(2)}, u32[]{:S(2)}) collective-permute-start(f32[384,1536]{1,0:T(8,128)} %get-tuple-element.68), channel_id=1, source_target_pairs={{0,8},{8,0},{1,9},{9,1},{2,10},{10,2},{3,11},{11,3},{4,12},{12,4},... | collective-permute-start | bytes 7077896 | tf_op jit(solution)/shard_map/ppermute | solution.py:267
Sparse Core Ops, SparseCore 0:
  16.0 35.3 all-gather.8

commit v2 on v1

v2 whole, which is shorter than its diff:
```python
import functools

import jax
import jax.numpy as jnp
import numpy as np
from jax import lax
from jax.experimental import pallas as pl
from jax.experimental.pallas import tpu as pltpu
from jax.sharding import Mesh, PartitionSpec as P

TILE = 128
AXES = ("zh", "x", "core", "zl", "y")
SIZES = (2, 4, 2, 2, 4)
ROW, COL = ("zh", "x", "core"), ("zl", "y")
BF16, F32, I32 = jnp.bfloat16, jnp.float32, jnp.int32
FLAG_ROWS = 8
VMEM_LIMIT = 60 << 20


def iota(shape, dim):
    return lax.broadcasted_iota(I32, shape, dim)


def whole(n, space=pltpu.VMEM):
    return [pl.BlockSpec(memory_space=space)] * n


def screen_kernel(tall, order, pattern, place, a_ref, keep_ref, send_ref):
    row, col, core = place[0], place[1], place[2]
    rows, cols = a_ref.shape
    half = cols // TILE // 2
    for i in range(rows // TILE):
        high = pl.ds(i * TILE, TILE)
        for j in range(half):
            for ref, base in ((keep_ref, core * half), (send_ref, (1 - core) * half)):
                tile = base + j
                on = pattern[order[row * tall + i], order[col * 2 * half + tile]]
                scale = on.astype(F32).astype(BF16)
                part = a_ref[high, pl.ds(pl.multiple_of(tile * TILE, TILE), TILE)]
                ref[high, pl.ds(j * TILE, TILE)] = part * scale


def screen(integrals, tile_pattern, tile_order, place, tall):
    rows, cols = integrals.shape
    return pl.pallas_call(
        functools.partial(screen_kernel, tall),
        grid_spec=pltpu.PrefetchScalarGridSpec(num_scalar_prefetch=3, grid=(), in_specs=whole(1), out_specs=whole(2)),
        out_shape=[jax.ShapeDtypeStruct((rows, cols // 2), BF16)] * 2,
        name="screen",
    )(tile_order, tile_pattern, place, integrals)


def plan_kernel(tall, slots, order, d_ref, pos_ref, start_ref, flag_ref, dom):
    tiles, pairs = dom.shape
    for s in range(tiles):
        dom[pl.ds(s, 1), :] = d_ref[pl.ds(order[s], 1), :]
    live = dom[...].astype(F32).astype(BF16)
    blocks = pairs // TILE
    spread = (iota((pairs, TILE), 0) // TILE == iota((pairs, TILE), 1)).astype(F32).astype(BF16)
    counts = jnp.dot(live, spread, preferred_element_type=F32)
    below = (iota((TILE, TILE), 0) < iota((TILE, TILE), 1)).astype(F32).astype(BF16)
    upto = (iota((TILE, TILE), 0) <= iota((TILE, TILE), 1)).astype(F32).astype(BF16)
    s0, s1 = iota((tiles, tiles), 0), iota((tiles, tiles), 1)
    before = ((s0 // tall == s1 // tall) & (s1 < s0)).astype(F32).astype(BF16)
    counted = counts.astype(BF16)
    ahead = jnp.sum(jnp.dot(before, counted, preferred_element_type=F32), axis=1, keepdims=True)
    starts = jnp.dot(counted, below, preferred_element_type=F32) + ahead
    start_ref[...] = starts.astype(I32)
    for b in range(blocks):
        lanes = pl.ds(b * TILE, TILE)
        here = live[:, b * TILE : (b + 1) * TILE]
        slot = jnp.dot(here, upto, preferred_element_type=F32) + (starts[:, b : b + 1] - 1.0)
        pos_ref[:, lanes] = jnp.where(dom[:, lanes] > 0, slot.astype(I32), -1)
    most = jnp.max(ahead + jnp.sum(counts, axis=1, keepdims=True), axis=0, keepdims=True)
    flag_ref[...] = jnp.broadcast_to(jnp.where(most > slots, 1.0, 0.0).astype(F32), flag_ref.shape).astype(BF16)


def plan(pair_domain, tile_order, tall, slots, cols):
    tiles, pairs = pair_domain.shape
    return pl.pallas_call(
        functools.partial(plan_kernel, tall, slots),
        grid_spec=pltpu.PrefetchScalarGridSpec(
            num_scalar_prefetch=1,
            grid=(),
            in_specs=whole(1),
            out_specs=whole(3),
            scratch_shapes=[pltpu.VMEM((tiles, pairs), I32)],
        ),
        out_shape=[
            jax.ShapeDtypeStruct((tiles, pairs), I32),
            jax.ShapeDtypeStruct((tiles, TILE), I32),
            jax.ShapeDtypeStruct((FLAG_ROWS, cols), BF16),
        ],
        name="plan",
    )(tile_order, pair_domain)


def compact_kernel(slots, start, place, b_ref, pos_ref, u_ref, total):
    tall = b_ref.shape[0] // TILE
    total[...] = jnp.zeros_like(total)
    for i in range(tall):
        s = place[0] * tall + i
        slot = pos_ref[pl.ds(s, 1), :]
        for b in range(b_ref.shape[1] // TILE):
            lanes = pl.ds(b * TILE, TILE)
            at = jnp.minimum(start[s, b] // TILE * TILE, slots)
            at = pl.multiple_of(at, TILE)
            pick = (iota((2 * TILE, TILE), 0) + at == slot[:, b * TILE : (b + 1) * TILE]).astype(F32).astype(BF16)
            moved = lax.dot_general(
                b_ref[pl.ds(i * TILE, TILE), lanes], pick, (((1,), (1,)), ((), ())), preferred_element_type=F32
            )
            total[:, pl.ds(at, 2 * TILE)] += moved
    u_ref[...] = total[:, :slots].astype(BF16)


def compact(start, place, amplitudes, pos, slots):
    return pl.pallas_call(
        functools.partial(compact_kernel, slots),
        grid_spec=pltpu.PrefetchScalarGridSpec(
            num_scalar_prefetch=2,
            grid=(),
            in_specs=whole(2),
            out_specs=pl.BlockSpec(memory_space=pltpu.VMEM),
            scratch_shapes=[pltpu.VMEM((TILE, slots + 2 * TILE), F32)],
        ),
        out_shape=jax.ShapeDtypeStruct((TILE, slots), BF16),
        name="compact",
    )(start, place, amplitudes, pos)


def product_kernel(tall, n, na, nb, first, start, ids, which, source, *refs):
    a_refs, in_refs, pos_ref, refs = refs[:na], refs[na : na + nb], refs[na + nb], refs[na + nb + 1 :]
    if not first:
        sums, refs = refs[:3], refs[3:]
    outs, (a_all, held, b_all, a_sem, sem) = refs[:3], refs[3:]
    rows = outs[0].shape[0]
    slots = in_refs[0].shape[1]
    depth = tall * TILE

    def fetch(options, choice, target, done):
        for j, option in enumerate(options):

            @pl.when(choice == j)
            def _(option=option):
                pltpu.make_async_copy(option, target, done).start()

    def a_slot(k):
        return a_all.at[:, pl.ds(k * depth, depth)]

    def b_slot(k):
        return held.at[k, :, pl.ds(0, slots)]

    @pl.when(pl.program_id(0) == 0)
    def _():
        for k in range(n):
            fetch(in_refs, source[k], b_slot(k), sem.at[k])
        for k in range(n):
            fetch(a_refs, which[k], a_slot(k), a_sem.at[k])
            held[k, :, pl.ds(slots, TILE)] = jnp.zeros((TILE, TILE), BF16)
        for k in range(n):
            pltpu.make_async_copy(in_refs[0], b_slot(k), sem.at[k]).wait()

    wide = pos_ref.shape[1]
    strip = pl.program_id(0) * (wide // TILE)
    lines = iota((2 * TILE, TILE), 0).astype(F32).astype(BF16)
    for k in range(n):
        for i in range(tall):
            s = ids[k] * tall + i
            slot = pos_ref[pl.ds(s, 1), :]
            for b in range(wide // TILE):
                at = jnp.minimum(start[s, strip + b] // TILE * TILE, slots - TILE)
                at = pl.multiple_of(at, TILE)
                here = slot[:, b * TILE : (b + 1) * TILE] - at
                here = jnp.where((here < 0) | (here >= 2 * TILE), -1, here).astype(F32).astype(BF16)
                pick = jnp.where(lines == here, jnp.ones((), BF16), jnp.zeros((), BF16))
                spread = jnp.dot(held[k, :, pl.ds(at, 2 * TILE)], pick, preferred_element_type=F32)
                b_all[pl.ds((k * tall + i) * TILE, TILE), pl.ds(b * TILE, TILE)] = spread.astype(BF16)

    @pl.when(pl.program_id(0) == 0)
    def _():
        for k in range(n):
            pltpu.make_async_copy(a_refs[0], a_slot(k), a_sem.at[k]).wait()

    for h in range(2):
        total = jnp.dot(a_all[pl.ds(h * rows, rows), :], b_all[...], preferred_element_type=F32)
        outs[h][...] = total if first else sums[h][...] + total
    flags = [a_all[pl.ds(2 * rows, FLAG_ROWS), pl.ds(k * depth, TILE)].astype(F32) for k in range(n)]
    if not first:
        flags.append(sums[2][...])
    outs[2][...] = functools.reduce(jnp.maximum, flags)


def product(start, ids, which, source, a_parts, arrays, pos, tall, sums=None, wide=512):
    n, (tiles, pairs) = ids.shape[0], pos.shape
    slots = arrays[0].shape[1]
    depth = tall * TILE
    high = a_parts[0].shape[0]
    rows = (high - FLAG_ROWS) // 2
    first = sums is None
    strip = lambda h: pl.BlockSpec((h, wide), lambda i, *_: (0, i))
    result = [strip(rows)] * 2 + [pl.BlockSpec((FLAG_ROWS, TILE), lambda i, *_: (0, 0))]
    return pl.pallas_call(
        functools.partial(product_kernel, tall, n, len(a_parts), len(arrays), first),
        grid_spec=pltpu.PrefetchScalarGridSpec(
            num_scalar_prefetch=4,
            grid=(pairs // wide,),
            in_specs=whole(len(a_parts) + len(arrays), pltpu.HBM) + [strip(tiles)] + ([] if first else result),
            out_specs=result,
            scratch_shapes=[
                pltpu.VMEM((high, n * depth), BF16),
                pltpu.VMEM((n, TILE, slots + TILE), BF16),
                pltpu.VMEM((n * depth, wide), BF16),
                pltpu.SemaphoreType.DMA((n,)),
                pltpu.SemaphoreType.DMA((n,)),
            ],
        ),
        out_shape=[jax.ShapeDtypeStruct((rows, pairs), F32)] * 2 + [jax.ShapeDtypeStruct((FLAG_ROWS, TILE), F32)],
        compiler_params=pltpu.CompilerParams(vmem_limit_bytes=VMEM_LIMIT),
        cost_estimate=pl.CostEstimate(
            flops=4 * rows * n * depth * pairs, bytes_accessed=2 * n * depth * (high + pairs) + 8 * rows * pairs, transcendentals=0
        ),
        name="product",
    )(start, ids, which, source, *a_parts, *arrays, pos, *(() if first else sums))


def shift(value, axis, by):
    n = lax.axis_size(axis)
    return lax.ppermute(value, axis, [(i, (i + by) % n) for i in range(n)])


def together(*values):
    return lax.optimization_barrier(values)


def dense(integrals, amplitudes, tile_pattern, pair_domain, tile_order):
    count = tile_order.shape[0]
    placed = (tile_order[:, None] == jnp.arange(count, dtype=I32)[None, :]).astype(F32)
    exact = functools.partial(jnp.dot, precision=lax.Precision.HIGHEST)
    pattern = exact(exact(placed, tile_pattern.astype(F32)), placed.T)
    domain = exact(placed, pair_domain.astype(F32))
    here = count // (lax.axis_size(ROW))
    pattern = lax.dynamic_slice_in_dim(pattern, lax.axis_index(ROW) * here, here, 0)
    mask = jnp.repeat(jnp.repeat(pattern, TILE, axis=0), TILE, axis=1).astype(BF16)
    screened = lax.all_gather(integrals, COL, axis=1, tiled=True) * mask
    domain = jnp.repeat(domain, TILE, axis=0).astype(BF16)
    restricted = lax.all_gather(amplitudes, ROW, axis=0, tiled=True) * domain
    return jnp.dot(screened, restricted, preferred_element_type=F32)


def on_device(integrals, amplitudes, tile_pattern, pair_domain, tile_order):
    zh, x, core = lax.axis_index("zh"), lax.axis_index("x"), lax.axis_index("core")
    zl, y = lax.axis_index("zl"), lax.axis_index("y")
    tall = amplitudes.shape[0] // TILE
    slots = amplitudes.shape[1] * tall * 5 // 9 // TILE * TILE
    place = jnp.stack([(zh * 4 + x) * 2 + core, zl * 4 + y, core]).astype(I32)
    keep, send = screen(integrals, tile_pattern, tile_order, place, tall)
    recv = shift(send, "core", 1)
    pos, start, flags = plan(pair_domain, tile_order, tall, slots, keep.shape[1])
    u = compact(start, place, amplitudes, pos, slots)
    recv, u = together(recv, u)
    mine = jnp.concatenate([recv, keep, flags], axis=0)

    up, um = shift(u, "x", -1), shift(u, "x", 1)
    ap, am, there = shift(mine, "y", -1), shift(mine, "y", 1), shift(mine, "zl", 1)
    up, um, ap, am, there = together(up, um, ap, am, there)
    u2, q = shift(um, "x", 1), shift(u, "zh", 1)
    tp, tm = shift(there, "y", -1), shift(there, "y", 1)
    u2, q, tp, tm = together(u2, q, tp, tm)
    qp, qm, q2 = shift(q, "x", -1), shift(q, "x", 1), shift(u2, "zh", 1)
    a2, t2 = shift(am, "y", 1), shift(tp, "y", -1)

    same = (zh == zl).astype(I32)

    def blocks(picks, n_hops):
        ids, which, source = [], [], []
        for dz, hop in picks:
            across = (y + hop) % 4
            ids.append((((zh + dz) % 2) * 4 + across) * 2 + core)
            own = same if dz == 0 else 1 - same
            which.append(n_hops.index(hop) + (1 - own) * len(n_hops))
            source.append(dz * 4 + (across - x) % 4)
        return [jnp.stack(v).astype(I32) for v in (ids, which, source)]

    near, far = [u, up, u2, um], [q, qp, q2, qm]
    sums = product(start, *blocks([(0, 0), (0, 1), (0, 3)], [0, 1, 3]), [mine, ap, am, there, tp, tm], near, pos, tall)
    other, own, flags = product(
        start,
        *blocks([(0, 2), (1, 0), (1, 1), (1, 2), (1, 3)], [0, 1, 2, 3]),
        [mine, ap, a2, am, there, tp, t2, tm],
        near + far,
        pos,
        tall,
        sums,
    )
    theirs = shift(other, "core", 1)
    return lax.cond(
        jnp.max(flags) > 0.5,
        lambda *args: dense(*args[:5]),
        lambda *args: args[5] + args[6],
        integrals,
        amplitudes,
        tile_pattern,
        pair_domain,
        tile_order,
        own,
        theirs,
    )


def solution(mesh):
    fine = Mesh(np.asarray(mesh.devices).reshape(SIZES), AXES)
    return jax.shard_map(
        on_device,
        mesh=fine,
        in_specs=(P(ROW, COL), P(ROW, COL), P(), P(None, COL), P()),
        out_specs=P(ROW, COL),
        check_vma=False,
    )
```

time: 141 us -> 116 us (0.82)
  Pallas kernels: 53.5 us -> 36.8 us
  waiting for transfers between devices: 36.9 us -> 27.6 us
  starting transfers between devices: 19.6 us -> 26.1 us
  local copies, waits for them, and re-layouts: 6.59 us -> 3.74 us
  other arithmetic: 8.26 us -> 6.72 us
    pallas_call x5 -> x3, Pallas kernels: 45.5 us -> 29.4 us  [the longest x2 26.4 us: product(): pl.pallas_call(functools.partial(product_kernel, tall, n, len(a_parts), l...]
    ppermute x15 -> x16, waiting for transfers between devices: 36.9 us -> 27.6 us  [shift(): return lax.ppermute(value, axis, [(i, (i + by) % n) for i in range(n)])]
    ppermute x15 -> x16, starting transfers between devices: 19.6 us -> 26.1 us  [shift(): return lax.ppermute(value, axis, [(i, (i + by) % n) for i in range(n)])]
    unnamed x21 -> x24, local copies, waits for them, and re-layouts: 3.09 us -> 1.09 us
    slice x3 -> x0, local copies, waits for them, and re-layouts: 1.87 us -> none  [the longest x2 0.94 us: on_device(): pg3 = shift(jnp.concatenate([g, up[first:], um[first:]], axis=0), 'zh', 1)]
  transfers between devices with their start and end apart: 16 -> 16, of which waited for: 5 -> 4; matrix products, arithmetic and copies ran while one was open for 5% -> 5% of each run, Pallas kernels for 20% -> 16%
where the time goes in v2:
time: 116 us; the launch traced here: 115 us
  Pallas kernels  36.8 us (32%)
  waiting for transfers between devices  27.6 us (24%)
  starting transfers between devices  26.1 us (22%)
  between operations  14.2 us (12%)
  other arithmetic  6.72 us (6%)
  local copies, waits for them, and re-layouts  3.74 us (3%)
    ppermute x16, waiting for transfers between devices, shift(): return lax.ppermute(value, axis, [(i, (i + by) % n) for i in range(n)])  27.6 us
    pallas_call x2, Pallas kernels, product(): pl.pallas_call(functools.partial(product_kernel, tall, n, len(a_parts), l...  26.4 us
    ppermute x16, starting transfers between devices, shift(): return lax.ppermute(value, axis, [(i, (i + by) % n) for i in range(n)])  26.1 us
    pallas_call x1, Pallas kernels, compact(): pl.pallas_call(functools.partial(compact_kernel, slots), grid_spec=pltpu....  4.28 us
    add x1, other arithmetic, on_device(): args[5] + args[6]  3.59 us
    pallas_call x1, Pallas kernels, screen(): pl.pallas_call(functools.partial(screen_kernel, tall), grid_spec=pltpu.Pr...  3.07 us
    pallas_call x1, Pallas kernels, plan(): pl.pallas_call(functools.partial(plan_kernel, tall, slots), grid_spec=plt...  3.06 us
  transfers between devices with their start and end apart: 16, of which 4 were waited for; matrix products, arithmetic and copies ran while one was open for 5% of the time, Pallas kernels for 16%

profile of v2, /device:TPU:1, one launch (start us, length us, event | category | flops | bytes accessed | tf_op | source)
XLA Modules:
  0.0 115.1 jit_solution(9420394202481732368)
XLA Ops:
  6.5 0.6 pad_add_fusion.place
  7.2 3.1 %screen.1 = (bf16[384,384]{1,0:T(8,128)(2,1)}, bf16[384,384]{1,0:T(8,128)(2,1)}) custom-call(s32[48]{0:T(128)} %order.3, s32[48,48]{1,0:T(8,128)} %pattern.1, s32[3]{0:T(128)} %pad_add_fusion.place, bf16[384,768]{1,0:T(8,128)(2,1)} %a_ref.1), custom_call_target="tpu_custom_call" | custom-call | tf_op jit(solution)/shard_map/screen/pallas_call | solution.py:45
  10.2 1.4 %collective-permute-start = (bf16[384,384]{1,0:T(8,128)(2,1)}, bf16[384,384]{1,0:T(8,128)(2,1)S(1)}, u32[]{:S(2)}, u32[]{:S(2)}) collective-permute-start(bf16[384,384]{1,0:T(8,128)(2,1)} %get-tuple-element.52), channel_id=1, source_target_pairs={{0,8},{8,0},{1,9},{9,1},{2,10},{10,2},{3,11},{11,3},{4,12},{12,4},... | collective-permute-start | bytes 884744 | tf_op jit(solution)/shard_map/ppermute | solution.py:228
  11.6 3.1 %plan.1 = (s32[48,1536]{1,0:T(8,128)}, s32[48,128]{1,0:T(8,128)}, bf16[8,384]{1,0:T(8,128)(2,1)}) custom-call(s32[48]{0:T(128)} %order.3, s32[48,1536]{1,0:T(8,128)} %d_ref.1), custom_call_target="tpu_custom_call" | custom-call | tf_op jit(solution)/shard_map/plan/pallas_call | solution.py:80
  14.7 4.3 %compact.1.refs_6_.refs_8_ = bf16[128,2560]{1,0:T(8,128)(2,1)} custom-call(s32[48,128]{1,0:T(8,128)} %get-tuple-element.51.start, s32[3]{0:T(128)} %pad_add_fusion.place, bf16[384,1536]{1,0:T(8,128)(2,1)} %b_ref.1, s32[48,1536]{1,0:T(8,128)} %get-tuple-element.53.pos_ref.refs_10_.refs_16_), custom_call_target="tpu_custom_call" | custom-call | tf_op jit(solution)/shard_map/compact/pallas_call | solution.py:117
  19.0 0.0 collective-permute-done
  19.0 2.6 %collective-permute-start.1 = (bf16[128,2560]{1,0:T(8,128)(2,1)}, bf16[128,2560]{1,0:T(8,128)(2,1)S(1)}, u32[]{:S(2)}, u32[]{:S(2)}) collective-permute-start(bf16[128,2560]{1,0:T(8,128)(2,1)} %compact.1.refs_6_.refs_8_), channel_id=1, source_target_pairs={{0,48},{16,0},{32,16},{48,32},{1,49},{17,1},{33,17},{49,33},{2,50}... | collective-permute-start | bytes 1966088 | tf_op jit(solution)/shard_map/ppermute | solution.py:228
  21.5 0.0 collective-permute-start.2
  21.6 1.0 constant_dynamic-update-slice_fusion.1
  22.6 0.7 constant_dynamic-update-slice_fusion.refs_0_
  23.3 2.7 %collective-permute-start.3 = (bf16[776,384]{1,0:T(8,128)(2,1)S(1)}, bf16[776,384]{1,0:T(8,128)(2,1)S(1)}, u32[]{:S(2)}, u32[]{:S(2)}) collective-permute-start(bf16[776,384]{1,0:T(8,128)(2,1)S(1)} %constant_dynamic-update-slice_fusion.refs_0_), channel_id=1, source_target_pairs={{0,3},{1,0},{2,1},{3,2},{4,7},{5,4},{6,5},{7,6},{8,11},{9,8},{10,9... | collective-permute-start | bytes 1787912 | tf_op jit(solution)/shard_map/ppermute | solution.py:228
  26.0 0.0 collective-permute-start.4
  26.0 1.6 %collective-permute-start.5 = (bf16[776,384]{1,0:T(8,128)(2,1)S(1)}, bf16[776,384]{1,0:T(8,128)(2,1)S(1)}, u32[]{:S(2)}, u32[]{:S(2)}) collective-permute-start(bf16[776,384]{1,0:T(8,128)(2,1)S(1)} %constant_dynamic-update-slice_fusion.refs_0_), channel_id=1, source_target_pairs={{0,4},{4,0},{1,5},{5,1},{2,6},{6,2},{3,7},{7,3},{8,12},{12,8},{9,1... | collective-permute-start | bytes 1787912 | tf_op jit(solution)/shard_map/ppermute | solution.py:228
  27.7 10.9 %collective-permute-done.3.refs_1_ = bf16[776,384]{1,0:T(8,128)(2,1)S(1)} collective-permute-done((bf16[776,384]{1,0:T(8,128)(2,1)S(1)}, bf16[776,384]{1,0:T(8,128)(2,1)S(1)}, u32[]{:S(2)}, u32[]{:S(2)}) %collective-permute-start.3) | collective-permute-done | bytes 596000 | tf_op jit(solution)/shard_map/ppermute | solution.py:228
  38.6 3.6 %collective-permute-start.8 = (bf16[128,2560]{1,0:T(8,128)(2,1)}, bf16[128,2560]{1,0:T(8,128)(2,1)S(1)}, u32[]{:S(2)}, u32[]{:S(2)}) collective-permute-start(bf16[128,2560]{1,0:T(8,128)(2,1)} %compact.1.refs_6_.refs_8_), channel_id=1, source_target_pairs={{0,64},{64,0},{1,65},{65,1},{2,66},{66,2},{3,67},{67,3},{4,68},{68... | collective-permute-start | bytes 1966088 | tf_op jit(solution)/shard_map/ppermute | solution.py:228
  42.2 0.0 collective-permute-done.4.refs_2_.refs_3_
  42.2 0.0 collective-permute-done.5.refs_3_.refs_4_
  42.2 0.0 collective-permute-done.1.refs_7_.refs_9_
  42.2 0.0 copy-start.5
  42.2 0.0 collective-permute-done.2.refs_9_.refs_11_
  42.2 0.0 copy-start.6
  42.2 0.1 collective-permute-start.7
  42.3 3.5 %collective-permute-start.9 = (bf16[776,384]{1,0:T(8,128)(2,1)S(1)}, bf16[776,384]{1,0:T(8,128)(2,1)}, u32[]{:S(2)}, u32[]{:S(2)}) collective-permute-start(bf16[776,384]{1,0:T(8,128)(2,1)S(1)} %collective-permute-done.5.refs_3_.refs_4_), channel_id=1, source_target_pairs={{0,3},{1,0},{2,1},{3,2},{4,7},{5,4},{6,5},{7,6},{8,11},{9,8},{10,9... | collective-permute-start | bytes 1787912 | tf_op jit(solution)/shard_map/ppermute | solution.py:228
  45.8 0.0 collective-permute-start.10
  45.8 12.2 %collective-permute-done.8.refs_12_ = bf16[128,2560]{1,0:T(8,128)(2,1)S(1)} collective-permute-done((bf16[128,2560]{1,0:T(8,128)(2,1)}, bf16[128,2560]{1,0:T(8,128)(2,1)S(1)}, u32[]{:S(2)}, u32[]{:S(2)}) %collective-permute-start.8) | collective-permute-done | bytes 655392 | tf_op jit(solution)/shard_map/ppermute | solution.py:228
  58.0 0.0 collective-permute-done.9.refs_4_.refs_5_
  58.0 1.9 %collective-permute-done.10.refs_5_.refs_7_ = bf16[776,384]{1,0:T(8,128)(2,1)S(1)} collective-permute-done((bf16[776,384]{1,0:T(8,128)(2,1)S(1)}, bf16[776,384]{1,0:T(8,128)(2,1)S(1)}, u32[]{:S(2)}, u32[]{:S(2)}) %collective-permute-start.10) | collective-permute-done | bytes 596000 | tf_op jit(solution)/shard_map/ppermute | solution.py:228
  59.9 0.0 collective-permute-done.7.refs_8_.refs_10_
  59.9 2.8 %collective-permute-start.12 = (bf16[128,2560]{1,0:T(8,128)(2,1)S(1)}, bf16[128,2560]{1,0:T(8,128)(2,1)}, u32[]{:S(2)}, u32[]{:S(2)}) collective-permute-start(bf16[128,2560]{1,0:T(8,128)(2,1)S(1)} %collective-permute-done.8.refs_12_), channel_id=1, source_target_pairs={{0,48},{16,0},{32,16},{48,32},{1,49},{17,1},{33,17},{49,33},{2,50}... | collective-permute-start | bytes 1966088 | tf_op jit(solution)/shard_map/ppermute | solution.py:228
  62.7 0.0 copy-done.9
  62.7 0.4 collective-permute-start.13
  63.1 0.0 copy-done.10
  63.1 0.0 collective-permute-start.14
  63.1 0.0 copy-done.11
  63.1 0.1 collective-permute-start.6
  63.2 2.7 %collective-permute-start.11 = (bf16[776,384]{1,0:T(8,128)(2,1)}, bf16[776,384]{1,0:T(8,128)(2,1)}, u32[]{:S(2)}, u32[]{:S(2)}) collective-permute-start(bf16[776,384]{1,0:T(8,128)(2,1)} %collective-permute-done.9.refs_4_.refs_5_), channel_id=1, source_target_pairs={{0,3},{1,0},{2,1},{3,2},{4,7},{5,4},{6,5},{7,6},{8,11},{9,8},{10,9... | collective-permute-start | bytes 1787912 | tf_op jit(solution)/shard_map/ppermute | solution.py:228
  65.9 0.7 stack.107.ids
  66.5 0.7 stack.113.which
  67.2 0.6 stack.119.source
  67.8 0.6 pad_add_fusion.3.source
  68.5 0.6 pad_add_fusion.1
  69.1 0.0 copy-done.1
  69.1 0.0 copy-done.5
  69.1 0.0 copy-done.6
  69.1 0.0 copy-done.8
  69.1 11.0 %product.2 = (f32[384,1536]{1,0:T(8,128)}, f32[384,1536]{1,0:T(8,128)}, f32[8,128]{1,0:T(8,128)}) custom-call(s32[48,128]{1,0:T(8,128)} %get-tuple-element.51.start, s32[3]{0:T(128)} %get-tuple-element.74.ids, s32[3]{0:T(128)} %get-tuple-element.75.which, s32[3]{0:T(128)} %pad_add_fusion.3.source, bf16[776,384]{1,0:T(8,128)(2,1)} %copy-done.1, ...), custom_call_target="tpu_custom_call" | custom-call | flops 2717908992 | bytes 10045440 | tf_op jit(solution)/shard_map/product/pallas_call | solution.py:202
  80.1 0.0 copy-done.7
  80.1 0.0 collective-permute-done.6.refs_2_
  80.1 0.0 collective-permute-done.11.refs_6_
  80.1 0.0 collective-permute-done.12.refs_13_
  80.2 0.0 collective-permute-done.13.refs_14_
  80.2 0.0 collective-permute-done.14.refs_15_
  80.2 0.0 copy-start
  80.2 0.0 copy-start.2
  80.2 0.0 copy-start.3
  80.2 15.3 %product.3 = (f32[384,1536]{1,0:T(8,128)}, f32[384,1536]{1,0:T(8,128)S(1)}, f32[8,128]{1,0:T(8,128)}) custom-call(s32[48,128]{1,0:T(8,128)} %get-tuple-element.51.start, s32[5]{0:T(128)} %stack.107.ids, s32[5]{0:T(128)} %stack.113.which, s32[5]{0:T(128)} %stack.119.source, bf16[776,384]{1,0:T(8,128)(2,1)} %copy-done.1, bf16[776,384]{1,0:T(8,128)(2,1)} %copy-done.9, ...), custom_call_target="tpu_custom_call" | custom-call | flops 4529848320 | bytes 13596672 | tf_op jit(solution)/shard_map/product/pallas_call | solution.py:202
  95.6 4.6 %collective-permute-start.15 = (f32[384,1536]{1,0:T(8,128)}, f32[384,1536]{1,0:T(8,128)}, u32[]{:S(2)}, u32[]{:S(2)}) collective-permute-start(f32[384,1536]{1,0:T(8,128)} %get-tuple-element.72), channel_id=1, source_target_pairs={{0,8},{8,0},{1,9},{9,1},{2,10},{10,2},{3,11},{11,3},{4,12},{12,4},... | collective-permute-start | bytes 7077896 | tf_op jit(solution)/shard_map/ppermute | solution.py:228
  100.2 1.3 %reduce_max.9 = f32[]{:T(128)} reduce(f32[8,128]{1,0:T(8,128)} %get-tuple-element.70, f32[]{:T(128)} %constant.133.clone.1), dimensions={0,1}, to_apply=%region_0.1 | reduce | flops 1023 | bytes 4104 | tf_op jit(solution)/shard_map/reduce_max | solution.py:297
  102.1 2.6 %collective-permute-done.15 = f32[384,1536]{1,0:T(8,128)} collective-permute-done((f32[384,1536]{1,0:T(8,128)}, f32[384,1536]{1,0:T(8,128)}, u32[]{:S(2)}, u32[]{:S(2)}) %collective-permute-start.15) | collective-permute-done | bytes 2359328 | tf_op jit(solution)/shard_map/ppermute | solution.py:228
  104.7 0.0 copy-done
  104.7 0.0 copy-done.2
  104.7 0.0 copy-done.3
  104.7 3.6 %conditional.1 = (f32[384,1536]{1,0:T(8,128)}) conditional(s32[]{:T(128)} %convert_element_type.32, (f32[384,1536]{1,0:T(8,128)S(1)}, f32[384,1536]{1,0:T(8,128)}) %tuple.17, (bf16[384,768]{1,0:T(8,128)(2,1)}, s32[48]{0:T(128)S(1)}, s32[48,48]{1,0:T(8,128)S(1)}, bf16[384,1536]{1,0:T(8,128)(2,1)}, s32[48,1536]{1,0:T(8,128)S(1)}) %tuple.30), branch_computations={%region_1.2_spmd, %region_2.3_spmd} | conditional | flops 7304832000 | bytes 168797408 | solution.py:296
  104.7 3.6 %add.115 = f32[384,1536]{1,0:T(8,128)} add(f32[384,1536]{1,0:T(8,128)S(1)} %get-tuple-element.22, f32[384,1536]{1,0:T(8,128)} %get-tuple-element.23) | non-fusion elementwise | flops 589824 | bytes 7077888 | tf_op jit(solution)/shard_map/cond/branch_0_fun/add | solution.py:299
  (7 shorter events, 0.0 us)
Async XLA Ops:
  10.2 8.8 %collective-permute-start = (bf16[384,384]{1,0:T(8,128)(2,1)}, bf16[384,384]{1,0:T(8,128)(2,1)S(1)}, u32[]{:S(2)}, u32[]{:S(2)}) collective-permute-start(bf16[384,384]{1,0:T(8,128)(2,1)} %get-tuple-element.52), channel_id=1, source_target_pairs={{0,8},{8,0},{1,9},{9,1},{2,10},{10,2},{3,11},{11,3},{4,12},{12,4},... | collective-permute-start | bytes 884744 | tf_op jit(solution)/shard_map/ppermute | solution.py:228
  19.0 23.2 %collective-permute-start.1 = (bf16[128,2560]{1,0:T(8,128)(2,1)}, bf16[128,2560]{1,0:T(8,128)(2,1)S(1)}, u32[]{:S(2)}, u32[]{:S(2)}) collective-permute-start(bf16[128,2560]{1,0:T(8,128)(2,1)} %compact.1.refs_6_.refs_8_), channel_id=1, source_target_pairs={{0,48},{16,0},{32,16},{48,32},{1,49},{17,1},{33,17},{49,33},{2,50}... | collective-permute-start | bytes 1966088 | tf_op jit(solution)/shard_map/ppermute | solution.py:228
  21.5 20.7 %collective-permute-start.2 = (bf16[128,2560]{1,0:T(8,128)(2,1)}, bf16[128,2560]{1,0:T(8,128)(2,1)S(1)}, u32[]{:S(2)}, u32[]{:S(2)}) collective-permute-start(bf16[128,2560]{1,0:T(8,128)(2,1)} %compact.1.refs_6_.refs_8_), channel_id=1, source_target_pairs={{0,16},{16,32},{32,48},{48,0},{1,17},{17,33},{33,49},{49,1},{2,18}... | collective-permute-start | bytes 1966088 | tf_op jit(solution)/shard_map/ppermute | solution.py:228
  23.3 45.8 %copy-start.1 = (bf16[776,384]{1,0:T(8,128)(2,1)}, bf16[776,384]{1,0:T(8,128)(2,1)S(1)}, u32[]{:S(2)}) copy-start(bf16[776,384]{1,0:T(8,128)(2,1)S(1)} %constant_dynamic-update-slice_fusion.refs_0_) | copy-start | bytes 1787908
  23.3 15.3 %collective-permute-start.3 = (bf16[776,384]{1,0:T(8,128)(2,1)S(1)}, bf16[776,384]{1,0:T(8,128)(2,1)S(1)}, u32[]{:S(2)}, u32[]{:S(2)}) collective-permute-start(bf16[776,384]{1,0:T(8,128)(2,1)S(1)} %constant_dynamic-update-slice_fusion.refs_0_), channel_id=1, source_target_pairs={{0,3},{1,0},{2,1},{3,2},{4,7},{5,4},{6,5},{7,6},{8,11},{9,8},{10,9... | collective-permute-start | bytes 1787912 | tf_op jit(solution)/shard_map/ppermute | solution.py:228
  26.0 16.2 %collective-permute-start.4 = (bf16[776,384]{1,0:T(8,128)(2,1)S(1)}, bf16[776,384]{1,0:T(8,128)(2,1)}, u32[]{:S(2)}, u32[]{:S(2)}) collective-permute-start(bf16[776,384]{1,0:T(8,128)(2,1)S(1)} %constant_dynamic-update-slice_fusion.refs_0_), channel_id=1, source_target_pairs={{0,1},{1,2},{2,3},{3,0},{4,5},{5,6},{6,7},{7,4},{8,9},{9,10},{10,1... | collective-permute-start | bytes 1787912 | tf_op jit(solution)/shard_map/ppermute | solution.py:228
  26.0 16.2 %collective-permute-start.5 = (bf16[776,384]{1,0:T(8,128)(2,1)S(1)}, bf16[776,384]{1,0:T(8,128)(2,1)S(1)}, u32[]{:S(2)}, u32[]{:S(2)}) collective-permute-start(bf16[776,384]{1,0:T(8,128)(2,1)S(1)} %constant_dynamic-update-slice_fusion.refs_0_), channel_id=1, source_target_pairs={{0,4},{4,0},{1,5},{5,1},{2,6},{6,2},{3,7},{7,3},{8,12},{12,8},{9,1... | collective-permute-start | bytes 1787912 | tf_op jit(solution)/shard_map/ppermute | solution.py:228
  38.6 24.1 %copy-start.9 = (bf16[776,384]{1,0:T(8,128)(2,1)}, bf16[776,384]{1,0:T(8,128)(2,1)S(1)}, u32[]{:S(2)}) copy-start(bf16[776,384]{1,0:T(8,128)(2,1)S(1)} %collective-permute-done.3.refs_1_) | copy-start | bytes 1787908
  38.6 19.4 %collective-permute-start.8 = (bf16[128,2560]{1,0:T(8,128)(2,1)}, bf16[128,2560]{1,0:T(8,128)(2,1)S(1)}, u32[]{:S(2)}, u32[]{:S(2)}) collective-permute-start(bf16[128,2560]{1,0:T(8,128)(2,1)} %compact.1.refs_6_.refs_8_), channel_id=1, source_target_pairs={{0,64},{64,0},{1,65},{65,1},{2,66},{66,2},{3,67},{67,3},{4,68},{68... | collective-permute-start | bytes 1966088 | tf_op jit(solution)/shard_map/ppermute | solution.py:228
  42.2 20.9 %copy-start.10 = (bf16[776,384]{1,0:T(8,128)(2,1)}, bf16[776,384]{1,0:T(8,128)(2,1)S(1)}, u32[]{:S(2)}) copy-start(bf16[776,384]{1,0:T(8,128)(2,1)S(1)} %collective-permute-done.5.refs_3_.refs_4_) | copy-start | bytes 1787908
  42.2 26.9 %copy-start.5 = (bf16[128,2560]{1,0:T(8,128)(2,1)}, bf16[128,2560]{1,0:T(8,128)(2,1)S(1)}, u32[]{:S(2)}) copy-start(bf16[128,2560]{1,0:T(8,128)(2,1)S(1)} %collective-permute-done.1.refs_7_.refs_9_) | copy-start | bytes 1966084
  42.2 26.8 %copy-start.6 = (bf16[128,2560]{1,0:T(8,128)(2,1)}, bf16[128,2560]{1,0:T(8,128)(2,1)S(1)}, u32[]{:S(2)}) copy-start(bf16[128,2560]{1,0:T(8,128)(2,1)S(1)} %collective-permute-done.2.refs_9_.refs_11_) | copy-start | bytes 1966084
  42.2 17.6 %collective-permute-start.7 = (bf16[128,2560]{1,0:T(8,128)(2,1)S(1)}, bf16[128,2560]{1,0:T(8,128)(2,1)S(1)}, u32[]{:S(2)}, u32[]{:S(2)}) collective-permute-start(bf16[128,2560]{1,0:T(8,128)(2,1)S(1)} %collective-permute-done.2.refs_9_.refs_11_), channel_id=1, source_target_pairs={{0,16},{16,32},{32,48},{48,0},{1,17},{17,33},{33,49},{49,1},{2,18}... | collective-permute-start | bytes 1966088 | tf_op jit(solution)/shard_map/ppermute | solution.py:228
  42.3 15.7 %collective-permute-start.9 = (bf16[776,384]{1,0:T(8,128)(2,1)S(1)}, bf16[776,384]{1,0:T(8,128)(2,1)}, u32[]{:S(2)}, u32[]{:S(2)}) collective-permute-start(bf16[776,384]{1,0:T(8,128)(2,1)S(1)} %collective-permute-done.5.refs_3_.refs_4_), channel_id=1, source_target_pairs={{0,3},{1,0},{2,1},{3,2},{4,7},{5,4},{6,5},{7,6},{8,11},{9,8},{10,9... | collective-permute-start | bytes 1787912 | tf_op jit(solution)/shard_map/ppermute | solution.py:228
  45.8 14.1 %collective-permute-start.10 = (bf16[776,384]{1,0:T(8,128)(2,1)S(1)}, bf16[776,384]{1,0:T(8,128)(2,1)S(1)}, u32[]{:S(2)}, u32[]{:S(2)}) collective-permute-start(bf16[776,384]{1,0:T(8,128)(2,1)S(1)} %collective-permute-done.5.refs_3_.refs_4_), channel_id=1, source_target_pairs={{0,1},{1,2},{2,3},{3,0},{4,5},{5,6},{6,7},{7,4},{8,9},{9,10},{10,1... | collective-permute-start | bytes 1787912 | tf_op jit(solution)/shard_map/ppermute | solution.py:228
  58.0 22.1 %copy-start.7 = (bf16[128,2560]{1,0:T(8,128)(2,1)}, bf16[128,2560]{1,0:T(8,128)(2,1)S(1)}, u32[]{:S(2)}) copy-start(bf16[128,2560]{1,0:T(8,128)(2,1)S(1)} %collective-permute-done.8.refs_12_) | copy-start | bytes 1966084
  59.9 3.2 %copy-start.11 = (bf16[776,384]{1,0:T(8,128)(2,1)}, bf16[776,384]{1,0:T(8,128)(2,1)S(1)}, u32[]{:S(2)}) copy-start(bf16[776,384]{1,0:T(8,128)(2,1)S(1)} %collective-permute-done.10.refs_5_.refs_7_) | copy-start | bytes 1787908
  59.9 9.2 %copy-start.8 = (bf16[128,2560]{1,0:T(8,128)(2,1)}, bf16[128,2560]{1,0:T(8,128)(2,1)S(1)}, u32[]{:S(2)}) copy-start(bf16[128,2560]{1,0:T(8,128)(2,1)S(1)} %collective-permute-done.7.refs_8_.refs_10_) | copy-start | bytes 1966084
  59.9 20.3 %collective-permute-start.12 = (bf16[128,2560]{1,0:T(8,128)(2,1)S(1)}, bf16[128,2560]{1,0:T(8,128)(2,1)}, u32[]{:S(2)}, u32[]{:S(2)}) collective-permute-start(bf16[128,2560]{1,0:T(8,128)(2,1)S(1)} %collective-permute-done.8.refs_12_), channel_id=1, source_target_pairs={{0,48},{16,0},{32,16},{48,32},{1,49},{17,1},{33,17},{49,33},{2,50}... | collective-permute-start | bytes 1966088 | tf_op jit(solution)/shard_map/ppermute | solution.py:228
  62.7 17.5 %collective-permute-start.13 = (bf16[128,2560]{1,0:T(8,128)(2,1)S(1)}, bf16[128,2560]{1,0:T(8,128)(2,1)}, u32[]{:S(2)}, u32[]{:S(2)}) collective-permute-start(bf16[128,2560]{1,0:T(8,128)(2,1)S(1)} %collective-permute-done.7.refs_8_.refs_10_), channel_id=1, source_target_pairs={{0,64},{64,0},{1,65},{65,1},{2,66},{66,2},{3,67},{67,3},{4,68},{68... | collective-permute-start | bytes 1966088 | tf_op jit(solution)/shard_map/ppermute | solution.py:228
  63.1 17.0 %collective-permute-start.14 = (bf16[128,2560]{1,0:T(8,128)(2,1)S(1)}, bf16[128,2560]{1,0:T(8,128)(2,1)}, u32[]{:S(2)}, u32[]{:S(2)}) collective-permute-start(bf16[128,2560]{1,0:T(8,128)(2,1)S(1)} %collective-permute-done.8.refs_12_), channel_id=1, source_target_pairs={{0,16},{16,32},{32,48},{48,0},{1,17},{17,33},{33,49},{49,1},{2,18}... | collective-permute-start | bytes 1966088 | tf_op jit(solution)/shard_map/ppermute | solution.py:228
  63.1 17.0 %collective-permute-start.6 = (bf16[776,384]{1,0:T(8,128)(2,1)}, bf16[776,384]{1,0:T(8,128)(2,1)}, u32[]{:S(2)}, u32[]{:S(2)}) collective-permute-start(bf16[776,384]{1,0:T(8,128)(2,1)} %collective-permute-done.4.refs_2_.refs_3_), channel_id=1, source_target_pairs={{0,1},{1,2},{2,3},{3,0},{4,5},{5,6},{6,7},{7,4},{8,9},{9,10},{10,1... | collective-permute-start | bytes 1787912 | tf_op jit(solution)/shard_map/ppermute | solution.py:228
  63.2 16.9 %collective-permute-start.11 = (bf16[776,384]{1,0:T(8,128)(2,1)}, bf16[776,384]{1,0:T(8,128)(2,1)}, u32[]{:S(2)}, u32[]{:S(2)}) collective-permute-start(bf16[776,384]{1,0:T(8,128)(2,1)} %collective-permute-done.9.refs_4_.refs_5_), channel_id=1, source_target_pairs={{0,3},{1,0},{2,1},{3,2},{4,7},{5,4},{6,5},{7,6},{8,11},{9,8},{10,9... | collective-permute-start | bytes 1787912 | tf_op jit(solution)/shard_map/ppermute | solution.py:228
  80.2 24.5 %copy-start = (s32[48,1536]{1,0:T(8,128)S(1)}, s32[48,1536]{1,0:T(8,128)}, u32[]{:S(2)}) copy-start(s32[48,1536]{1,0:T(8,128)} %d_ref.1) | copy-start | bytes 884740
  80.2 24.5 %copy-start.2 = (s32[48,48]{1,0:T(8,128)S(1)}, s32[48,48]{1,0:T(8,128)}, u32[]{:S(2)}) copy-start(s32[48,48]{1,0:T(8,128)} %pattern.1) | copy-start | bytes 27652
  80.2 24.5 %copy-start.3 = (s32[48]{0:T(128)S(1)}, s32[48]{0:T(128)}, u32[]{:S(2)}) copy-start(s32[48]{0:T(128)} %order.3) | copy-start | bytes 580
  95.6 9.1 %collective-permute-start.15 = (f32[384,1536]{1,0:T(8,128)}, f32[384,1536]{1,0:T(8,128)}, u32[]{:S(2)}, u32[]{:S(2)}) collective-permute-start(f32[384,1536]{1,0:T(8,128)} %get-tuple-element.72), channel_id=1, source_target_pairs={{0,8},{8,0},{1,9},{9,1},{2,10},{10,2},{3,11},{11,3},{4,12},{12,4},... | collective-permute-start | bytes 7077896 | tf_op jit(solution)/shard_map/ppermute | solution.py:228

commit v3 on v2

v3 whole, which is shorter than its diff:
```python
import functools

import jax
import jax.numpy as jnp
import numpy as np
from jax import lax
from jax.experimental import pallas as pl
from jax.experimental.pallas import tpu as pltpu
from jax.sharding import Mesh, PartitionSpec as P

TILE = 128
AXES = ("zh", "x", "core", "zl", "y")
SIZES = (2, 4, 2, 2, 4)
ROW, COL = ("zh", "x", "core"), ("zl", "y")
BF16, F32, I32 = jnp.bfloat16, jnp.float32, jnp.int32
FLAG_ROWS = 8
VMEM_LIMIT = 60 << 20


def where_am_i():
    row = (lax.axis_index("zh") * 4 + lax.axis_index("x")) * 2 + lax.axis_index("core")
    return row, lax.axis_index("zl") * 4 + lax.axis_index("y"), lax.axis_index("core")


def iota(shape, dim):
    return lax.broadcasted_iota(I32, shape, dim)


def whole(n, space=pltpu.VMEM):
    return [pl.BlockSpec(memory_space=space)] * n


def join_kernel(tall, order, pattern, over_ref, a_ref, recv_ref, join_ref):
    row, col, core = where_am_i()
    rows, cols = a_ref.shape
    half = cols // TILE // 2
    for which, ref in ((1, recv_ref), (0, a_ref)):
        block = jnp.bitwise_xor(row, which)
        for i in range(rows // TILE):
            high = pl.ds(i * TILE, TILE)
            for j in range(half):
                tile = core * half + j
                on = pattern[order[block * tall + i], order[col * 2 * half + tile]]
                scale = on.astype(F32).astype(BF16)
                part = ref[high, pl.ds(pl.multiple_of(tile * TILE, TILE), TILE)]
                join_ref[pl.ds((1 - which) * rows + i * TILE, TILE), pl.ds(j * TILE, TILE)] = part * scale
    join_ref[pl.ds(2 * rows, FLAG_ROWS), :] = over_ref[...]


def join(integrals, recv, over, tile_pattern, tile_order, tall):
    rows, cols = integrals.shape
    return pl.pallas_call(
        functools.partial(join_kernel, tall),
        grid_spec=pltpu.PrefetchScalarGridSpec(
            num_scalar_prefetch=2, grid=(), in_specs=whole(3), out_specs=pl.BlockSpec(memory_space=pltpu.VMEM)
        ),
        out_shape=jax.ShapeDtypeStruct((2 * rows + FLAG_ROWS, cols // 2), BF16),
        name="join",
    )(tile_order, tile_pattern, over, integrals, recv)


def pack_kernel(
    tall, slots, order, d_ref, b_ref, pos_ref, start_ref, u_ref, over_ref, dom, total, start, sem
):
    tiles, pairs = dom.shape
    for s in range(tiles):
        dom[pl.ds(s, 1), :] = d_ref[pl.ds(order[s], 1), :]
    live = dom[...].astype(F32).astype(BF16)
    blocks = pairs // TILE
    spread = (iota((pairs, TILE), 0) // TILE == iota((pairs, TILE), 1)).astype(F32).astype(BF16)
    counts = jnp.dot(live, spread, preferred_element_type=F32)
    below = (iota((TILE, TILE), 0) < iota((TILE, TILE), 1)).astype(F32).astype(BF16)
    upto = (iota((TILE, TILE), 0) <= iota((TILE, TILE), 1)).astype(F32).astype(BF16)
    s0, s1 = iota((tiles, tiles), 0), iota((tiles, tiles), 1)
    before = ((s0 // tall == s1 // tall) & (s1 < s0)).astype(F32).astype(BF16)
    counted = counts.astype(BF16)
    ahead = jnp.sum(jnp.dot(before, counted, preferred_element_type=F32), axis=1, keepdims=True)
    starts = jnp.dot(counted, below, preferred_element_type=F32) + ahead
    start_ref[...] = starts.astype(I32)
    copy = pltpu.make_async_copy(start_ref, start, sem)
    copy.start()
    for b in range(blocks):
        lanes = pl.ds(b * TILE, TILE)
        here = live[:, b * TILE : (b + 1) * TILE]
        slot = jnp.dot(here, upto, preferred_element_type=F32) + (starts[:, b : b + 1] - 1.0)
        pos_ref[:, lanes] = jnp.where(dom[:, lanes] > 0, slot.astype(I32), -1)
    most = jnp.max(ahead + jnp.sum(counts, axis=1, keepdims=True), axis=0, keepdims=True)
    flag = jnp.where(most > slots, 1.0, 0.0).astype(F32)
    over_ref[...] = jnp.broadcast_to(flag, over_ref.shape).astype(BF16)
    total[...] = jnp.zeros_like(total)
    copy.wait()
    for i in range(tall):
        s = where_am_i()[0] * tall + i
        slot = pos_ref[pl.ds(s, 1), :]
        for b in range(blocks):
            lanes = pl.ds(b * TILE, TILE)
            at = jnp.minimum(start[s, b] // TILE * TILE, slots)
            at = pl.multiple_of(at, TILE)
            pick = (iota((2 * TILE, TILE), 0) + at == slot[:, b * TILE : (b + 1) * TILE]).astype(F32).astype(BF16)
            moved = lax.dot_general(
                b_ref[pl.ds(i * TILE, TILE), lanes], pick, (((1,), (1,)), ((), ())), preferred_element_type=F32
            )
            total[:, pl.ds(at, 2 * TILE)] += moved
    u_ref[...] = total[:, :slots].astype(BF16)


def pack(pair_domain, amplitudes, tile_order, tall, slots, cols):
    tiles, pairs = pair_domain.shape
    return pl.pallas_call(
        functools.partial(pack_kernel, tall, slots),
        grid_spec=pltpu.PrefetchScalarGridSpec(
            num_scalar_prefetch=1,
            grid=(),
            in_specs=whole(2),
            out_specs=whole(4),
            scratch_shapes=[
                pltpu.VMEM((tiles, pairs), I32),
                pltpu.VMEM((TILE, slots + 2 * TILE), F32),
                pltpu.SMEM((tiles, TILE), I32),
                pltpu.SemaphoreType.DMA(()),
            ],
        ),
        out_shape=[
            jax.ShapeDtypeStruct((tiles, pairs), I32),
            jax.ShapeDtypeStruct((tiles, TILE), I32),
            jax.ShapeDtypeStruct((TILE, slots), BF16),
            jax.ShapeDtypeStruct((FLAG_ROWS, cols), BF16),
        ],
        name="pack",
    )(tile_order, pair_domain, amplitudes)


def product_kernel(tall, picks, hops, first, wide, start_ref, *refs):
    n, nh = len(picks), len(hops)
    a_refs, refs = refs[: 2 * nh], refs[2 * nh :]
    in_refs, pos_ref, refs = refs[:8], refs[8], refs[9:]
    if not first:
        sums, flags_ref, refs = refs[:2], refs[2], refs[3:]
    outs, flag_out, (a_all, held, b_all, held_sums, start, a_sem, sem, in_sem, out_sem, start_sem) = refs[:2], refs[2], refs[3:]
    rows, pairs = outs[0].shape
    slots = in_refs[0].shape[1]
    depth = tall * TILE
    zh, x, core, zl, y = (lax.axis_index(axis) for axis in AXES)
    starts = pltpu.make_async_copy(start_ref, start, start_sem)
    starts.start()

    def a_slot(k):
        return a_all.at[:, pl.ds(k * depth, depth)]

    def b_slot(k):
        return held.at[k, :, pl.ds(0, slots)]

    ids = []
    for k, (dz, hop) in enumerate(picks):
        across, far = (y + hop) % 4, zh if dz == 0 else 1 - zh
        ids.append((far * 4 + across) * 2 + core)
        for dx in range(4):

            @pl.when((across - x + 4) % 4 == dx)
            def _(k=k, option=in_refs[4 * dz + dx]):
                pltpu.make_async_copy(option, b_slot(k), sem.at[k]).start()

        for own in range(2):

            @pl.when((far == zl) == (own == 0))
            def _(k=k, option=a_refs[own * nh + hops.index(hop)]):
                pltpu.make_async_copy(option, a_slot(k), a_sem.at[k]).start()

    strips = pairs // wide

    def strip(b):
        return pl.ds(b * wide, wide)

    if not first:
        loads = [
            [pltpu.make_async_copy(sums[h].at[:, strip(b)], held_sums.at[h, :, strip(b)], in_sem.at[h, b]) for h in range(2)]
            for b in range(strips)
        ]
        for pair in loads:
            for load in pair:
                load.start()
    for k in range(n):
        held[k, :, pl.ds(slots, TILE)] = jnp.zeros((TILE, TILE), BF16)

    lines = iota((2 * TILE, TILE), 0).astype(F32).astype(BF16)
    stores = []
    starts.wait()
    for b in range(strips):
        for k in range(n):
            if b == 0:
                pltpu.make_async_copy(in_refs[0], b_slot(k), sem.at[k]).wait()
            for i in range(tall):
                s = ids[k] * tall + i
                slot = pos_ref[pl.ds(s, 1), :]
                for c in range(wide // TILE):
                    block = b * (wide // TILE) + c
                    at = jnp.minimum(start[s, block] // TILE * TILE, slots - TILE)
                    at = pl.multiple_of(at, TILE)
                    here = slot[:, block * TILE : (block + 1) * TILE] - at
                    here = jnp.where((here < 0) | (here >= 2 * TILE), -1, here).astype(F32).astype(BF16)
                    pick = jnp.where(lines == here, jnp.ones((), BF16), jnp.zeros((), BF16))
                    spread = jnp.dot(held[k, :, pl.ds(at, 2 * TILE)], pick, preferred_element_type=F32)
                    b_all[pl.ds((k * tall + i) * TILE, TILE), pl.ds(c * TILE, TILE)] = spread.astype(BF16)
        if b == 0:
            for k in range(n):
                pltpu.make_async_copy(a_refs[0], a_slot(k), a_sem.at[k]).wait()
        for h in range(2):
            total = jnp.dot(a_all[pl.ds(h * rows, rows), :], b_all[...], preferred_element_type=F32)
            if not first:
                loads[b][h].wait()
                total += held_sums[h, :, strip(b)]
            held_sums[h, :, strip(b)] = total
            store = pltpu.make_async_copy(held_sums.at[h, :, strip(b)], outs[h].at[:, strip(b)], out_sem.at[h, b])
            store.start()
            stores.append(store)
    flags = [a_all[pl.ds(2 * rows, FLAG_ROWS), pl.ds(k * depth, TILE)].astype(F32) for k in range(n)]
    if not first:
        flags.append(flags_ref[...])
    flag_out[...] = functools.reduce(jnp.maximum, flags)
    for store in stores:
        store.wait()


def product(start, picks, hops, a_parts, arrays, pos, tall, sums=None, wide=1536):
    n, (tiles, pairs) = len(picks), pos.shape
    slots = arrays[0].shape[1]
    depth = tall * TILE
    high = a_parts[0].shape[0]
    rows = (high - FLAG_ROWS) // 2
    first = sums is None
    strips = pairs // wide
    hbm = pl.BlockSpec(memory_space=pltpu.HBM)
    vmem = pl.BlockSpec(memory_space=pltpu.VMEM)
    return pl.pallas_call(
        functools.partial(product_kernel, tall, picks, hops, first, wide),
        grid_spec=pltpu.PrefetchScalarGridSpec(
            num_scalar_prefetch=0,
            grid=(),
            in_specs=[hbm] * (len(a_parts) + 9) + [vmem] + ([] if first else [hbm, hbm, vmem]),
            out_specs=[hbm, hbm, vmem],
            scratch_shapes=[
                pltpu.VMEM((high, n * depth), BF16),
                pltpu.VMEM((n, TILE, slots + TILE), BF16),
                pltpu.VMEM((n * depth, wide), BF16),
                pltpu.VMEM((2, rows, pairs), F32),
                pltpu.SMEM((tiles, TILE), I32),
                pltpu.SemaphoreType.DMA((n,)),
                pltpu.SemaphoreType.DMA((n,)),
                pltpu.SemaphoreType.DMA((2, strips)),
                pltpu.SemaphoreType.DMA((2, strips)),
                pltpu.SemaphoreType.DMA(()),
            ],
        ),
        out_shape=[jax.ShapeDtypeStruct((rows, pairs), F32)] * 2 + [jax.ShapeDtypeStruct((FLAG_ROWS, TILE), F32)],
        compiler_params=pltpu.CompilerParams(vmem_limit_bytes=VMEM_LIMIT),
        cost_estimate=pl.CostEstimate(
            flops=4 * rows * n * depth * pairs, bytes_accessed=2 * n * depth * (high + pairs) + 8 * rows * pairs, transcendentals=0
        ),
        name="product",
    )(start, *a_parts, *arrays, pos, *(() if first else sums))


def shift(value, axis, by):
    n = lax.axis_size(axis)
    return lax.ppermute(value, axis, [(i, (i + by) % n) for i in range(n)])


def together(*values):
    return lax.optimization_barrier(values)


def dense(integrals, amplitudes, tile_pattern, pair_domain, tile_order):
    count = tile_order.shape[0]
    placed = (tile_order[:, None] == jnp.arange(count, dtype=I32)[None, :]).astype(F32)
    exact = functools.partial(jnp.dot, precision=lax.Precision.HIGHEST)
    pattern = exact(exact(placed, tile_pattern.astype(F32)), placed.T)
    domain = exact(placed, pair_domain.astype(F32))
    here = count // (lax.axis_size(ROW))
    pattern = lax.dynamic_slice_in_dim(pattern, lax.axis_index(ROW) * here, here, 0)
    mask = jnp.repeat(jnp.repeat(pattern, TILE, axis=0), TILE, axis=1).astype(BF16)
    screened = lax.all_gather(integrals, COL, axis=1, tiled=True) * mask
    domain = jnp.repeat(domain, TILE, axis=0).astype(BF16)
    restricted = lax.all_gather(amplitudes, ROW, axis=0, tiled=True) * domain
    return jnp.dot(screened, restricted, preferred_element_type=F32)


def on_device(integrals, amplitudes, tile_pattern, pair_domain, tile_order):
    tall = amplitudes.shape[0] // TILE
    slots = amplitudes.shape[1] * tall * 5 // 9 // TILE * TILE
    recv = shift(integrals, "core", 1)
    pos, start, u, over = pack(pair_domain, amplitudes, tile_order, tall, slots, integrals.shape[1] // 2)
    mine = join(integrals, recv, over, tile_pattern, tile_order, tall)

    up, um = shift(u, "x", -1), shift(u, "x", 1)
    ap, am, there = shift(mine, "y", -1), shift(mine, "y", 1), shift(mine, "zl", 1)
    up, um, ap, am, there = together(up, um, ap, am, there)
    u2, q = shift(um, "x", 1), shift(u, "zh", 1)
    tp, tm = shift(there, "y", -1), shift(there, "y", 1)
    u2, q, tp, tm = together(u2, q, tp, tm)
    qp, qm, q2 = shift(q, "x", -1), shift(q, "x", 1), shift(u2, "zh", 1)
    a2, t2 = shift(am, "y", 1), shift(tp, "y", -1)

    arrays = [u, up, u2, um]
    early, late = ((0, 0), (0, 1), (0, 3)), ((0, 2), (1, 0), (1, 1), (1, 2), (1, 3))
    sums = product(start, early, (0, 1, 3), [mine, ap, am, there, tp, tm], arrays * 2, pos, tall)
    arrays += [q, qp, q2, qm]
    a_parts = [mine, ap, a2, am, there, tp, t2, tm]
    other, own, flags = product(start, late, (0, 1, 2, 3), a_parts, arrays, pos, tall, sums)
    theirs = shift(other, "core", 1)
    return lax.cond(
        jnp.max(flags) > 0.5,
        lambda *args: dense(*args[:5]),
        lambda *args: args[5] + args[6],
        integrals,
        amplitudes,
        tile_pattern,
        pair_domain,
        tile_order,
        own,
        theirs,
    )


def solution(mesh):
    fine = Mesh(np.asarray(mesh.devices).reshape(SIZES), AXES)
    return jax.shard_map(
        on_device,
        mesh=fine,
        in_specs=(P(ROW, COL), P(ROW, COL), P(), P(None, COL), P()),
        out_specs=P(ROW, COL),
        check_vma=False,
    )
```

time: 116 us -> 107 us (0.922)
  Pallas kernels: 36.8 us -> 32.1 us
  local copies, waits for them, and re-layouts: 3.74 us -> 1.72 us
  other arithmetic: 6.72 us -> 4.73 us
    pallas_call x5 -> x4, Pallas kernels: 36.8 us -> 32.1 us  [the longest x2 23.4 us: product(): pl.pallas_call(functools.partial(product_kernel, tall, picks, hops, first...]
    another operation x3 -> x0, local copies, waits for them, and re-layouts: 1.95 us -> none  [blocks(): return [jnp.stack(v).astype(I32) for v in (ids, which, source)]]
    another operation x3 -> x0, other arithmetic: 1.86 us -> none  [the longest x2 1.24 us: blocks(): return [jnp.stack(v).astype(I32) for v in (ids, which, source)]]
  transfers between devices with their start and end apart: 16 -> 16, of which waited for: 4 -> 5; matrix products, arithmetic and copies ran while one was open for 5% -> 1% of each run, Pallas kernels for 16% -> 17%
where the time goes in v3:
time: 107 us
  Pallas kernels  32.1 us (30%)
  waiting for transfers between devices  27.9 us (26%)
  starting transfers between devices  26.1 us (24%)
  between operations  14.2 us (13%)
  other arithmetic  4.73 us (4%)
  local copies, waits for them, and re-layouts  1.72 us (2%)
    ppermute x16, waiting for transfers between devices, shift(): return lax.ppermute(value, axis, [(i, (i + by) % n) for i in range(n)])  27.9 us
    ppermute x16, starting transfers between devices, shift(): return lax.ppermute(value, axis, [(i, (i + by) % n) for i in range(n)])  26.1 us
    pallas_call x2, Pallas kernels, product(): pl.pallas_call(functools.partial(product_kernel, tall, picks, hops, first...  23.4 us
    pallas_call x1, Pallas kernels, pack(): pl.pallas_call(functools.partial(pack_kernel, tall, slots), grid_spec=plt...  5.39 us
    add x1, other arithmetic, on_device(): args[5] + args[6]  3.45 us
    pallas_call x1, Pallas kernels, join(): pl.pallas_call(functools.partial(join_kernel, tall), grid_spec=pltpu.Pref...  3.28 us
  transfers between devices with their start and end apart: 16, of which 5 were waited for; matrix products, arithmetic and copies ran while one was open for 1% of the time, Pallas kernels for 17%

profile of v3, /device:TPU:1, one launch (start us, length us, event | category | flops | bytes accessed | tf_op | source)
XLA Modules:
  0.0 106.7 jit_solution(12422215801655464689)
XLA Ops:
  6.5 1.4 %collective-permute-start = (bf16[384,768]{1,0:T(8,128)(2,1)}, bf16[384,768]{1,0:T(8,128)(2,1)S(1)}, u32[]{:S(2)}, u32[]{:S(2)}) collective-permute-start(bf16[384,768]{1,0:T(8,128)(2,1)} %a_ref.1), channel_id=1, source_target_pairs={{0,8},{8,0},{1,9},{9,1},{2,10},{10,2},{3,11},{11,3},{4,12},{12,4},... | collective-permute-start | bytes 1769480 | tf_op jit(solution)/shard_map/ppermute | solution.py:265
  8.0 5.4 %pack.1 = (s32[48,1536]{1,0:T(8,128)}, s32[48,128]{1,0:T(8,128)}, bf16[128,2560]{1,0:T(8,128)(2,1)}, bf16[8,384]{1,0:T(8,128)(2,1)}) custom-call(s32[48]{0:T(128)} %order.3, s32[48,1536]{1,0:T(8,128)} %d_ref.1, bf16[384,1536]{1,0:T(8,128)(2,1)} %b_ref.1), custom_call_target="tpu_custom_call" | custom-call | tf_op jit(solution)/shard_map/pack/pallas_call | solution.py:109
  13.4 2.6 %collective-permute-start.1 = (bf16[128,2560]{1,0:T(8,128)(2,1)}, bf16[128,2560]{1,0:T(8,128)(2,1)S(1)}, u32[]{:S(2)}, u32[]{:S(2)}) collective-permute-start(bf16[128,2560]{1,0:T(8,128)(2,1)} %get-tuple-element.50.refs_6_.refs_10_.refs_8_), channel_id=1, source_target_pairs={{0,48},{16,0},{32,16},{48,32},{1,49},{17,1},{33,17},{49,33},{2,50}... | collective-permute-start | bytes 1966088 | tf_op jit(solution)/shard_map/ppermute | solution.py:265
  16.0 0.0 collective-permute-start.2
  16.0 0.0 collective-permute-done.recv_ref
  16.0 0.0 copy-start.1
  16.0 0.8 copy-done.1
  16.8 3.3 %join.1.refs_0_ = bf16[776,384]{1,0:T(8,128)(2,1)} custom-call(s32[48]{0:T(128)} %order.3, s32[48,48]{1,0:T(8,128)} %pattern.1, bf16[8,384]{1,0:T(8,128)(2,1)} %get-tuple-element.49.over_ref, bf16[384,768]{1,0:T(8,128)(2,1)} %a_ref.1, bf16[384,768]{1,0:T(8,128)(2,1)} %copy-done.1), custom_call_target="tpu_custom_call" | custom-call | tf_op jit(solution)/shard_map/join/pallas_call | solution.py:52
  20.1 2.7 %collective-permute-start.3 = (bf16[776,384]{1,0:T(8,128)(2,1)}, bf16[776,384]{1,0:T(8,128)(2,1)S(1)}, u32[]{:S(2)}, u32[]{:S(2)}) collective-permute-start(bf16[776,384]{1,0:T(8,128)(2,1)} %join.1.refs_0_), channel_id=1, source_target_pairs={{0,3},{1,0},{2,1},{3,2},{4,7},{5,4},{6,5},{7,6},{8,11},{9,8},{10,9... | collective-permute-start | bytes 1787912 | tf_op jit(solution)/shard_map/ppermute | solution.py:265
  22.8 0.0 collective-permute-start.4
  22.8 1.6 %collective-permute-start.5 = (bf16[776,384]{1,0:T(8,128)(2,1)}, bf16[776,384]{1,0:T(8,128)(2,1)S(1)}, u32[]{:S(2)}, u32[]{:S(2)}) collective-permute-start(bf16[776,384]{1,0:T(8,128)(2,1)} %join.1.refs_0_), channel_id=1, source_target_pairs={{0,4},{4,0},{1,5},{5,1},{2,6},{6,2},{3,7},{7,3},{8,12},{12,8},{9,1... | collective-permute-start | bytes 1787912 | tf_op jit(solution)/shard_map/ppermute | solution.py:265
  24.5 6.0 %collective-permute-done.1.refs_7_.refs_11_.refs_9_ = bf16[128,2560]{1,0:T(8,128)(2,1)S(1)} collective-permute-done((bf16[128,2560]{1,0:T(8,128)(2,1)}, bf16[128,2560]{1,0:T(8,128)(2,1)S(1)}, u32[]{:S(2)}, u32[]{:S(2)}) %collective-permute-start.1) | collective-permute-done | bytes 655392 | tf_op jit(solution)/shard_map/ppermute | solution.py:265
  30.5 0.0 copy-start.5
  30.5 3.6 %collective-permute-start.8 = (bf16[128,2560]{1,0:T(8,128)(2,1)}, bf16[128,2560]{1,0:T(8,128)(2,1)S(1)}, u32[]{:S(2)}, u32[]{:S(2)}) collective-permute-start(bf16[128,2560]{1,0:T(8,128)(2,1)} %get-tuple-element.50.refs_6_.refs_10_.refs_8_), channel_id=1, source_target_pairs={{0,64},{64,0},{1,65},{65,1},{2,66},{66,2},{3,67},{67,3},{4,68},{68... | collective-permute-start | bytes 1966088 | tf_op jit(solution)/shard_map/ppermute | solution.py:265
  34.1 0.0 collective-permute-done.2.refs_9_.refs_13_.refs_11_
  34.1 0.0 copy-start.6
  34.1 1.6 %collective-permute-done.3.refs_1_ = bf16[776,384]{1,0:T(8,128)(2,1)S(1)} collective-permute-done((bf16[776,384]{1,0:T(8,128)(2,1)}, bf16[776,384]{1,0:T(8,128)(2,1)S(1)}, u32[]{:S(2)}, u32[]{:S(2)}) %collective-permute-start.3) | collective-permute-done | bytes 596000 | tf_op jit(solution)/shard_map/ppermute | solution.py:265
  35.7 0.0 copy-start.10
  35.7 3.1 %collective-permute-done.4.refs_2_.refs_3_ = bf16[776,384]{1,0:T(8,128)(2,1)} collective-permute-done((bf16[776,384]{1,0:T(8,128)(2,1)}, bf16[776,384]{1,0:T(8,128)(2,1)}, u32[]{:S(2)}, u32[]{:S(2)}) %collective-permute-start.4) | collective-permute-done | bytes 596000 | tf_op jit(solution)/shard_map/ppermute | solution.py:265
  38.8 0.0 copy-done.10
  38.8 0.0 collective-permute-done.5.refs_3_.refs_4_
  38.8 0.0 copy-start.11
  38.8 0.1 collective-permute-start.7
  38.9 1.4 %collective-permute-start.9 = (bf16[776,384]{1,0:T(8,128)(2,1)S(1)}, bf16[776,384]{1,0:T(8,128)(2,1)}, u32[]{:S(2)}, u32[]{:S(2)}) collective-permute-start(bf16[776,384]{1,0:T(8,128)(2,1)S(1)} %collective-permute-done.5.refs_3_.refs_4_), channel_id=1, source_target_pairs={{0,3},{1,0},{2,1},{3,2},{4,7},{5,4},{6,5},{7,6},{8,11},{9,8},{10,9... | collective-permute-start | bytes 1787912 | tf_op jit(solution)/shard_map/ppermute | solution.py:265
  40.3 0.1 collective-permute-start.10
  40.4 14.6 %collective-permute-done.8.refs_12_ = bf16[128,2560]{1,0:T(8,128)(2,1)S(1)} collective-permute-done((bf16[128,2560]{1,0:T(8,128)(2,1)}, bf16[128,2560]{1,0:T(8,128)(2,1)S(1)}, u32[]{:S(2)}, u32[]{:S(2)}) %collective-permute-start.8) | collective-permute-done | bytes 655392 | tf_op jit(solution)/shard_map/ppermute | solution.py:265
  55.0 0.0 copy-start.7
  55.0 0.0 collective-permute-done.9.refs_4_.refs_5_
  55.0 0.0 collective-permute-done.10.refs_5_.refs_7_
  55.0 0.0 copy-done.11
  55.0 0.0 copy-start.12
  55.0 0.0 collective-permute-done.7.refs_8_.refs_12_.refs_10_
  55.1 0.0 copy-start.8
  55.1 2.4 %collective-permute-start.12 = (bf16[128,2560]{1,0:T(8,128)(2,1)S(1)}, bf16[128,2560]{1,0:T(8,128)(2,1)S(1)}, u32[]{:S(2)}, u32[]{:S(2)}) collective-permute-start(bf16[128,2560]{1,0:T(8,128)(2,1)S(1)} %collective-permute-done.8.refs_12_), channel_id=1, source_target_pairs={{0,48},{16,0},{32,16},{48,32},{1,49},{17,1},{33,17},{49,33},{2,50}... | collective-permute-start | bytes 1966088 | tf_op jit(solution)/shard_map/ppermute | solution.py:265
  57.5 0.0 copy-done.12
  57.5 2.0 %collective-permute-start.13 = (bf16[128,2560]{1,0:T(8,128)(2,1)S(1)}, bf16[128,2560]{1,0:T(8,128)(2,1)}, u32[]{:S(2)}, u32[]{:S(2)}) collective-permute-start(bf16[128,2560]{1,0:T(8,128)(2,1)S(1)} %collective-permute-done.7.refs_8_.refs_12_.refs_10_), channel_id=1, source_target_pairs={{0,64},{64,0},{1,65},{65,1},{2,66},{66,2},{3,67},{67,3},{4,68},{68... | collective-permute-start | bytes 1966088 | tf_op jit(solution)/shard_map/ppermute | solution.py:265
  59.5 0.5 collective-permute-start.14
  60.0 0.0 collective-permute-start.6
  60.0 2.7 %collective-permute-start.11 = (bf16[776,384]{1,0:T(8,128)(2,1)}, bf16[776,384]{1,0:T(8,128)(2,1)}, u32[]{:S(2)}, u32[]{:S(2)}) collective-permute-start(bf16[776,384]{1,0:T(8,128)(2,1)} %collective-permute-done.9.refs_4_.refs_5_), channel_id=1, source_target_pairs={{0,3},{1,0},{2,1},{3,2},{4,7},{5,4},{6,5},{7,6},{8,11},{9,8},{10,9... | collective-permute-start | bytes 1787912 | tf_op jit(solution)/shard_map/ppermute | solution.py:265
  62.7 0.0 copy-done.5
  62.7 0.0 copy-done.6
  62.7 0.0 copy-done.8
  62.7 9.9 %product.2 = (f32[384,1536]{1,0:T(8,128)}, f32[384,1536]{1,0:T(8,128)}, f32[8,128]{1,0:T(8,128)}) custom-call(s32[48,128]{1,0:T(8,128)} %get-tuple-element.48.start_ref, bf16[776,384]{1,0:T(8,128)(2,1)} %join.1.refs_0_, bf16[776,384]{1,0:T(8,128)(2,1)} %copy-done.10, bf16[776,384]{1,0:T(8,128)(2,1)} %collective-permute-done.4.refs_2_.refs_3_, ...), custom_call_target="tpu_custom_call" | custom-call | flops 2717908992 | bytes 10045440 | tf_op jit(solution)/shard_map/product/pallas_call | solution.py:234
  72.6 0.0 copy-done.7
  72.6 0.0 collective-permute-done.6.refs_2_
  72.6 0.0 collective-permute-done.11.refs_6_
  72.6 0.0 collective-permute-done.12.refs_13_
  72.6 0.0 copy-start.9
  72.7 0.0 collective-permute-done.13.refs_14_
  72.7 0.0 collective-permute-done.14.refs_15_
  72.7 0.9 copy-done.9
  73.6 0.0 copy-start
  73.6 0.0 copy-start.2
  73.6 0.0 copy-start.3
  73.6 13.5 %product.3 = (f32[384,1536]{1,0:T(8,128)}, f32[384,1536]{1,0:T(8,128)S(1)}, f32[8,128]{1,0:T(8,128)}) custom-call(s32[48,128]{1,0:T(8,128)} %get-tuple-element.48.start_ref, bf16[776,384]{1,0:T(8,128)(2,1)} %join.1.refs_0_, bf16[776,384]{1,0:T(8,128)(2,1)} %copy-done.10, bf16[776,384]{1,0:T(8,128)(2,1)} %collective-permute-done.6.refs_2_, ...), custom_call_target="tpu_custom_call" | custom-call | flops 4529848320 | bytes 13596672 | tf_op jit(solution)/shard_map/product/pallas_call | solution.py:234
  87.1 4.8 %collective-permute-start.15 = (f32[384,1536]{1,0:T(8,128)}, f32[384,1536]{1,0:T(8,128)}, u32[]{:S(2)}, u32[]{:S(2)}) collective-permute-start(f32[384,1536]{1,0:T(8,128)} %get-tuple-element.66), channel_id=1, source_target_pairs={{0,8},{8,0},{1,9},{9,1},{2,10},{10,2},{3,11},{11,3},{4,12},{12,4},... | collective-permute-start | bytes 7077896 | tf_op jit(solution)/shard_map/ppermute | solution.py:265
  91.9 1.3 %reduce_max.9 = f32[]{:T(128)} reduce(f32[8,128]{1,0:T(8,128)} %get-tuple-element.64, f32[]{:T(128)} %constant.27.clone.1), dimensions={0,1}, to_apply=%region_0.0 | reduce | flops 1023 | bytes 4104 | tf_op jit(solution)/shard_map/reduce_max | solution.py:311
  93.8 2.6 %collective-permute-done.15 = f32[384,1536]{1,0:T(8,128)} collective-permute-done((f32[384,1536]{1,0:T(8,128)}, f32[384,1536]{1,0:T(8,128)}, u32[]{:S(2)}, u32[]{:S(2)}) %collective-permute-start.15) | collective-permute-done | bytes 2359328 | tf_op jit(solution)/shard_map/ppermute | solution.py:265
  96.4 0.0 copy-done
  96.4 0.0 copy-done.2
  96.4 0.0 copy-done.3
  96.4 3.4 %conditional.1 = (f32[384,1536]{1,0:T(8,128)}) conditional(s32[]{:T(128)} %convert_element_type.28, (f32[384,1536]{1,0:T(8,128)S(1)}, f32[384,1536]{1,0:T(8,128)}) %tuple.15, (bf16[384,768]{1,0:T(8,128)(2,1)}, s32[48]{0:T(128)S(1)}, s32[48,48]{1,0:T(8,128)S(1)}, bf16[384,1536]{1,0:T(8,128)(2,1)}, s32[48,1536]{1,0:T(8,128)S(1)}) %tuple.27), branch_computations={%region_1.0_spmd, %region_2.0_spmd} | conditional | flops 7304832000 | bytes 168797408 | solution.py:310
  96.4 3.4 %add.8 = f32[384,1536]{1,0:T(8,128)} add(f32[384,1536]{1,0:T(8,128)S(1)} %get-tuple-element.22, f32[384,1536]{1,0:T(8,128)} %get-tuple-element.23) | non-fusion elementwise | flops 589824 | bytes 7077888 | tf_op jit(solution)/shard_map/cond/branch_0_fun/add | solution.py:313
Async XLA Ops:
  6.5 9.5 %collective-permute-start = (bf16[384,768]{1,0:T(8,128)(2,1)}, bf16[384,768]{1,0:T(8,128)(2,1)S(1)}, u32[]{:S(2)}, u32[]{:S(2)}) collective-permute-start(bf16[384,768]{1,0:T(8,128)(2,1)} %a_ref.1), channel_id=1, source_target_pairs={{0,8},{8,0},{1,9},{9,1},{2,10},{10,2},{3,11},{11,3},{4,12},{12,4},... | collective-permute-start | bytes 1769480 | tf_op jit(solution)/shard_map/ppermute | solution.py:265
  13.4 17.1 %collective-permute-start.1 = (bf16[128,2560]{1,0:T(8,128)(2,1)}, bf16[128,2560]{1,0:T(8,128)(2,1)S(1)}, u32[]{:S(2)}, u32[]{:S(2)}) collective-permute-start(bf16[128,2560]{1,0:T(8,128)(2,1)} %get-tuple-element.50.refs_6_.refs_10_.refs_8_), channel_id=1, source_target_pairs={{0,48},{16,0},{32,16},{48,32},{1,49},{17,1},{33,17},{49,33},{2,50}... | collective-permute-start | bytes 1966088 | tf_op jit(solution)/shard_map/ppermute | solution.py:265
  16.0 18.1 %collective-permute-start.2 = (bf16[128,2560]{1,0:T(8,128)(2,1)}, bf16[128,2560]{1,0:T(8,128)(2,1)S(1)}, u32[]{:S(2)}, u32[]{:S(2)}) collective-permute-start(bf16[128,2560]{1,0:T(8,128)(2,1)} %get-tuple-element.50.refs_6_.refs_10_.refs_8_), channel_id=1, source_target_pairs={{0,16},{16,32},{32,48},{48,0},{1,17},{17,33},{33,49},{49,1},{2,18}... | collective-permute-start | bytes 1966088 | tf_op jit(solution)/shard_map/ppermute | solution.py:265
  16.0 0.8 copy-start.1
  20.1 15.6 %collective-permute-start.3 = (bf16[776,384]{1,0:T(8,128)(2,1)}, bf16[776,384]{1,0:T(8,128)(2,1)S(1)}, u32[]{:S(2)}, u32[]{:S(2)}) collective-permute-start(bf16[776,384]{1,0:T(8,128)(2,1)} %join.1.refs_0_), channel_id=1, source_target_pairs={{0,3},{1,0},{2,1},{3,2},{4,7},{5,4},{6,5},{7,6},{8,11},{9,8},{10,9... | collective-permute-start | bytes 1787912 | tf_op jit(solution)/shard_map/ppermute | solution.py:265
  22.8 16.0 %collective-permute-start.4 = (bf16[776,384]{1,0:T(8,128)(2,1)}, bf16[776,384]{1,0:T(8,128)(2,1)}, u32[]{:S(2)}, u32[]{:S(2)}) collective-permute-start(bf16[776,384]{1,0:T(8,128)(2,1)} %join.1.refs_0_), channel_id=1, source_target_pairs={{0,1},{1,2},{2,3},{3,0},{4,5},{5,6},{6,7},{7,4},{8,9},{9,10},{10,1... | collective-permute-start | bytes 1787912 | tf_op jit(solution)/shard_map/ppermute | solution.py:265
  22.8 16.0 %collective-permute-start.5 = (bf16[776,384]{1,0:T(8,128)(2,1)}, bf16[776,384]{1,0:T(8,128)(2,1)S(1)}, u32[]{:S(2)}, u32[]{:S(2)}) collective-permute-start(bf16[776,384]{1,0:T(8,128)(2,1)} %join.1.refs_0_), channel_id=1, source_target_pairs={{0,4},{4,0},{1,5},{5,1},{2,6},{6,2},{3,7},{7,3},{8,12},{12,8},{9,1... | collective-permute-start | bytes 1787912 | tf_op jit(solution)/shard_map/ppermute | solution.py:265
  30.5 32.2 %copy-start.5 = (bf16[128,2560]{1,0:T(8,128)(2,1)}, bf16[128,2560]{1,0:T(8,128)(2,1)S(1)}, u32[]{:S(2)}) copy-start(bf16[128,2560]{1,0:T(8,128)(2,1)S(1)} %collective-permute-done.1.refs_7_.refs_11_.refs_9_) | copy-start | bytes 1966084
  30.5 24.5 %collective-permute-start.8 = (bf16[128,2560]{1,0:T(8,128)(2,1)}, bf16[128,2560]{1,0:T(8,128)(2,1)S(1)}, u32[]{:S(2)}, u32[]{:S(2)}) collective-permute-start(bf16[128,2560]{1,0:T(8,128)(2,1)} %get-tuple-element.50.refs_6_.refs_10_.refs_8_), channel_id=1, source_target_pairs={{0,64},{64,0},{1,65},{65,1},{2,66},{66,2},{3,67},{67,3},{4,68},{68... | collective-permute-start | bytes 1966088 | tf_op jit(solution)/shard_map/ppermute | solution.py:265
  34.1 28.6 %copy-start.6 = (bf16[128,2560]{1,0:T(8,128)(2,1)}, bf16[128,2560]{1,0:T(8,128)(2,1)S(1)}, u32[]{:S(2)}) copy-start(bf16[128,2560]{1,0:T(8,128)(2,1)S(1)} %collective-permute-done.2.refs_9_.refs_13_.refs_11_) | copy-start | bytes 1966084
  35.7 3.1 %copy-start.10 = (bf16[776,384]{1,0:T(8,128)(2,1)}, bf16[776,384]{1,0:T(8,128)(2,1)S(1)}, u32[]{:S(2)}) copy-start(bf16[776,384]{1,0:T(8,128)(2,1)S(1)} %collective-permute-done.3.refs_1_) | copy-start | bytes 1787908
  38.8 16.2 %copy-start.11 = (bf16[776,384]{1,0:T(8,128)(2,1)}, bf16[776,384]{1,0:T(8,128)(2,1)S(1)}, u32[]{:S(2)}) copy-start(bf16[776,384]{1,0:T(8,128)(2,1)S(1)} %collective-permute-done.5.refs_3_.refs_4_) | copy-start | bytes 1787908
  38.8 16.2 %collective-permute-start.7 = (bf16[128,2560]{1,0:T(8,128)(2,1)S(1)}, bf16[128,2560]{1,0:T(8,128)(2,1)S(1)}, u32[]{:S(2)}, u32[]{:S(2)}) collective-permute-start(bf16[128,2560]{1,0:T(8,128)(2,1)S(1)} %collective-permute-done.2.refs_9_.refs_13_.refs_11_), channel_id=1, source_target_pairs={{0,16},{16,32},{32,48},{48,0},{1,17},{17,33},{33,49},{49,1},{2,18}... | collective-permute-start | bytes 1966088 | tf_op jit(solution)/shard_map/ppermute | solution.py:265
  38.9 16.1 %collective-permute-start.9 = (bf16[776,384]{1,0:T(8,128)(2,1)S(1)}, bf16[776,384]{1,0:T(8,128)(2,1)}, u32[]{:S(2)}, u32[]{:S(2)}) collective-permute-start(bf16[776,384]{1,0:T(8,128)(2,1)S(1)} %collective-permute-done.5.refs_3_.refs_4_), channel_id=1, source_target_pairs={{0,3},{1,0},{2,1},{3,2},{4,7},{5,4},{6,5},{7,6},{8,11},{9,8},{10,9... | collective-permute-start | bytes 1787912 | tf_op jit(solution)/shard_map/ppermute | solution.py:265
  40.3 14.7 %collective-permute-start.10 = (bf16[776,384]{1,0:T(8,128)(2,1)S(1)}, bf16[776,384]{1,0:T(8,128)(2,1)S(1)}, u32[]{:S(2)}, u32[]{:S(2)}) collective-permute-start(bf16[776,384]{1,0:T(8,128)(2,1)S(1)} %collective-permute-done.5.refs_3_.refs_4_), channel_id=1, source_target_pairs={{0,1},{1,2},{2,3},{3,0},{4,5},{5,6},{6,7},{7,4},{8,9},{9,10},{10,1... | collective-permute-start | bytes 1787912 | tf_op jit(solution)/shard_map/ppermute | solution.py:265
  55.0 17.6 %copy-start.7 = (bf16[128,2560]{1,0:T(8,128)(2,1)}, bf16[128,2560]{1,0:T(8,128)(2,1)S(1)}, u32[]{:S(2)}) copy-start(bf16[128,2560]{1,0:T(8,128)(2,1)S(1)} %collective-permute-done.8.refs_12_) | copy-start | bytes 1966084
  55.0 2.5 %copy-start.12 = (bf16[776,384]{1,0:T(8,128)(2,1)}, bf16[776,384]{1,0:T(8,128)(2,1)S(1)}, u32[]{:S(2)}) copy-start(bf16[776,384]{1,0:T(8,128)(2,1)S(1)} %collective-permute-done.10.refs_5_.refs_7_) | copy-start | bytes 1787908
  55.1 7.6 %copy-start.8 = (bf16[128,2560]{1,0:T(8,128)(2,1)}, bf16[128,2560]{1,0:T(8,128)(2,1)S(1)}, u32[]{:S(2)}) copy-start(bf16[128,2560]{1,0:T(8,128)(2,1)S(1)} %collective-permute-done.7.refs_8_.refs_12_.refs_10_) | copy-start | bytes 1966084
  55.1 17.6 %collective-permute-start.12 = (bf16[128,2560]{1,0:T(8,128)(2,1)S(1)}, bf16[128,2560]{1,0:T(8,128)(2,1)S(1)}, u32[]{:S(2)}, u32[]{:S(2)}) collective-permute-start(bf16[128,2560]{1,0:T(8,128)(2,1)S(1)} %collective-permute-done.8.refs_12_), channel_id=1, source_target_pairs={{0,48},{16,0},{32,16},{48,32},{1,49},{17,1},{33,17},{49,33},{2,50}... | collective-permute-start | bytes 1966088 | tf_op jit(solution)/shard_map/ppermute | solution.py:265
  57.5 15.2 %collective-permute-start.13 = (bf16[128,2560]{1,0:T(8,128)(2,1)S(1)}, bf16[128,2560]{1,0:T(8,128)(2,1)}, u32[]{:S(2)}, u32[]{:S(2)}) collective-permute-start(bf16[128,2560]{1,0:T(8,128)(2,1)S(1)} %collective-permute-done.7.refs_8_.refs_12_.refs_10_), channel_id=1, source_target_pairs={{0,64},{64,0},{1,65},{65,1},{2,66},{66,2},{3,67},{67,3},{4,68},{68... | collective-permute-start | bytes 1966088 | tf_op jit(solution)/shard_map/ppermute | solution.py:265
  59.5 13.2 %collective-permute-start.14 = (bf16[128,2560]{1,0:T(8,128)(2,1)S(1)}, bf16[128,2560]{1,0:T(8,128)(2,1)}, u32[]{:S(2)}, u32[]{:S(2)}) collective-permute-start(bf16[128,2560]{1,0:T(8,128)(2,1)S(1)} %collective-permute-done.8.refs_12_), channel_id=1, source_target_pairs={{0,16},{16,32},{32,48},{48,0},{1,17},{17,33},{33,49},{49,1},{2,18}... | collective-permute-start | bytes 1966088 | tf_op jit(solution)/shard_map/ppermute | solution.py:265
  60.0 12.6 %collective-permute-start.6 = (bf16[776,384]{1,0:T(8,128)(2,1)}, bf16[776,384]{1,0:T(8,128)(2,1)}, u32[]{:S(2)}, u32[]{:S(2)}) collective-permute-start(bf16[776,384]{1,0:T(8,128)(2,1)} %collective-permute-done.4.refs_2_.refs_3_), channel_id=1, source_target_pairs={{0,1},{1,2},{2,3},{3,0},{4,5},{5,6},{6,7},{7,4},{8,9},{9,10},{10,1... | collective-permute-start | bytes 1787912 | tf_op jit(solution)/shard_map/ppermute | solution.py:265
  60.0 12.6 %collective-permute-start.11 = (bf16[776,384]{1,0:T(8,128)(2,1)}, bf16[776,384]{1,0:T(8,128)(2,1)}, u32[]{:S(2)}, u32[]{:S(2)}) collective-permute-start(bf16[776,384]{1,0:T(8,128)(2,1)} %collective-permute-done.9.refs_4_.refs_5_), channel_id=1, source_target_pairs={{0,3},{1,0},{2,1},{3,2},{4,7},{5,4},{6,5},{7,6},{8,11},{9,8},{10,9... | collective-permute-start | bytes 1787912 | tf_op jit(solution)/shard_map/ppermute | solution.py:265
  72.6 0.9 copy-start.9
  73.6 22.9 %copy-start = (s32[48,1536]{1,0:T(8,128)S(1)}, s32[48,1536]{1,0:T(8,128)}, u32[]{:S(2)}) copy-start(s32[48,1536]{1,0:T(8,128)} %d_ref.1) | copy-start | bytes 884740
  73.6 22.9 %copy-start.2 = (s32[48,48]{1,0:T(8,128)S(1)}, s32[48,48]{1,0:T(8,128)}, u32[]{:S(2)}) copy-start(s32[48,48]{1,0:T(8,128)} %pattern.1) | copy-start | bytes 27652
  73.6 22.9 %copy-start.3 = (s32[48]{0:T(128)S(1)}, s32[48]{0:T(128)}, u32[]{:S(2)}) copy-start(s32[48]{0:T(128)} %order.3) | copy-start | bytes 580
  87.1 9.3 %collective-permute-start.15 = (f32[384,1536]{1,0:T(8,128)}, f32[384,1536]{1,0:T(8,128)}, u32[]{:S(2)}, u32[]{:S(2)}) collective-permute-start(f32[384,1536]{1,0:T(8,128)} %get-tuple-element.66), channel_id=1, source_target_pairs={{0,8},{8,0},{1,9},{9,1},{2,10},{10,2},{3,11},{11,3},{4,12},{12,4},... | collective-permute-start | bytes 7077896 | tf_op jit(solution)/shard_map/ppermute | solution.py:265

commit v4 on v3

--- a/solution.py
+++ b/solution.py
@@ -14,7 +14,7 @@
 ROW, COL = ("zh", "x", "core"), ("zl", "y")
 BF16, F32, I32 = jnp.bfloat16, jnp.float32, jnp.int32
 FLAG_ROWS = 8
-VMEM_LIMIT = 60 << 20
+VMEM_LIMIT, LAST_LIMIT = 255 << 18, 60 << 20
 
 
 def where_am_i():
@@ -55,6 +55,7 @@
             num_scalar_prefetch=2, grid=(), in_specs=whole(3), out_specs=pl.BlockSpec(memory_space=pltpu.VMEM)
         ),
         out_shape=jax.ShapeDtypeStruct((2 * rows + FLAG_ROWS, cols // 2), BF16),
+        compiler_params=pltpu.CompilerParams(vmem_limit_bytes=VMEM_LIMIT),
         name="join",
     )(tile_order, tile_pattern, over, integrals, recv)
 
@@ -126,6 +127,7 @@
             jax.ShapeDtypeStruct((TILE, slots), BF16),
             jax.ShapeDtypeStruct((FLAG_ROWS, cols), BF16),
         ],
+        compiler_params=pltpu.CompilerParams(vmem_limit_bytes=VMEM_LIMIT),
         name="pack",
     )(tile_order, pair_domain, amplitudes)
 
@@ -252,7 +254,7 @@
             ],
         ),
         out_shape=[jax.ShapeDtypeStruct((rows, pairs), F32)] * 2 + [jax.ShapeDtypeStruct((FLAG_ROWS, TILE), F32)],
-        compiler_params=pltpu.CompilerParams(vmem_limit_bytes=VMEM_LIMIT),
+        compiler_params=pltpu.CompilerParams(vmem_limit_bytes=VMEM_LIMIT if first else LAST_LIMIT),
         cost_estimate=pl.CostEstimate(
             flops=4 * rows * n * depth * pairs, bytes_accessed=2 * n * depth * (high + pairs) + 8 * rows * pairs, transcendentals=0
         ),
@@ -296,13 +298,12 @@
     up, um, ap, am, there = together(up, um, ap, am, there)
     u2, q = shift(um, "x", 1), shift(u, "zh", 1)
     tp, tm = shift(there, "y", -1), shift(there, "y", 1)
-    u2, q, tp, tm = together(u2, q, tp, tm)
     qp, qm, q2 = shift(q, "x", -1), shift(q, "x", 1), shift(u2, "zh", 1)
     a2, t2 = shift(am, "y", 1), shift(tp, "y", -1)
 
     arrays = [u, up, u2, um]
     early, late = ((0, 0), (0, 1), (0, 3)), ((0, 2), (1, 0), (1, 1), (1, 2), (1, 3))
-    sums = product(start, early, (0, 1, 3), [mine, ap, am, there, tp, tm], arrays * 2, pos, tall)
+    sums = product(start, early, (0, 1, 3), [mine, ap, am, there, tp, tm], arrays + [q] * 4, pos, tall)
     arrays += [q, qp, q2, qm]
     a_parts = [mine, ap, a2, am, there, tp, t2, tm]
     other, own, flags = product(start, late, (0, 1, 2, 3), a_parts, arrays, pos, tall, sums)

time: 107 us -> 104 us (0.972)
  starting transfers between devices: 26.1 us -> 22.9 us
  waiting for transfers between devices: 27.9 us -> 29.4 us
    ppermute x16, starting transfers between devices: 26.1 us -> 22.9 us  [shift(): return lax.ppermute(value, axis, [(i, (i + by) % n) for i in range(n)])]
    ppermute x16, waiting for transfers between devices: 27.9 us -> 29.4 us  [shift(): return lax.ppermute(value, axis, [(i, (i + by) % n) for i in range(n)])]
  transfers between devices with their start and end apart: 16 -> 16, of which waited for: 5 -> 7; matrix products, arithmetic and copies ran while one was open for 1% -> 1% of each run, Pallas kernels for 17% -> 18%
where the time goes in v4:
time: 104 us
  Pallas kernels  32.1 us (31%)
  waiting for transfers between devices  29.4 us (28%)
  starting transfers between devices  22.9 us (22%)
  between operations  14.1 us (14%)
  other arithmetic  4.73 us (5%)
    ppermute x16, waiting for transfers between devices, shift(): return lax.ppermute(value, axis, [(i, (i + by) % n) for i in range(n)])  29.4 us
    pallas_call x2, Pallas kernels, product(): pl.pallas_call(functools.partial(product_kernel, tall, picks, hops, first...  23.5 us
    ppermute x16, starting transfers between devices, shift(): return lax.ppermute(value, axis, [(i, (i + by) % n) for i in range(n)])  22.9 us
    pallas_call x1, Pallas kernels, pack(): pl.pallas_call(functools.partial(pack_kernel, tall, slots), grid_spec=plt...  5.36 us
    add x1, other arithmetic, on_device(): args[5] + args[6]  3.45 us
    pallas_call x1, Pallas kernels, join(): pl.pallas_call(functools.partial(join_kernel, tall), grid_spec=pltpu.Pref...  3.28 us
  transfers between devices with their start and end apart: 16, of which 7 were waited for; matrix products, arithmetic and copies ran while one was open for 1% of the time, Pallas kernels for 18%

profile of v4, /device:TPU:1, one launch (start us, length us, event | category | flops | bytes accessed | tf_op | source)
XLA Modules:
  0.0 104.0 jit_solution(18183947837863186151)
XLA Ops:
  6.5 1.4 %collective-permute-start = (bf16[384,768]{1,0:T(8,128)(2,1)}, bf16[384,768]{1,0:T(8,128)(2,1)}, u32[]{:S(2)}, u32[]{:S(2)}) collective-permute-start(bf16[384,768]{1,0:T(8,128)(2,1)} %a_ref.1), channel_id=1, source_target_pairs={{0,8},{8,0},{1,9},{9,1},{2,10},{10,2},{3,11},{11,3},{4,12},{12,4},... | collective-permute-start | bytes 1769480 | tf_op jit(solution)/shard_map/ppermute | solution.py:267
  8.0 5.4 %pack.1 = (s32[48,1536]{1,0:T(8,128)}, s32[48,128]{1,0:T(8,128)}, bf16[128,2560]{1,0:T(8,128)(2,1)}, bf16[8,384]{1,0:T(8,128)(2,1)}) custom-call(s32[48]{0:T(128)} %order.3, s32[48,1536]{1,0:T(8,128)} %d_ref.1, bf16[384,1536]{1,0:T(8,128)(2,1)} %b_ref.1), custom_call_target="tpu_custom_call" | custom-call | tf_op jit(solution)/shard_map/pack/pallas_call | solution.py:110
  13.3 2.6 %collective-permute-start.1 = (bf16[128,2560]{1,0:T(8,128)(2,1)}, bf16[128,2560]{1,0:T(8,128)(2,1)}, u32[]{:S(2)}, u32[]{:S(2)}) collective-permute-start(bf16[128,2560]{1,0:T(8,128)(2,1)} %get-tuple-element.46.refs_6_.refs_8_), channel_id=1, source_target_pairs={{0,48},{16,0},{32,16},{48,32},{1,49},{17,1},{33,17},{49,33},{2,50}... | collective-permute-start | bytes 1966088 | tf_op jit(solution)/shard_map/ppermute | solution.py:267
  16.0 0.0 collective-permute-start.2
  16.0 0.0 collective-permute-done.recv_ref
  16.0 3.3 %join.1.refs_0_ = bf16[776,384]{1,0:T(8,128)(2,1)} custom-call(s32[48]{0:T(128)} %order.3, s32[48,48]{1,0:T(8,128)} %pattern.1, bf16[8,384]{1,0:T(8,128)(2,1)} %get-tuple-element.45.over_ref, bf16[384,768]{1,0:T(8,128)(2,1)} %a_ref.1, bf16[384,768]{1,0:T(8,128)(2,1)} %collective-permute-done.recv_ref), custom_call_target="tpu_custom_call" | custom-call | tf_op jit(solution)/shard_map/join/pallas_call | solution.py:52
  19.2 2.7 %collective-permute-start.3 = (bf16[776,384]{1,0:T(8,128)(2,1)}, bf16[776,384]{1,0:T(8,128)(2,1)}, u32[]{:S(2)}, u32[]{:S(2)}) collective-permute-start(bf16[776,384]{1,0:T(8,128)(2,1)} %join.1.refs_0_), channel_id=1, source_target_pairs={{0,3},{1,0},{2,1},{3,2},{4,7},{5,4},{6,5},{7,6},{8,11},{9,8},{10,9... | collective-permute-start | bytes 1787912 | tf_op jit(solution)/shard_map/ppermute | solution.py:267
  22.0 0.0 collective-permute-start.4
  22.0 1.6 %collective-permute-start.5 = (bf16[776,384]{1,0:T(8,128)(2,1)}, bf16[776,384]{1,0:T(8,128)(2,1)S(1)}, u32[]{:S(2)}, u32[]{:S(2)}) collective-permute-start(bf16[776,384]{1,0:T(8,128)(2,1)} %join.1.refs_0_), channel_id=1, source_target_pairs={{0,4},{4,0},{1,5},{5,1},{2,6},{6,2},{3,7},{7,3},{8,12},{12,8},{9,1... | collective-permute-start | bytes 1787912 | tf_op jit(solution)/shard_map/ppermute | solution.py:267
  23.6 6.8 %collective-permute-done.1.refs_7_.refs_9_ = bf16[128,2560]{1,0:T(8,128)(2,1)} collective-permute-done((bf16[128,2560]{1,0:T(8,128)(2,1)}, bf16[128,2560]{1,0:T(8,128)(2,1)}, u32[]{:S(2)}, u32[]{:S(2)}) %collective-permute-start.1) | collective-permute-done | bytes 655392 | tf_op jit(solution)/shard_map/ppermute | solution.py:267
  30.4 3.6 %collective-permute-start.11 = (bf16[128,2560]{1,0:T(8,128)(2,1)}, bf16[128,2560]{1,0:T(8,128)(2,1)}, u32[]{:S(2)}, u32[]{:S(2)}) collective-permute-start(bf16[128,2560]{1,0:T(8,128)(2,1)} %get-tuple-element.46.refs_6_.refs_8_), channel_id=1, source_target_pairs={{0,64},{64,0},{1,65},{65,1},{2,66},{66,2},{3,67},{67,3},{4,68},{68... | collective-permute-start | bytes 1966088 | tf_op jit(solution)/shard_map/ppermute | solution.py:267
  34.0 0.0 collective-permute-done.2.refs_9_.refs_11_
  34.0 0.8 collective-permute-done.3.refs_1_
  34.9 3.1 %collective-permute-done.4.refs_2_.refs_3_ = bf16[776,384]{1,0:T(8,128)(2,1)} collective-permute-done((bf16[776,384]{1,0:T(8,128)(2,1)}, bf16[776,384]{1,0:T(8,128)(2,1)}, u32[]{:S(2)}, u32[]{:S(2)}) %collective-permute-start.4) | collective-permute-done | bytes 596000 | tf_op jit(solution)/shard_map/ppermute | solution.py:267
  38.0 0.0 collective-permute-done.5.refs_3_.refs_4_
  38.0 0.0 copy-start.4
  38.0 0.0 collective-permute-start.10
  38.0 1.5 %collective-permute-start.7 = (bf16[776,384]{1,0:T(8,128)(2,1)S(1)}, bf16[776,384]{1,0:T(8,128)(2,1)}, u32[]{:S(2)}, u32[]{:S(2)}) collective-permute-start(bf16[776,384]{1,0:T(8,128)(2,1)S(1)} %collective-permute-done.5.refs_3_.refs_4_), channel_id=1, source_target_pairs={{0,3},{1,0},{2,1},{3,2},{4,7},{5,4},{6,5},{7,6},{8,11},{9,8},{10,9... | collective-permute-start | bytes 1787912 | tf_op jit(solution)/shard_map/ppermute | solution.py:267
  39.5 0.0 copy-done.4
  39.5 0.1 collective-permute-start.9
  39.5 14.8 %collective-permute-done.11.refs_10_.refs_11_.refs_12_.refs_13_ = bf16[128,2560]{1,0:T(8,128)(2,1)} collective-permute-done((bf16[128,2560]{1,0:T(8,128)(2,1)}, bf16[128,2560]{1,0:T(8,128)(2,1)}, u32[]{:S(2)}, u32[]{:S(2)}) %collective-permute-start.11) | collective-permute-done | bytes 655392 | tf_op jit(solution)/shard_map/ppermute | solution.py:267
  54.3 2.4 %collective-permute-start.12 = (bf16[128,2560]{1,0:T(8,128)(2,1)}, bf16[128,2560]{1,0:T(8,128)(2,1)}, u32[]{:S(2)}, u32[]{:S(2)}) collective-permute-start(bf16[128,2560]{1,0:T(8,128)(2,1)} %collective-permute-done.11.refs_10_.refs_11_.refs_12_.refs_13_), channel_id=1, source_target_pairs={{0,48},{16,0},{32,16},{48,32},{1,49},{17,1},{33,17},{49,33},{2,50}... | collective-permute-start | bytes 1966088 | tf_op jit(solution)/shard_map/ppermute | solution.py:267
  56.6 0.0 collective-permute-start.14
  56.6 0.0 collective-permute-done.10.refs_8_.refs_10_
  56.6 1.3 %collective-permute-start.13 = (bf16[128,2560]{1,0:T(8,128)(2,1)}, bf16[128,2560]{1,0:T(8,128)(2,1)}, u32[]{:S(2)}, u32[]{:S(2)}) collective-permute-start(bf16[128,2560]{1,0:T(8,128)(2,1)} %collective-permute-done.10.refs_8_.refs_10_), channel_id=1, source_target_pairs={{0,64},{64,0},{1,65},{65,1},{2,66},{66,2},{3,67},{67,3},{4,68},{68... | collective-permute-start | bytes 1966088 | tf_op jit(solution)/shard_map/ppermute | solution.py:267
  57.9 0.0 collective-permute-done.7.refs_4_.refs_5_
  57.9 0.0 collective-permute-start.6
  57.9 0.0 collective-permute-done.9.refs_5_.refs_7_
  57.9 0.0 copy-start.5
  57.9 0.8 copy-done.5
  58.8 2.7 %collective-permute-start.8 = (bf16[776,384]{1,0:T(8,128)(2,1)}, bf16[776,384]{1,0:T(8,128)(2,1)}, u32[]{:S(2)}, u32[]{:S(2)}) collective-permute-start(bf16[776,384]{1,0:T(8,128)(2,1)} %collective-permute-done.7.refs_4_.refs_5_), channel_id=1, source_target_pairs={{0,3},{1,0},{2,1},{3,2},{4,7},{5,4},{6,5},{7,6},{8,11},{9,8},{10,9... | collective-permute-start | bytes 1787912 | tf_op jit(solution)/shard_map/ppermute | solution.py:267
  61.4 9.9 %product.2 = (f32[384,1536]{1,0:T(8,128)}, f32[384,1536]{1,0:T(8,128)}, f32[8,128]{1,0:T(8,128)}) custom-call(s32[48,128]{1,0:T(8,128)} %get-tuple-element.44.start_ref, bf16[776,384]{1,0:T(8,128)(2,1)} %join.1.refs_0_, bf16[776,384]{1,0:T(8,128)(2,1)} %collective-permute-done.3.refs_1_, bf16[776,384]{1,0:T(8,128)(2,1)} %collective-permute-done.4.refs_2_.refs_3_, ...), custom_call_target="tpu_custom_call" | custom-call | flops 2717908992 | bytes 10045440 | tf_op jit(solution)/shard_map/product/pallas_call | solution.py:236
  71.4 0.0 collective-permute-done.12.refs_13_
  71.4 1.0 collective-permute-done.14.refs_15_
  72.4 0.0 collective-permute-done.6.refs_2_
  72.4 0.0 collective-permute-done.8.refs_6_
  72.4 0.3 collective-permute-done.13.refs_14_
  72.7 0.0 copy-start
  72.7 0.0 copy-start.1
  72.7 0.0 copy-start.2
  72.7 13.5 %product.3 = (f32[384,1536]{1,0:T(8,128)}, f32[384,1536]{1,0:T(8,128)S(1)}, f32[8,128]{1,0:T(8,128)}) custom-call(s32[48,128]{1,0:T(8,128)} %get-tuple-element.44.start_ref, bf16[776,384]{1,0:T(8,128)(2,1)} %join.1.refs_0_, bf16[776,384]{1,0:T(8,128)(2,1)} %collective-permute-done.3.refs_1_, bf16[776,384]{1,0:T(8,128)(2,1)} %collective-permute-done.6.refs_2_, ...), custom_call_target="tpu_custom_call" | custom-call | flops 4529848320 | bytes 13596672 | tf_op jit(solution)/shard_map/product/pallas_call | solution.py:236
  86.2 3.0 %collective-permute-start.15 = (f32[384,1536]{1,0:T(8,128)}, f32[384,1536]{1,0:T(8,128)}, u32[]{:S(2)}, u32[]{:S(2)}) collective-permute-start(f32[384,1536]{1,0:T(8,128)} %get-tuple-element.58), channel_id=1, source_target_pairs={{0,8},{8,0},{1,9},{9,1},{2,10},{10,2},{3,11},{11,3},{4,12},{12,4},... | collective-permute-start | bytes 7077896 | tf_op jit(solution)/shard_map/ppermute | solution.py:267
  89.2 1.3 %reduce_max.9 = f32[]{:T(128)} reduce(f32[8,128]{1,0:T(8,128)} %get-tuple-element.56, f32[]{:T(128)} %constant.27.clone.1), dimensions={0,1}, to_apply=%region_0.0 | reduce | flops 1023 | bytes 4104 | tf_op jit(solution)/shard_map/reduce_max | solution.py:312
  91.2 2.6 %collective-permute-done.15 = f32[384,1536]{1,0:T(8,128)} collective-permute-done((f32[384,1536]{1,0:T(8,128)}, f32[384,1536]{1,0:T(8,128)}, u32[]{:S(2)}, u32[]{:S(2)}) %collective-permute-start.15) | collective-permute-done | bytes 2359328 | tf_op jit(solution)/shard_map/ppermute | solution.py:267
  93.7 0.0 copy-done
  93.7 0.0 copy-done.1
  93.7 0.0 copy-done.2
  93.7 3.4 %conditional.1 = (f32[384,1536]{1,0:T(8,128)}) conditional(s32[]{:T(128)} %convert_element_type.28, (f32[384,1536]{1,0:T(8,128)S(1)}, f32[384,1536]{1,0:T(8,128)}) %tuple.13, (bf16[384,768]{1,0:T(8,128)(2,1)}, s32[48]{0:T(128)S(1)}, s32[48,48]{1,0:T(8,128)S(1)}, bf16[384,1536]{1,0:T(8,128)(2,1)}, s32[48,1536]{1,0:T(8,128)S(1)}) %tuple.25), branch_computations={%region_1.0_spmd, %region_2.0_spmd} | conditional | flops 7304832000 | bytes 168797408 | solution.py:311
  93.7 3.4 %add.8 = f32[384,1536]{1,0:T(8,128)} add(f32[384,1536]{1,0:T(8,128)S(1)} %get-tuple-element.22, f32[384,1536]{1,0:T(8,128)} %get-tuple-element.23) | non-fusion elementwise | flops 589824 | bytes 7077888 | tf_op jit(solution)/shard_map/cond/branch_0_fun/add | solution.py:314
Async XLA Ops:
  6.5 9.4 %collective-permute-start = (bf16[384,768]{1,0:T(8,128)(2,1)}, bf16[384,768]{1,0:T(8,128)(2,1)}, u32[]{:S(2)}, u32[]{:S(2)}) collective-permute-start(bf16[384,768]{1,0:T(8,128)(2,1)} %a_ref.1), channel_id=1, source_target_pairs={{0,8},{8,0},{1,9},{9,1},{2,10},{10,2},{3,11},{11,3},{4,12},{12,4},... | collective-permute-start | bytes 1769480 | tf_op jit(solution)/shard_map/ppermute | solution.py:267
  13.3 17.1 %collective-permute-start.1 = (bf16[128,2560]{1,0:T(8,128)(2,1)}, bf16[128,2560]{1,0:T(8,128)(2,1)}, u32[]{:S(2)}, u32[]{:S(2)}) collective-permute-start(bf16[128,2560]{1,0:T(8,128)(2,1)} %get-tuple-element.46.refs_6_.refs_8_), channel_id=1, source_target_pairs={{0,48},{16,0},{32,16},{48,32},{1,49},{17,1},{33,17},{49,33},{2,50}... | collective-permute-start | bytes 1966088 | tf_op jit(solution)/shard_map/ppermute | solution.py:267
  16.0 18.1 %collective-permute-start.2 = (bf16[128,2560]{1,0:T(8,128)(2,1)}, bf16[128,2560]{1,0:T(8,128)(2,1)}, u32[]{:S(2)}, u32[]{:S(2)}) collective-permute-start(bf16[128,2560]{1,0:T(8,128)(2,1)} %get-tuple-element.46.refs_6_.refs_8_), channel_id=1, source_target_pairs={{0,16},{16,32},{32,48},{48,0},{1,17},{17,33},{33,49},{49,1},{2,18}... | collective-permute-start | bytes 1966088 | tf_op jit(solution)/shard_map/ppermute | solution.py:267
  19.2 15.6 %collective-permute-start.3 = (bf16[776,384]{1,0:T(8,128)(2,1)}, bf16[776,384]{1,0:T(8,128)(2,1)}, u32[]{:S(2)}, u32[]{:S(2)}) collective-permute-start(bf16[776,384]{1,0:T(8,128)(2,1)} %join.1.refs_0_), channel_id=1, source_target_pairs={{0,3},{1,0},{2,1},{3,2},{4,7},{5,4},{6,5},{7,6},{8,11},{9,8},{10,9... | collective-permute-start | bytes 1787912 | tf_op jit(solution)/shard_map/ppermute | solution.py:267
  22.0 16.0 %collective-permute-start.4 = (bf16[776,384]{1,0:T(8,128)(2,1)}, bf16[776,384]{1,0:T(8,128)(2,1)}, u32[]{:S(2)}, u32[]{:S(2)}) collective-permute-start(bf16[776,384]{1,0:T(8,128)(2,1)} %join.1.refs_0_), channel_id=1, source_target_pairs={{0,1},{1,2},{2,3},{3,0},{4,5},{5,6},{6,7},{7,4},{8,9},{9,10},{10,1... | collective-permute-start | bytes 1787912 | tf_op jit(solution)/shard_map/ppermute | solution.py:267
  22.0 16.0 %collective-permute-start.5 = (bf16[776,384]{1,0:T(8,128)(2,1)}, bf16[776,384]{1,0:T(8,128)(2,1)S(1)}, u32[]{:S(2)}, u32[]{:S(2)}) collective-permute-start(bf16[776,384]{1,0:T(8,128)(2,1)} %join.1.refs_0_), channel_id=1, source_target_pairs={{0,4},{4,0},{1,5},{5,1},{2,6},{6,2},{3,7},{7,3},{8,12},{12,8},{9,1... | collective-permute-start | bytes 1787912 | tf_op jit(solution)/shard_map/ppermute | solution.py:267
  30.4 23.8 %collective-permute-start.11 = (bf16[128,2560]{1,0:T(8,128)(2,1)}, bf16[128,2560]{1,0:T(8,128)(2,1)}, u32[]{:S(2)}, u32[]{:S(2)}) collective-permute-start(bf16[128,2560]{1,0:T(8,128)(2,1)} %get-tuple-element.46.refs_6_.refs_8_), channel_id=1, source_target_pairs={{0,64},{64,0},{1,65},{65,1},{2,66},{66,2},{3,67},{67,3},{4,68},{68... | collective-permute-start | bytes 1966088 | tf_op jit(solution)/shard_map/ppermute | solution.py:267
  38.0 1.5 %copy-start.4 = (bf16[776,384]{1,0:T(8,128)(2,1)}, bf16[776,384]{1,0:T(8,128)(2,1)S(1)}, u32[]{:S(2)}) copy-start(bf16[776,384]{1,0:T(8,128)(2,1)S(1)} %collective-permute-done.5.refs_3_.refs_4_) | copy-start | bytes 1787908
  38.0 18.7 %collective-permute-start.10 = (bf16[128,2560]{1,0:T(8,128)(2,1)}, bf16[128,2560]{1,0:T(8,128)(2,1)}, u32[]{:S(2)}, u32[]{:S(2)}) collective-permute-start(bf16[128,2560]{1,0:T(8,128)(2,1)} %collective-permute-done.2.refs_9_.refs_11_), channel_id=1, source_target_pairs={{0,16},{16,32},{32,48},{48,0},{1,17},{17,33},{33,49},{49,1},{2,18}... | collective-permute-start | bytes 1966088 | tf_op jit(solution)/shard_map/ppermute | solution.py:267
  38.0 19.9 %collective-permute-start.7 = (bf16[776,384]{1,0:T(8,128)(2,1)S(1)}, bf16[776,384]{1,0:T(8,128)(2,1)}, u32[]{:S(2)}, u32[]{:S(2)}) collective-permute-start(bf16[776,384]{1,0:T(8,128)(2,1)S(1)} %collective-permute-done.5.refs_3_.refs_4_), channel_id=1, source_target_pairs={{0,3},{1,0},{2,1},{3,2},{4,7},{5,4},{6,5},{7,6},{8,11},{9,8},{10,9... | collective-permute-start | bytes 1787912 | tf_op jit(solution)/shard_map/ppermute | solution.py:267
  39.5 18.5 %collective-permute-start.9 = (bf16[776,384]{1,0:T(8,128)(2,1)S(1)}, bf16[776,384]{1,0:T(8,128)(2,1)S(1)}, u32[]{:S(2)}, u32[]{:S(2)}) collective-permute-start(bf16[776,384]{1,0:T(8,128)(2,1)S(1)} %collective-permute-done.5.refs_3_.refs_4_), channel_id=1, source_target_pairs={{0,1},{1,2},{2,3},{3,0},{4,5},{5,6},{6,7},{7,4},{8,9},{9,10},{10,1... | collective-permute-start | bytes 1787912 | tf_op jit(solution)/shard_map/ppermute | solution.py:267
  54.3 17.1 %collective-permute-start.12 = (bf16[128,2560]{1,0:T(8,128)(2,1)}, bf16[128,2560]{1,0:T(8,128)(2,1)}, u32[]{:S(2)}, u32[]{:S(2)}) collective-permute-start(bf16[128,2560]{1,0:T(8,128)(2,1)} %collective-permute-done.11.refs_10_.refs_11_.refs_12_.refs_13_), channel_id=1, source_target_pairs={{0,48},{16,0},{32,16},{48,32},{1,49},{17,1},{33,17},{49,33},{2,50}... | collective-permute-start | bytes 1966088 | tf_op jit(solution)/shard_map/ppermute | solution.py:267
  56.6 15.7 %collective-permute-start.14 = (bf16[128,2560]{1,0:T(8,128)(2,1)}, bf16[128,2560]{1,0:T(8,128)(2,1)}, u32[]{:S(2)}, u32[]{:S(2)}) collective-permute-start(bf16[128,2560]{1,0:T(8,128)(2,1)} %collective-permute-done.11.refs_10_.refs_11_.refs_12_.refs_13_), channel_id=1, source_target_pairs={{0,16},{16,32},{32,48},{48,0},{1,17},{17,33},{33,49},{49,1},{2,18}... | collective-permute-start | bytes 1966088 | tf_op jit(solution)/shard_map/ppermute | solution.py:267
  56.6 16.0 %collective-permute-start.13 = (bf16[128,2560]{1,0:T(8,128)(2,1)}, bf16[128,2560]{1,0:T(8,128)(2,1)}, u32[]{:S(2)}, u32[]{:S(2)}) collective-permute-start(bf16[128,2560]{1,0:T(8,128)(2,1)} %collective-permute-done.10.refs_8_.refs_10_), channel_id=1, source_target_pairs={{0,64},{64,0},{1,65},{65,1},{2,66},{66,2},{3,67},{67,3},{4,68},{68... | collective-permute-start | bytes 1966088 | tf_op jit(solution)/shard_map/ppermute | solution.py:267
  57.9 14.5 %collective-permute-start.6 = (bf16[776,384]{1,0:T(8,128)(2,1)}, bf16[776,384]{1,0:T(8,128)(2,1)}, u32[]{:S(2)}, u32[]{:S(2)}) collective-permute-start(bf16[776,384]{1,0:T(8,128)(2,1)} %collective-permute-done.4.refs_2_.refs_3_), channel_id=1, source_target_pairs={{0,1},{1,2},{2,3},{3,0},{4,5},{5,6},{6,7},{7,4},{8,9},{9,10},{10,1... | collective-permute-start | bytes 1787912 | tf_op jit(solution)/shard_map/ppermute | solution.py:267
  57.9 0.8 copy-start.5
  58.8 13.6 %collective-permute-start.8 = (bf16[776,384]{1,0:T(8,128)(2,1)}, bf16[776,384]{1,0:T(8,128)(2,1)}, u32[]{:S(2)}, u32[]{:S(2)}) collective-permute-start(bf16[776,384]{1,0:T(8,128)(2,1)} %collective-permute-done.7.refs_4_.refs_5_), channel_id=1, source_target_pairs={{0,3},{1,0},{2,1},{3,2},{4,7},{5,4},{6,5},{7,6},{8,11},{9,8},{10,9... | collective-permute-start | bytes 1787912 | tf_op jit(solution)/shard_map/ppermute | solution.py:267
  72.7 21.1 %copy-start = (s32[48,1536]{1,0:T(8,128)S(1)}, s32[48,1536]{1,0:T(8,128)}, u32[]{:S(2)}) copy-start(s32[48,1536]{1,0:T(8,128)} %d_ref.1) | copy-start | bytes 884740
  72.7 21.1 %copy-start.1 = (s32[48,48]{1,0:T(8,128)S(1)}, s32[48,48]{1,0:T(8,128)}, u32[]{:S(2)}) copy-start(s32[48,48]{1,0:T(8,128)} %pattern.1) | copy-start | bytes 27652
  72.7 21.1 %copy-start.2 = (s32[48]{0:T(128)S(1)}, s32[48]{0:T(128)}, u32[]{:S(2)}) copy-start(s32[48]{0:T(128)} %order.3) | copy-start | bytes 580
  86.2 7.5 %collective-permute-start.15 = (f32[384,1536]{1,0:T(8,128)}, f32[384,1536]{1,0:T(8,128)}, u32[]{:S(2)}, u32[]{:S(2)}) collective-permute-start(f32[384,1536]{1,0:T(8,128)} %get-tuple-element.58), channel_id=1, source_target_pairs={{0,8},{8,0},{1,9},{9,1},{2,10},{10,2},{3,11},{11,3},{4,12},{12,4},... | collective-permute-start | bytes 7077896 | tf_op jit(solution)/shard_map/ppermute | solution.py:267

commit v5 on v4

--- a/solution.py
+++ b/solution.py
@@ -60,12 +60,8 @@
     )(tile_order, tile_pattern, over, integrals, recv)
 
 
-def pack_kernel(
-    tall, slots, order, d_ref, b_ref, pos_ref, start_ref, u_ref, over_ref, dom, total, start, sem
-):
+def number(tall, dom, pos_ref, start_ref, started=None):
     tiles, pairs = dom.shape
-    for s in range(tiles):
-        dom[pl.ds(s, 1), :] = d_ref[pl.ds(order[s], 1), :]
     live = dom[...].astype(F32).astype(BF16)
     blocks = pairs // TILE
     spread = (iota((pairs, TILE), 0) // TILE == iota((pairs, TILE), 1)).astype(F32).astype(BF16)
@@ -78,24 +74,60 @@
     ahead = jnp.sum(jnp.dot(before, counted, preferred_element_type=F32), axis=1, keepdims=True)
     starts = jnp.dot(counted, below, preferred_element_type=F32) + ahead
     start_ref[...] = starts.astype(I32)
-    copy = pltpu.make_async_copy(start_ref, start, sem)
-    copy.start()
+    if started is not None:
+        started.start()
     for b in range(blocks):
         lanes = pl.ds(b * TILE, TILE)
         here = live[:, b * TILE : (b + 1) * TILE]
         slot = jnp.dot(here, upto, preferred_element_type=F32) + (starts[:, b : b + 1] - 1.0)
         pos_ref[:, lanes] = jnp.where(dom[:, lanes] > 0, slot.astype(I32), -1)
-    most = jnp.max(ahead + jnp.sum(counts, axis=1, keepdims=True), axis=0, keepdims=True)
+
+
+def plan_kernel(tall, order, d_ref, pos_ref, start_ref, dom):
+    for s in range(dom.shape[0]):
+        dom[pl.ds(s, 1), :] = d_ref[pl.ds(order[s], 1), :]
+    number(tall, dom, pos_ref, start_ref)
+
+
+def plan(pair_domain, tile_order, tall):
+    tiles, pairs = pair_domain.shape
+    return pl.pallas_call(
+        functools.partial(plan_kernel, tall),
+        grid_spec=pltpu.PrefetchScalarGridSpec(
+            num_scalar_prefetch=1,
+            grid=(),
+            in_specs=whole(1),
+            out_specs=whole(2),
+            scratch_shapes=[pltpu.VMEM((tiles, pairs), I32)],
+        ),
+        out_shape=[jax.ShapeDtypeStruct((tiles, pairs), I32), jax.ShapeDtypeStruct((tiles, TILE), I32)],
+        compiler_params=pltpu.CompilerParams(vmem_limit_bytes=VMEM_LIMIT),
+        cost_estimate=pl.CostEstimate(flops=0, bytes_accessed=4_000_000, transcendentals=0),
+        name="plan",
+    )(tile_order, pair_domain)
+
+
+def pack_kernel(tall, slots, order, d_ref, b_ref, u_ref, over_ref, dom, pos, held, total, start, sem):
+    tiles, pairs = d_ref.shape
+    row = where_am_i()[0]
+    dom[...] = jnp.zeros_like(dom)
+    for i in range(tall):
+        dom[pl.ds(i, 1), :] = d_ref[pl.ds(order[row * tall + i], 1), :]
+    copy = pltpu.make_async_copy(held, start, sem)
+    number(tall, dom, pos, held, copy)
+    most = jnp.zeros((1, 1), I32)
+    for s in range(0, tiles, tall):
+        line = sum(d_ref[pl.ds(order[s + i], 1), :] for i in range(tall))
+        most = jnp.maximum(most, jnp.sum(line, axis=1, keepdims=True))
     flag = jnp.where(most > slots, 1.0, 0.0).astype(F32)
     over_ref[...] = jnp.broadcast_to(flag, over_ref.shape).astype(BF16)
     total[...] = jnp.zeros_like(total)
     copy.wait()
     for i in range(tall):
-        s = where_am_i()[0] * tall + i
-        slot = pos_ref[pl.ds(s, 1), :]
-        for b in range(blocks):
+        slot = pos[pl.ds(i, 1), :]
+        for b in range(pairs // TILE):
             lanes = pl.ds(b * TILE, TILE)
-            at = jnp.minimum(start[s, b] // TILE * TILE, slots)
+            at = jnp.minimum(start[i, b] // TILE * TILE, slots)
             at = pl.multiple_of(at, TILE)
             pick = (iota((2 * TILE, TILE), 0) + at == slot[:, b * TILE : (b + 1) * TILE]).astype(F32).astype(BF16)
             moved = lax.dot_general(
@@ -113,20 +145,17 @@
             num_scalar_prefetch=1,
             grid=(),
             in_specs=whole(2),
-            out_specs=whole(4),
+            out_specs=whole(2),
             scratch_shapes=[
-                pltpu.VMEM((tiles, pairs), I32),
+                pltpu.VMEM((8, pairs), I32),
+                pltpu.VMEM((8, pairs), I32),
+                pltpu.VMEM((8, TILE), I32),
                 pltpu.VMEM((TILE, slots + 2 * TILE), F32),
-                pltpu.SMEM((tiles, TILE), I32),
+                pltpu.SMEM((8, TILE), I32),
                 pltpu.SemaphoreType.DMA(()),
             ],
         ),
-        out_shape=[
-            jax.ShapeDtypeStruct((tiles, pairs), I32),
-            jax.ShapeDtypeStruct((tiles, TILE), I32),
-            jax.ShapeDtypeStruct((TILE, slots), BF16),
-            jax.ShapeDtypeStruct((FLAG_ROWS, cols), BF16),
-        ],
+        out_shape=[jax.ShapeDtypeStruct((TILE, slots), BF16), jax.ShapeDtypeStruct((FLAG_ROWS, cols), BF16)],
         compiler_params=pltpu.CompilerParams(vmem_limit_bytes=VMEM_LIMIT),
         name="pack",
     )(tile_order, pair_domain, amplitudes)
@@ -290,12 +319,14 @@
     tall = amplitudes.shape[0] // TILE
     slots = amplitudes.shape[1] * tall * 5 // 9 // TILE * TILE
     recv = shift(integrals, "core", 1)
-    pos, start, u, over = pack(pair_domain, amplitudes, tile_order, tall, slots, integrals.shape[1] // 2)
+    u, over = pack(pair_domain, amplitudes, tile_order, tall, slots, integrals.shape[1] // 2)
     mine = join(integrals, recv, over, tile_pattern, tile_order, tall)
 
     up, um = shift(u, "x", -1), shift(u, "x", 1)
     ap, am, there = shift(mine, "y", -1), shift(mine, "y", 1), shift(mine, "zl", 1)
-    up, um, ap, am, there = together(up, um, ap, am, there)
+    late_domain, _ = together(pair_domain, mine)
+    pos, start = plan(late_domain, tile_order, tall)
+    up, um, ap, am, there, pos, start = together(up, um, ap, am, there, pos, start)
     u2, q = shift(um, "x", 1), shift(u, "zh", 1)
     tp, tm = shift(there, "y", -1), shift(there, "y", 1)
     qp, qm, q2 = shift(q, "x", -1), shift(q, "x", 1), shift(u2, "zh", 1)

time: 104 us -> 104 us (level)
  Pallas kernels: 32.1 us -> 34.7 us
  waiting for transfers between devices: 29.4 us -> 27.1 us
    pallas_call x0 -> x1, Pallas kernels: none -> 3.06 us  [plan(): pl.pallas_call(functools.partial(plan_kernel, tall), grid_spec=pltpu.Pref...]
    ppermute x16, waiting for transfers between devices: 29.4 us -> 27.1 us  [shift(): return lax.ppermute(value, axis, [(i, (i + by) % n) for i in range(n)])]
  transfers between devices with their start and end apart: 16 -> 16, of which waited for: 7 -> 7; matrix products, arithmetic and copies ran while one was open for 1% -> 1% of each run, Pallas kernels for 18% -> 20%
where the time goes in v5:
time: 104 us
  Pallas kernels  34.7 us (33%)
  waiting for transfers between devices  27.1 us (26%)
  starting transfers between devices  22.9 us (22%)
  between operations  14.1 us (14%)
  other arithmetic  4.72 us (5%)
    ppermute x16, waiting for transfers between devices, shift(): return lax.ppermute(value, axis, [(i, (i + by) % n) for i in range(n)])  27.1 us
    pallas_call x2, Pallas kernels, product(): pl.pallas_call(functools.partial(product_kernel, tall, picks, hops, first...  23.4 us
    ppermute x16, starting transfers between devices, shift(): return lax.ppermute(value, axis, [(i, (i + by) % n) for i in range(n)])  22.9 us
    pallas_call x1, Pallas kernels, pack(): pl.pallas_call(functools.partial(pack_kernel, tall, slots), grid_spec=plt...  4.94 us
    add x1, other arithmetic, on_device(): args[5] + args[6]  3.45 us
    pallas_call x1, Pallas kernels, join(): pl.pallas_call(functools.partial(join_kernel, tall), grid_spec=pltpu.Pref...  3.29 us
    pallas_call x1, Pallas kernels, plan(): pl.pallas_call(functools.partial(plan_kernel, tall), grid_spec=pltpu.Pref...  3.06 us
  transfers between devices with their start and end apart: 16, of which 7 were waited for; matrix products, arithmetic and copies ran while one was open for 1% of the time, Pallas kernels for 20%

profile of v5, /device:TPU:1, one launch (start us, length us, event | category | flops | bytes accessed | tf_op | source)
XLA Modules:
  0.0 103.6 jit_solution(984261441781920877)
XLA Ops:
  6.5 1.4 %collective-permute-start.2 = (bf16[384,768]{1,0:T(8,128)(2,1)}, bf16[384,768]{1,0:T(8,128)(2,1)}, u32[]{:S(2)}, u32[]{:S(2)}) collective-permute-start(bf16[384,768]{1,0:T(8,128)(2,1)} %a_ref.1), channel_id=1, source_target_pairs={{0,8},{8,0},{1,9},{9,1},{2,10},{10,2},{3,11},{11,3},{4,12},{12,4},... | collective-permute-start | bytes 1769480 | tf_op jit(solution)/shard_map/ppermute | solution.py:296
  8.0 4.9 %pack.1 = (bf16[128,2560]{1,0:T(8,128)(2,1)}, bf16[8,384]{1,0:T(8,128)(2,1)}) custom-call(s32[48]{0:T(128)} %order.5, s32[48,1536]{1,0:T(8,128)} %d_ref.2, bf16[384,1536]{1,0:T(8,128)(2,1)} %b_ref.1), custom_call_target="tpu_custom_call" | custom-call | tf_op jit(solution)/shard_map/pack/pallas_call | solution.py:142
  12.9 2.6 %collective-permute-start = (bf16[128,2560]{1,0:T(8,128)(2,1)}, bf16[128,2560]{1,0:T(8,128)(2,1)}, u32[]{:S(2)}, u32[]{:S(2)}) collective-permute-start(bf16[128,2560]{1,0:T(8,128)(2,1)} %get-tuple-element.47.refs_6_.refs_8_), channel_id=1, source_target_pairs={{0,48},{16,0},{32,16},{48,32},{1,49},{17,1},{33,17},{49,33},{2,50}... | collective-permute-start | bytes 1966088 | tf_op jit(solution)/shard_map/ppermute | solution.py:296
  15.5 0.0 collective-permute-start.1
  15.5 0.0 collective-permute-done.2.recv_ref
  15.5 3.3 %join.1.refs_0_ = bf16[776,384]{1,0:T(8,128)(2,1)} custom-call(s32[48]{0:T(128)} %order.5, s32[48,48]{1,0:T(8,128)} %pattern.1, bf16[8,384]{1,0:T(8,128)(2,1)} %get-tuple-element.48.over_ref, bf16[384,768]{1,0:T(8,128)(2,1)} %a_ref.1, bf16[384,768]{1,0:T(8,128)(2,1)} %collective-permute-done.2.recv_ref), custom_call_target="tpu_custom_call" | custom-call | tf_op jit(solution)/shard_map/join/pallas_call | solution.py:52
  18.8 2.7 %collective-permute-start.3 = (bf16[776,384]{1,0:T(8,128)(2,1)}, bf16[776,384]{1,0:T(8,128)(2,1)}, u32[]{:S(2)}, u32[]{:S(2)}) collective-permute-start(bf16[776,384]{1,0:T(8,128)(2,1)} %join.1.refs_0_), channel_id=1, source_target_pairs={{0,3},{1,0},{2,1},{3,2},{4,7},{5,4},{6,5},{7,6},{8,11},{9,8},{10,9... | collective-permute-start | bytes 1787912 | tf_op jit(solution)/shard_map/ppermute | solution.py:296
  21.6 0.0 collective-permute-start.4
  21.6 1.6 %collective-permute-start.5 = (bf16[776,384]{1,0:T(8,128)(2,1)}, bf16[776,384]{1,0:T(8,128)(2,1)}, u32[]{:S(2)}, u32[]{:S(2)}) collective-permute-start(bf16[776,384]{1,0:T(8,128)(2,1)} %join.1.refs_0_), channel_id=1, source_target_pairs={{0,4},{4,0},{1,5},{5,1},{2,6},{6,2},{3,7},{7,3},{8,12},{12,8},{9,1... | collective-permute-start | bytes 1787912 | tf_op jit(solution)/shard_map/ppermute | solution.py:296
  23.2 3.1 %plan.1 = (s32[48,1536]{1,0:T(8,128)}, s32[48,128]{1,0:T(8,128)}) custom-call(s32[48]{0:T(128)} %order.5, s32[48,1536]{1,0:T(8,128)} %d_ref.2), custom_call_target="tpu_custom_call" | custom-call | bytes 4000000 | tf_op jit(solution)/shard_map/plan/pallas_call | solution.py:94
  26.3 3.7 %collective-permute-done.refs_7_.refs_9_ = bf16[128,2560]{1,0:T(8,128)(2,1)} collective-permute-done((bf16[128,2560]{1,0:T(8,128)(2,1)}, bf16[128,2560]{1,0:T(8,128)(2,1)}, u32[]{:S(2)}, u32[]{:S(2)}) %collective-permute-start) | collective-permute-done | bytes 655392 | tf_op jit(solution)/shard_map/ppermute | solution.py:296
  30.0 3.6 %collective-permute-start.11 = (bf16[128,2560]{1,0:T(8,128)(2,1)}, bf16[128,2560]{1,0:T(8,128)(2,1)}, u32[]{:S(2)}, u32[]{:S(2)}) collective-permute-start(bf16[128,2560]{1,0:T(8,128)(2,1)} %get-tuple-element.47.refs_6_.refs_8_), channel_id=1, source_target_pairs={{0,64},{64,0},{1,65},{65,1},{2,66},{66,2},{3,67},{67,3},{4,68},{68... | collective-permute-start | bytes 1966088 | tf_op jit(solution)/shard_map/ppermute | solution.py:296
  33.6 0.0 collective-permute-done.1.refs_9_.refs_11_
  33.6 0.9 collective-permute-done.3.refs_1_
  34.5 3.1 %collective-permute-done.4.refs_2_.refs_3_ = bf16[776,384]{1,0:T(8,128)(2,1)} collective-permute-done((bf16[776,384]{1,0:T(8,128)(2,1)}, bf16[776,384]{1,0:T(8,128)(2,1)}, u32[]{:S(2)}, u32[]{:S(2)}) %collective-permute-start.4) | collective-permute-done | bytes 596000 | tf_op jit(solution)/shard_map/ppermute | solution.py:296
  37.6 0.0 collective-permute-done.5.refs_3_.refs_4_
  37.6 0.0 collective-permute-start.10
  37.6 1.6 %collective-permute-start.7 = (bf16[776,384]{1,0:T(8,128)(2,1)}, bf16[776,384]{1,0:T(8,128)(2,1)}, u32[]{:S(2)}, u32[]{:S(2)}) collective-permute-start(bf16[776,384]{1,0:T(8,128)(2,1)} %collective-permute-done.5.refs_3_.refs_4_), channel_id=1, source_target_pairs={{0,3},{1,0},{2,1},{3,2},{4,7},{5,4},{6,5},{7,6},{8,11},{9,8},{10,9... | collective-permute-start | bytes 1787912 | tf_op jit(solution)/shard_map/ppermute | solution.py:296
  39.1 0.0 collective-permute-start.9
  39.1 14.7 %collective-permute-done.11.refs_10_.refs_11_.refs_12_.refs_13_ = bf16[128,2560]{1,0:T(8,128)(2,1)} collective-permute-done((bf16[128,2560]{1,0:T(8,128)(2,1)}, bf16[128,2560]{1,0:T(8,128)(2,1)}, u32[]{:S(2)}, u32[]{:S(2)}) %collective-permute-start.11) | collective-permute-done | bytes 655392 | tf_op jit(solution)/shard_map/ppermute | solution.py:296
  53.9 2.4 %collective-permute-start.12 = (bf16[128,2560]{1,0:T(8,128)(2,1)}, bf16[128,2560]{1,0:T(8,128)(2,1)}, u32[]{:S(2)}, u32[]{:S(2)}) collective-permute-start(bf16[128,2560]{1,0:T(8,128)(2,1)} %collective-permute-done.11.refs_10_.refs_11_.refs_12_.refs_13_), channel_id=1, source_target_pairs={{0,48},{16,0},{32,16},{48,32},{1,49},{17,1},{33,17},{49,33},{2,50}... | collective-permute-start | bytes 1966088 | tf_op jit(solution)/shard_map/ppermute | solution.py:296
  56.2 0.0 collective-permute-start.14
  56.2 0.0 collective-permute-done.10.refs_8_.refs_10_
  56.2 1.3 %collective-permute-start.13 = (bf16[128,2560]{1,0:T(8,128)(2,1)}, bf16[128,2560]{1,0:T(8,128)(2,1)}, u32[]{:S(2)}, u32[]{:S(2)}) collective-permute-start(bf16[128,2560]{1,0:T(8,128)(2,1)} %collective-permute-done.10.refs_8_.refs_10_), channel_id=1, source_target_pairs={{0,64},{64,0},{1,65},{65,1},{2,66},{66,2},{3,67},{67,3},{4,68},{68... | collective-permute-start | bytes 1966088 | tf_op jit(solution)/shard_map/ppermute | solution.py:296
  57.5 0.0 collective-permute-done.7.refs_4_.refs_5_
  57.5 0.0 collective-permute-start.6
  57.5 0.0 collective-permute-done.9.refs_5_.refs_7_
  57.5 2.7 %collective-permute-start.8 = (bf16[776,384]{1,0:T(8,128)(2,1)}, bf16[776,384]{1,0:T(8,128)(2,1)}, u32[]{:S(2)}, u32[]{:S(2)}) collective-permute-start(bf16[776,384]{1,0:T(8,128)(2,1)} %collective-permute-done.7.refs_4_.refs_5_), channel_id=1, source_target_pairs={{0,3},{1,0},{2,1},{3,2},{4,7},{5,4},{6,5},{7,6},{8,11},{9,8},{10,9... | collective-permute-start | bytes 1787912 | tf_op jit(solution)/shard_map/ppermute | solution.py:296
  60.2 9.9 %product.2 = (f32[384,1536]{1,0:T(8,128)}, f32[384,1536]{1,0:T(8,128)}, f32[8,128]{1,0:T(8,128)}) custom-call(s32[48,128]{1,0:T(8,128)} %get-tuple-element.52.start_ref, bf16[776,384]{1,0:T(8,128)(2,1)} %join.1.refs_0_, bf16[776,384]{1,0:T(8,128)(2,1)} %collective-permute-done.3.refs_1_, bf16[776,384]{1,0:T(8,128)(2,1)} %collective-permute-done.4.refs_2_.refs_3_, ...), custom_call_target="tpu_custom_call" | custom-call | flops 2717908992 | bytes 10045440 | tf_op jit(solution)/shard_map/product/pallas_call | solution.py:265
  70.1 0.0 collective-permute-done.12.refs_13_
  70.1 1.8 %collective-permute-done.14.refs_15_ = bf16[128,2560]{1,0:T(8,128)(2,1)} collective-permute-done((bf16[128,2560]{1,0:T(8,128)(2,1)}, bf16[128,2560]{1,0:T(8,128)(2,1)}, u32[]{:S(2)}, u32[]{:S(2)}) %collective-permute-start.14) | collective-permute-done | bytes 655392 | tf_op jit(solution)/shard_map/ppermute | solution.py:296
  71.9 0.0 collective-permute-done.6.refs_2_
  71.9 0.0 collective-permute-done.8.refs_6_
  71.9 0.3 collective-permute-done.13.refs_14_
  72.2 0.0 copy-start
  72.2 0.0 copy-start.1
  72.2 0.0 copy-start.2
  72.2 13.5 %product.3 = (f32[384,1536]{1,0:T(8,128)}, f32[384,1536]{1,0:T(8,128)S(1)}, f32[8,128]{1,0:T(8,128)}) custom-call(s32[48,128]{1,0:T(8,128)} %get-tuple-element.52.start_ref, bf16[776,384]{1,0:T(8,128)(2,1)} %join.1.refs_0_, bf16[776,384]{1,0:T(8,128)(2,1)} %collective-permute-done.3.refs_1_, bf16[776,384]{1,0:T(8,128)(2,1)} %collective-permute-done.6.refs_2_, ...), custom_call_target="tpu_custom_call" | custom-call | flops 4529848320 | bytes 13596672 | tf_op jit(solution)/shard_map/product/pallas_call | solution.py:265
  85.8 3.0 %collective-permute-start.15 = (f32[384,1536]{1,0:T(8,128)}, f32[384,1536]{1,0:T(8,128)}, u32[]{:S(2)}, u32[]{:S(2)}) collective-permute-start(f32[384,1536]{1,0:T(8,128)} %get-tuple-element.64), channel_id=1, source_target_pairs={{0,8},{8,0},{1,9},{9,1},{2,10},{10,2},{3,11},{11,3},{4,12},{12,4},... | collective-permute-start | bytes 7077896 | tf_op jit(solution)/shard_map/ppermute | solution.py:296
  88.8 1.3 %reduce_max.9 = f32[]{:T(128)} reduce(f32[8,128]{1,0:T(8,128)} %get-tuple-element.62, f32[]{:T(128)} %constant.27.clone.1), dimensions={0,1}, to_apply=%region_0.0 | reduce | flops 1023 | bytes 4104 | tf_op jit(solution)/shard_map/reduce_max | solution.py:343
  90.7 2.6 %collective-permute-done.15 = f32[384,1536]{1,0:T(8,128)} collective-permute-done((f32[384,1536]{1,0:T(8,128)}, f32[384,1536]{1,0:T(8,128)}, u32[]{:S(2)}, u32[]{:S(2)}) %collective-permute-start.15) | collective-permute-done | bytes 2359328 | tf_op jit(solution)/shard_map/ppermute | solution.py:296
  93.3 0.0 copy-done
  93.3 0.0 copy-done.1
  93.3 0.0 copy-done.2
  93.3 3.4 %conditional.1 = (f32[384,1536]{1,0:T(8,128)}) conditional(s32[]{:T(128)} %convert_element_type.28, (f32[384,1536]{1,0:T(8,128)S(1)}, f32[384,1536]{1,0:T(8,128)}) %tuple.15, (bf16[384,768]{1,0:T(8,128)(2,1)}, s32[48]{0:T(128)S(1)}, s32[48,48]{1,0:T(8,128)S(1)}, bf16[384,1536]{1,0:T(8,128)(2,1)}, s32[48,1536]{1,0:T(8,128)S(1)}) %tuple.27), branch_computations={%region_1.0_spmd, %region_2.0_spmd} | conditional | flops 7304832000 | bytes 168797408 | solution.py:342
  93.3 3.4 %add.8 = f32[384,1536]{1,0:T(8,128)} add(f32[384,1536]{1,0:T(8,128)S(1)} %get-tuple-element.22, f32[384,1536]{1,0:T(8,128)} %get-tuple-element.23) | non-fusion elementwise | flops 589824 | bytes 7077888 | tf_op jit(solution)/shard_map/cond/branch_0_fun/add | solution.py:345
Async XLA Ops:
  6.5 9.0 %collective-permute-start.2 = (bf16[384,768]{1,0:T(8,128)(2,1)}, bf16[384,768]{1,0:T(8,128)(2,1)}, u32[]{:S(2)}, u32[]{:S(2)}) collective-permute-start(bf16[384,768]{1,0:T(8,128)(2,1)} %a_ref.1), channel_id=1, source_target_pairs={{0,8},{8,0},{1,9},{9,1},{2,10},{10,2},{3,11},{11,3},{4,12},{12,4},... | collective-permute-start | bytes 1769480 | tf_op jit(solution)/shard_map/ppermute | solution.py:296
  12.9 17.1 %collective-permute-start = (bf16[128,2560]{1,0:T(8,128)(2,1)}, bf16[128,2560]{1,0:T(8,128)(2,1)}, u32[]{:S(2)}, u32[]{:S(2)}) collective-permute-start(bf16[128,2560]{1,0:T(8,128)(2,1)} %get-tuple-element.47.refs_6_.refs_8_), channel_id=1, source_target_pairs={{0,48},{16,0},{32,16},{48,32},{1,49},{17,1},{33,17},{49,33},{2,50}... | collective-permute-start | bytes 1966088 | tf_op jit(solution)/shard_map/ppermute | solution.py:296
  15.5 18.1 %collective-permute-start.1 = (bf16[128,2560]{1,0:T(8,128)(2,1)}, bf16[128,2560]{1,0:T(8,128)(2,1)}, u32[]{:S(2)}, u32[]{:S(2)}) collective-permute-start(bf16[128,2560]{1,0:T(8,128)(2,1)} %get-tuple-element.47.refs_6_.refs_8_), channel_id=1, source_target_pairs={{0,16},{16,32},{32,48},{48,0},{1,17},{17,33},{33,49},{49,1},{2,18}... | collective-permute-start | bytes 1966088 | tf_op jit(solution)/shard_map/ppermute | solution.py:296
  18.8 15.6 %collective-permute-start.3 = (bf16[776,384]{1,0:T(8,128)(2,1)}, bf16[776,384]{1,0:T(8,128)(2,1)}, u32[]{:S(2)}, u32[]{:S(2)}) collective-permute-start(bf16[776,384]{1,0:T(8,128)(2,1)} %join.1.refs_0_), channel_id=1, source_target_pairs={{0,3},{1,0},{2,1},{3,2},{4,7},{5,4},{6,5},{7,6},{8,11},{9,8},{10,9... | collective-permute-start | bytes 1787912 | tf_op jit(solution)/shard_map/ppermute | solution.py:296
  21.6 16.0 %collective-permute-start.4 = (bf16[776,384]{1,0:T(8,128)(2,1)}, bf16[776,384]{1,0:T(8,128)(2,1)}, u32[]{:S(2)}, u32[]{:S(2)}) collective-permute-start(bf16[776,384]{1,0:T(8,128)(2,1)} %join.1.refs_0_), channel_id=1, source_target_pairs={{0,1},{1,2},{2,3},{3,0},{4,5},{5,6},{6,7},{7,4},{8,9},{9,10},{10,1... | collective-permute-start | bytes 1787912 | tf_op jit(solution)/shard_map/ppermute | solution.py:296
  21.6 16.0 %collective-permute-start.5 = (bf16[776,384]{1,0:T(8,128)(2,1)}, bf16[776,384]{1,0:T(8,128)(2,1)}, u32[]{:S(2)}, u32[]{:S(2)}) collective-permute-start(bf16[776,384]{1,0:T(8,128)(2,1)} %join.1.refs_0_), channel_id=1, source_target_pairs={{0,4},{4,0},{1,5},{5,1},{2,6},{6,2},{3,7},{7,3},{8,12},{12,8},{9,1... | collective-permute-start | bytes 1787912 | tf_op jit(solution)/shard_map/ppermute | solution.py:296
  30.0 23.8 %collective-permute-start.11 = (bf16[128,2560]{1,0:T(8,128)(2,1)}, bf16[128,2560]{1,0:T(8,128)(2,1)}, u32[]{:S(2)}, u32[]{:S(2)}) collective-permute-start(bf16[128,2560]{1,0:T(8,128)(2,1)} %get-tuple-element.47.refs_6_.refs_8_), channel_id=1, source_target_pairs={{0,64},{64,0},{1,65},{65,1},{2,66},{66,2},{3,67},{67,3},{4,68},{68... | collective-permute-start | bytes 1966088 | tf_op jit(solution)/shard_map/ppermute | solution.py:296
  37.6 18.7 %collective-permute-start.10 = (bf16[128,2560]{1,0:T(8,128)(2,1)}, bf16[128,2560]{1,0:T(8,128)(2,1)}, u32[]{:S(2)}, u32[]{:S(2)}) collective-permute-start(bf16[128,2560]{1,0:T(8,128)(2,1)} %collective-permute-done.1.refs_9_.refs_11_), channel_id=1, source_target_pairs={{0,16},{16,32},{32,48},{48,0},{1,17},{17,33},{33,49},{49,1},{2,18}... | collective-permute-start | bytes 1966088 | tf_op jit(solution)/shard_map/ppermute | solution.py:296
  37.6 19.9 %collective-permute-start.7 = (bf16[776,384]{1,0:T(8,128)(2,1)}, bf16[776,384]{1,0:T(8,128)(2,1)}, u32[]{:S(2)}, u32[]{:S(2)}) collective-permute-start(bf16[776,384]{1,0:T(8,128)(2,1)} %collective-permute-done.5.refs_3_.refs_4_), channel_id=1, source_target_pairs={{0,3},{1,0},{2,1},{3,2},{4,7},{5,4},{6,5},{7,6},{8,11},{9,8},{10,9... | collective-permute-start | bytes 1787912 | tf_op jit(solution)/shard_map/ppermute | solution.py:296
  39.1 18.4 %collective-permute-start.9 = (bf16[776,384]{1,0:T(8,128)(2,1)}, bf16[776,384]{1,0:T(8,128)(2,1)}, u32[]{:S(2)}, u32[]{:S(2)}) collective-permute-start(bf16[776,384]{1,0:T(8,128)(2,1)} %collective-permute-done.5.refs_3_.refs_4_), channel_id=1, source_target_pairs={{0,1},{1,2},{2,3},{3,0},{4,5},{5,6},{6,7},{7,4},{8,9},{9,10},{10,1... | collective-permute-start | bytes 1787912 | tf_op jit(solution)/shard_map/ppermute | solution.py:296
  53.9 16.3 %collective-permute-start.12 = (bf16[128,2560]{1,0:T(8,128)(2,1)}, bf16[128,2560]{1,0:T(8,128)(2,1)}, u32[]{:S(2)}, u32[]{:S(2)}) collective-permute-start(bf16[128,2560]{1,0:T(8,128)(2,1)} %collective-permute-done.11.refs_10_.refs_11_.refs_12_.refs_13_), channel_id=1, source_target_pairs={{0,48},{16,0},{32,16},{48,32},{1,49},{17,1},{33,17},{49,33},{2,50}... | collective-permute-start | bytes 1966088 | tf_op jit(solution)/shard_map/ppermute | solution.py:296
  56.2 15.7 %collective-permute-start.14 = (bf16[128,2560]{1,0:T(8,128)(2,1)}, bf16[128,2560]{1,0:T(8,128)(2,1)}, u32[]{:S(2)}, u32[]{:S(2)}) collective-permute-start(bf16[128,2560]{1,0:T(8,128)(2,1)} %collective-permute-done.11.refs_10_.refs_11_.refs_12_.refs_13_), channel_id=1, source_target_pairs={{0,16},{16,32},{32,48},{48,0},{1,17},{17,33},{33,49},{49,1},{2,18}... | collective-permute-start | bytes 1966088 | tf_op jit(solution)/shard_map/ppermute | solution.py:296
  56.2 16.0 %collective-permute-start.13 = (bf16[128,2560]{1,0:T(8,128)(2,1)}, bf16[128,2560]{1,0:T(8,128)(2,1)}, u32[]{:S(2)}, u32[]{:S(2)}) collective-permute-start(bf16[128,2560]{1,0:T(8,128)(2,1)} %collective-permute-done.10.refs_8_.refs_10_), channel_id=1, source_target_pairs={{0,64},{64,0},{1,65},{65,1},{2,66},{66,2},{3,67},{67,3},{4,68},{68... | collective-permute-start | bytes 1966088 | tf_op jit(solution)/shard_map/ppermute | solution.py:296
  57.5 14.5 %collective-permute-start.6 = (bf16[776,384]{1,0:T(8,128)(2,1)}, bf16[776,384]{1,0:T(8,128)(2,1)}, u32[]{:S(2)}, u32[]{:S(2)}) collective-permute-start(bf16[776,384]{1,0:T(8,128)(2,1)} %collective-permute-done.4.refs_2_.refs_3_), channel_id=1, source_target_pairs={{0,1},{1,2},{2,3},{3,0},{4,5},{5,6},{6,7},{7,4},{8,9},{9,10},{10,1... | collective-permute-start | bytes 1787912 | tf_op jit(solution)/shard_map/ppermute | solution.py:296
  57.5 14.5 %collective-permute-start.8 = (bf16[776,384]{1,0:T(8,128)(2,1)}, bf16[776,384]{1,0:T(8,128)(2,1)}, u32[]{:S(2)}, u32[]{:S(2)}) collective-permute-start(bf16[776,384]{1,0:T(8,128)(2,1)} %collective-permute-done.7.refs_4_.refs_5_), channel_id=1, source_target_pairs={{0,3},{1,0},{2,1},{3,2},{4,7},{5,4},{6,5},{7,6},{8,11},{9,8},{10,9... | collective-permute-start | bytes 1787912 | tf_op jit(solution)/shard_map/ppermute | solution.py:296
  72.2 21.1 %copy-start = (s32[48,1536]{1,0:T(8,128)S(1)}, s32[48,1536]{1,0:T(8,128)}, u32[]{:S(2)}) copy-start(s32[48,1536]{1,0:T(8,128)} %d_ref.2) | copy-start | bytes 884740
  72.2 21.1 %copy-start.1 = (s32[48,48]{1,0:T(8,128)S(1)}, s32[48,48]{1,0:T(8,128)}, u32[]{:S(2)}) copy-start(s32[48,48]{1,0:T(8,128)} %pattern.1) | copy-start | bytes 27652
  72.2 21.1 %copy-start.2 = (s32[48]{0:T(128)S(1)}, s32[48]{0:T(128)}, u32[]{:S(2)}) copy-start(s32[48]{0:T(128)} %order.5) | copy-start | bytes 580
  85.8 7.5 %collective-permute-start.15 = (f32[384,1536]{1,0:T(8,128)}, f32[384,1536]{1,0:T(8,128)}, u32[]{:S(2)}, u32[]{:S(2)}) collective-permute-start(f32[384,1536]{1,0:T(8,128)} %get-tuple-element.64), channel_id=1, source_target_pairs={{0,8},{8,0},{1,9},{9,1},{2,10},{10,2},{3,11},{11,3},{4,12},{12,4},... | collective-permute-start | bytes 7077896 | tf_op jit(solution)/shard_map/ppermute | solution.py:296
